TPU v7x, 512 devices: a whole 4x4x16 slice. The times are simulated.
512 devices in a mesh: sub: 32 (over z, core), mem: 16 (over x, y).
Axes of the slice: x: 4, y: 4, z: 16, core: 2. Of those that a mesh axis runs over, the one named last changes fastest.
Arguments:
- dechirped_echo_matrix: bfloat16 [32, 2, 256, 8192], P('sub', None, 'mem'), may hold values from -6 to 6
- bearing_rotation_table: float32 [32, 16, 512, 256], P('sub', 'mem'), may hold values from -3.140625 to 3.140625
- patch_subset_holder: int32 [32, 16, 16], P('sub', 'mem'), may hold values from 0 to 31, as said below
- modulation_slope: float32 [32, 16, 2, 16], P('sub', 'mem'), may hold values from -0.5 to 0.5
- regrid_lead_cell: int32 [32, 16, 2, 128], P('sub', 'mem'), may hold values from 0 to 124
- regrid_weight: float32 [32, 16, 2, 128], P('sub', 'mem'), may hold values from 0 to 1
Outputs:
- ground_image: bfloat16 [512, 2, 128, 128], P(('sub', 'mem'))
Inputs may be any that keep to these rules, and one draw needn't show every extreme that they name: `patch_subset_holder`: each group and sector sends at most 2 of its 16 blocks to any one tile; in every sector some tile receives exactly 2 blocks from every group.
All inputs are finite; a program needn't handle non-finite values.
Results may differ from a plain program's by a relative error of at most 0.014.
Values may be sent and summed in bfloat16 or wider, within the bound.
No kernel may reach another device: no remote copies, remote signals or barrier semaphores. Data moves between devices by JAX's collectives and lax.ppermute only.
A program may use at most 64 MiB of HBM per device.

v0:
```python
import math

import jax
import jax.numpy as jnp
from jax import lax
from jax.sharding import PartitionSpec as P

FREQUENCIES = 8192
FIRST_RADIX = 64
SECOND_RADIX = 128
SWEEPS = 256
ANGLES = 512
BLOCK_SIDE = 128


def dft_tables(length):
    positions = jnp.arange(length, dtype=jnp.int32)
    turns = positions[:, None] * positions[None, :] % length
    phase_angle = turns.astype(jnp.float32) * (2.0 * math.pi / length)
    return jnp.stack([jnp.cos(phase_angle), jnp.sin(phase_angle)]).astype(jnp.bfloat16)


def twiddle(row_count, column_count, length):
    row_index = jnp.arange(row_count, dtype=jnp.int32)
    column_index = jnp.arange(column_count, dtype=jnp.int32)
    turns = row_index[:, None] * column_index[None, :] % length
    phase_angle = turns.astype(jnp.float32) * (2.0 * math.pi / length)
    return (jnp.cos(phase_angle), jnp.sin(phase_angle))


def combine(product):
    return (product[0, 0] - product[1, 1], product[0, 1] + product[1, 0])


def range_transform(sweeps):
    sweep_count = sweeps.shape[1]
    reshaped = sweeps.reshape(2, sweep_count, FIRST_RADIX, SECOND_RADIX)
    product = jnp.einsum(
        "qrk,pskj->qpsrj", dft_tables(FIRST_RADIX), reshaped, preferred_element_type=jnp.float32
    )
    inphase_part, quadrature_part = combine(product)
    cosine, sine_part = twiddle(FIRST_RADIX, SECOND_RADIX, FREQUENCIES)
    turned = jnp.stack(
        [
            inphase_part * cosine - quadrature_part * sine_part,
            inphase_part * sine_part + quadrature_part * cosine,
        ]
    ).astype(jnp.bfloat16)
    product = jnp.einsum(
        "quj,psrj->qpsur", dft_tables(SECOND_RADIX), turned, preferred_element_type=jnp.float32
    )
    inphase_part, quadrature_part = combine(product)
    factor = 1.0 / math.sqrt(FREQUENCIES)
    return (
        (jnp.stack([inphase_part, quadrature_part]) * factor)
        .astype(jnp.bfloat16)
        .reshape(2, sweep_count, FREQUENCIES)
    )


def phase_tables(angles):
    factor = 1.0 / math.sqrt(SWEEPS)
    return jnp.stack([jnp.cos(angles) * factor, jnp.sin(angles) * factor]).astype(jnp.bfloat16)


def strip_modulation(
    inphase_part, quadrature_part, modulation_line_entries, tilt_patches, slant_patches
):
    tilt_linear_slope = modulation_line_entries[0].reshape(tilt_patches, slant_patches)
    slant_linear_slope = modulation_line_entries[1].reshape(tilt_patches, slant_patches)
    positions = jnp.arange(BLOCK_SIDE, dtype=jnp.float32)
    phase_angle = (
        tilt_linear_slope[:, None, :, None] * positions[None, :, None, None]
        + slant_linear_slope[:, None, :, None] * positions[None, None, None, :]
    )
    cosine = jnp.cos(phase_angle)
    sine_part = jnp.sin(phase_angle)
    inphase_part = inphase_part.reshape(tilt_patches, BLOCK_SIDE, slant_patches, BLOCK_SIDE)
    quadrature_part = quadrature_part.reshape(tilt_patches, BLOCK_SIDE, slant_patches, BLOCK_SIDE)
    return jnp.stack(
        [
            inphase_part * cosine - quadrature_part * sine_part,
            inphase_part * sine_part + quadrature_part * cosine,
        ]
    ).astype(jnp.bfloat16)


def stencil(offsets, fractions):
    weights = [
        -fractions * (fractions - 1.0) * (fractions - 2.0) / 6.0,
        (fractions + 1.0) * (fractions - 1.0) * (fractions - 2.0) / 2.0,
        -(fractions + 1.0) * fractions * (fractions - 2.0) / 2.0,
        (fractions + 1.0) * fractions * (fractions - 1.0) / 6.0,
    ]
    sources = jnp.arange(fractions.shape[-1], dtype=jnp.int32)
    distance = sources - offsets[..., None]
    weights_sum = jnp.zeros(distance.shape, jnp.float32)
    for stencil_tap in range(4):
        weights_sum = weights_sum + jnp.where(
            distance == stencil_tap, weights[stencil_tap][..., None], jnp.float32(0.0)
        )
    return weights_sum.astype(jnp.bfloat16)


def on_device(
    dechirped_echo_matrix,
    bearing_rotation_table,
    patch_subset_holder,
    modulation_slope,
    regrid_lead_cell,
    regrid_weight,
):
    groups = lax.axis_size("sub")
    members = lax.axis_size("mem")
    sector = FREQUENCIES // members
    tilt_patches = ANGLES // BLOCK_SIDE
    slant_patches = sector // BLOCK_SIDE
    block_count = tilt_patches * slant_patches
    capacity = max(2, 2 * block_count // groups)
    spectrum = range_transform(dechirped_echo_matrix[0])
    sweep_count = spectrum.shape[1]
    by_sector = spectrum.reshape(2, sweep_count, members, sector)
    tables = phase_tables(bearing_rotation_table[0, 0])
    product = jnp.einsum(
        "qas,psc->qpac",
        tables,
        lax.all_to_all(by_sector, "mem", split_axis=2, concat_axis=1, tiled=True)[:, :, 0, :],
        preferred_element_type=jnp.float32,
    )
    inphase_part, quadrature_part = combine(product)
    focused_image = jnp.stack([inphase_part, quadrature_part])[:, :, None, :]
    patch_list = strip_modulation(
        focused_image[0, :, 0, :],
        focused_image[1, :, 0, :],
        modulation_slope[0, 0],
        tilt_patches,
        slant_patches,
    )
    own_tables = stencil(regrid_lead_cell[0, 0], regrid_weight[0, 0])
    owners = patch_subset_holder[0, 0]
    onehot = owners[:, None] == jnp.arange(groups, dtype=jnp.int32)[None, :]
    counts = onehot.astype(jnp.int32)
    before = jnp.cumsum(counts, axis=0) - counts
    rank_within = jnp.sum(before * counts, axis=1)
    slot_index = owners * capacity + rank_within
    selector = (
        slot_index[None, :] == jnp.arange(groups * capacity, dtype=jnp.int32)[:, None]
    ).astype(jnp.bfloat16)
    selector = selector.reshape(groups * capacity, tilt_patches, slant_patches)
    packed = jnp.einsum(
        "kAC,pAaCc->kpac", selector, patch_list, preferred_element_type=jnp.float32
    ).astype(jnp.bfloat16)
    packed = packed.reshape(groups, capacity, 2, BLOCK_SIDE, BLOCK_SIDE)
    rows_done = jnp.einsum(
        "ya,skpac->skpyc",
        own_tables[0],
        lax.all_to_all(packed, "sub", split_axis=0, concat_axis=0, tiled=True),
        preferred_element_type=jnp.float32,
    ).astype(jnp.bfloat16)
    interpolated = jnp.einsum(
        "skpyc,xc->skpyx", rows_done, own_tables[1], preferred_element_type=jnp.float32
    )
    per_source = lax.optimization_barrier(jnp.sum(interpolated, axis=1).astype(jnp.bfloat16))
    ground = jnp.sum(per_source.astype(jnp.float32), axis=0)
    return (0.25 * ground).astype(jnp.bfloat16)[None]


def solution(mesh):
    return jax.shard_map(
        on_device,
        mesh=mesh,
        in_specs=(
            P("sub", None, "mem", None),
            P("sub", "mem", None, None),
            P("sub", "mem", None),
            P("sub", "mem", None, None),
            P("sub", "mem", None, None),
            P("sub", "mem", None, None),
        ),
        out_specs=P(("sub", "mem"), None, None, None),
        check_vma=False,
    )
```

profile of v0, /device:TPU:32, one launch (start us, length us, event | category | flops | bytes accessed | tf_op | source)
XLA Modules:
  0.0 251.5 jit_solution(1296951972144069994)
XLA Ops:
  0.0 0.2 sine_convert_fusion.1
  0.2 0.1 fusion.59
  0.3 0.3 sine_convert_fusion
  0.6 1.2 copy.78
  1.8 0.4 convolution_bitcast_fusion.2
  2.2 0.2 subtract_convert_fusion
  2.4 0.4 convolution_bitcast_fusion.1
  2.8 0.2 slice_subtract_fusion.1
  3.0 0.3 copy.53
  3.4 0.3 add.211
  3.7 0.3 copy.52
  4.0 0.3 sub.102
  4.3 0.1 fusion.22
  4.4 1.1 copy.54
  5.5 7.0 %all-to-all-start = ((bf16[2,16,16,512]{3,1,0,2:T(8,128)(2,1)}), bf16[2,16,16,512]{3,1,0,2:T(8,128)(2,1)S(1)}, u32[]{:S(2)}, u32[]{:S(2)}) async-start(bf16[2,16,16,512]{3,1,0,2:T(8,128)(2,1)} %copy.54), calls=%async_computation | async-start | bytes 1048576 | tf_op jit(solution)/shard_map/all_to_all | solution.py:127
  12.9 0.2 select_reduce_fusion
  13.4 1.9 fusion.30
  15.3 8.7 %all-to-all-done = bf16[2,16,16,512]{3,1,0,2:T(8,128)(2,1)S(1)} async-done(((bf16[2,16,16,512]{3,1,0,2:T(8,128)(2,1)}), bf16[2,16,16,512]{3,1,0,2:T(8,128)(2,1)S(1)}, u32[]{:S(2)}, u32[]{:S(2)}) %all-to-all-start) | async-done | bytes 524320 | tf_op jit(solution)/shard_map/all_to_all | solution.py:127
  24.1 0.8 convolution_bitcast_fusion
  24.9 0.5 slice_subtract_fusion
  25.3 0.8 copy.57
  26.1 0.8 copy.59
  26.9 4.6 %fusion.19 = (bf16[1,4,128,4,128]{4,2,3,1,0:T(8,128)(2,1)S(1)}, bf16[1,4,128,4,128]{4,2,3,1,0:T(8,128)(2,1)S(1)}) fusion(f32[1,4,128,4,128]{4,3,0,2,1:T(4,128)S(1)} %bitcast.122, f32[1,4,128,4,128]{4,3,0,2,1:T(4,128)S(1)} %bitcast.121, f32[4,4,128]{2,1,0:T(4,128)S(1)} %iota_multiply_fusion, f32[4,128,4]{1,2,0:T(4,128)S(1)} %iota_multiply_fusion.1), kind=kLoop, calls=%fused_computation.18 | loop fusion | flops 2359296 | bytes 3162112 | tf_op jit(solution)/shard_map/convert
  31.6 0.1 pad_maximum_fusion
  31.7 1.9 bitcast_convert_fusion
  33.6 6.6 %copy.64 = bf16[32,2,2,128,128]{4,1,3,2,0:T(2,128)(2,1)} copy(bf16[32,2,2,128,128]{4,1,0,3,2:T(2,128)(2,1)S(1)} %bitcast.123) | data formatting | bytes 8388608 | tf_op jit(solution)/shard_map/reshape | solution.py:153
  40.2 15.5 %all-to-all-start.1 = ((bf16[32,2,2,128,128]{4,1,3,2,0:T(2,128)(2,1)}), bf16[32,2,2,128,128]{4,1,3,2,0:T(2,128)(2,1)}, u32[]{:S(2)}, u32[]{:S(2)}) async-start(bf16[32,2,2,128,128]{4,1,3,2,0:T(2,128)(2,1)} %copy.64), calls=%async_computation.1 | async-start | bytes 8388608 | tf_op jit(solution)/shard_map/all_to_all | solution.py:157
  55.8 0.2 add_convert_fusion.1
  56.0 189.5 %all-to-all-done.1 = bf16[32,2,2,128,128]{4,1,3,2,0:T(2,128)(2,1)} async-done(((bf16[32,2,2,128,128]{4,1,3,2,0:T(2,128)(2,1)}), bf16[32,2,2,128,128]{4,1,3,2,0:T(2,128)(2,1)}, u32[]{:S(2)}, u32[]{:S(2)}) %all-to-all-start.1) | async-done | bytes 4194336 | tf_op jit(solution)/shard_map/all_to_all | solution.py:157
  245.5 5.0 %fusion.9 = bf16[32,2,128,128]{3,2,1,0:T(8,128)(2,1)S(1)} fusion(bf16[32,2,2,128,128]{4,1,3,2,0:T(2,128)(2,1)} %all-to-all-done.1, bf16[2,128,128]{2,1,0:T(8,128)(2,1)S(1)} %add_convert_fusion.1), kind=kOutput, calls=%fused_computation.7 | convolution fusion | flops 1076887552 | bytes 6356992 | tf_op jit(solution)/shard_map/skpyc,xc->skpyx/dot_general | solution.py:160
  250.5 0.3 convert_reduce_fusion
  250.8 0.6 fusion.39
  (23 shorter events, 0.7 us)
Async XLA Ops:
  3.4 9.2 %copy-start.4 = (f32[1,1,2,16]{3,2,1,0:T(2,128)S(1)}, f32[1,1,2,16]{3,2,1,0:T(2,128)}, u32[]{:S(2)}) copy-start(f32[1,1,2,16]{3,2,1,0:T(2,128)} %param.9) | copy-start | bytes 388
  3.4 9.4 %copy-start.1 = (s32[1,1,16]{2,1,0:T(1,128)S(1)}, s32[1,1,16]{2,1,0:T(1,128)}, u32[]{:S(2)}) copy-start(s32[1,1,16]{2,1,0:T(1,128)} %param.8) | copy-start | bytes 196
  3.4 10.0 %copy-start = (f32[1,1,512,256]{3,2,1,0:T(8,128)S(1)}, f32[1,1,512,256]{3,2,1,0:T(8,128)}, u32[]{:S(2)}) copy-start(f32[1,1,512,256]{3,2,1,0:T(8,128)} %param.7) | copy-start | bytes 1572868
  5.5 18.5 %all-to-all-start = ((bf16[2,16,16,512]{3,1,0,2:T(8,128)(2,1)}), bf16[2,16,16,512]{3,1,0,2:T(8,128)(2,1)S(1)}, u32[]{:S(2)}, u32[]{:S(2)}) async-start(bf16[2,16,16,512]{3,1,0,2:T(8,128)(2,1)} %copy.54), calls=%async_computation | async-start | bytes 1048576 | tf_op jit(solution)/shard_map/all_to_all | solution.py:127
  40.2 15.6 %copy-start.3 = (f32[1,1,2,128]{3,2,1,0:T(2,128)S(1)}, f32[1,1,2,128]{3,2,1,0:T(2,128)}, u32[]{:S(2)}) copy-start(f32[1,1,2,128]{3,2,1,0:T(2,128)} %param.11) | copy-start | bytes 3076
  40.2 15.6 %copy-start.2 = (s32[1,1,2,128]{3,2,1,0:T(2,128)S(1)}, s32[1,1,2,128]{3,2,1,0:T(2,128)}, u32[]{:S(2)}) copy-start(s32[1,1,2,128]{3,2,1,0:T(2,128)} %param.10) | copy-start | bytes 3076
  40.2 205.3 %all-to-all-start.1 = ((bf16[32,2,2,128,128]{4,1,3,2,0:T(2,128)(2,1)}), bf16[32,2,2,128,128]{4,1,3,2,0:T(2,128)(2,1)}, u32[]{:S(2)}, u32[]{:S(2)}) async-start(bf16[32,2,2,128,128]{4,1,3,2,0:T(2,128)(2,1)} %copy.64), calls=%async_computation.1 | async-start | bytes 8388608 | tf_op jit(solution)/shard_map/all_to_all | solution.py:157
where the time goes:
time: 252 us; the launch traced here: 251 us
  waiting for transfers between devices  198 us (79%)
  starting transfers between devices  22.6 us (9%)
  local copies, waits for them, and re-layouts  12.1 us (5%)
  other arithmetic  9.92 us (4%)
  matrix products  8.43 us (3%)
    all_to_all x1, waiting for transfers between devices, on_device(): lax.all_to_all(packed, 'sub', split_axis=0, concat_axis=0, tiled=True)  189 us
    all_to_all x1, starting transfers between devices, on_device(): lax.all_to_all(packed, 'sub', split_axis=0, concat_axis=0, tiled=True)  15.5 us
    all_to_all x1, waiting for transfers between devices, on_device(): lax.all_to_all(by_sector, 'mem', split_axis=2, concat_axis=1, tiled=True)  8.73 us
    all_to_all x1, starting transfers between devices, on_device(): lax.all_to_all(by_sector, 'mem', split_axis=2, concat_axis=1, tiled=True)  7.04 us
    reshape x1, local copies, waits for them, and re-layouts, on_device(): packed = packed.reshape(groups, capacity, 2, BLOCK_SIDE, BLOCK_SIDE)  6.62 us
    another operation x4, other arithmetic  5.31 us
  transfers between devices with their start and end apart: 2, of which 2 were waited for; matrix products, arithmetic and copies ran while one was open for 1% of the time, Pallas kernels for 0%

commit v1 on v0

v1 whole, which is shorter than its diff:
```python
import functools
import math

import jax
import jax.numpy as jnp
from jax import lax
from jax.experimental import pallas as pl
from jax.experimental.pallas import tpu as pltpu
from jax.sharding import PartitionSpec as P

FREQUENCIES = 8192
FIRST_RADIX = 64
SECOND_RADIX = 128
SWEEPS = 256
ANGLES = 512
BLOCK_SIDE = 128
F32 = jnp.float32
BF16 = jnp.bfloat16


def dft_tables(length):
    positions = jnp.arange(length, dtype=jnp.int32)
    turns = positions[:, None] * positions[None, :] % length
    phase_angle = turns.astype(F32) * (2.0 * math.pi / length)
    return jnp.stack([jnp.cos(phase_angle), jnp.sin(phase_angle)]).astype(BF16)


def twiddle(row_count, column_count, length):
    row_index = jnp.arange(row_count, dtype=jnp.int32)
    column_index = jnp.arange(column_count, dtype=jnp.int32)
    turns = row_index[:, None] * column_index[None, :] % length
    phase_angle = turns.astype(F32) * (2.0 * math.pi / length)
    return (jnp.cos(phase_angle), jnp.sin(phase_angle))


def combine(product):
    return (product[0, 0] - product[1, 1], product[0, 1] + product[1, 0])


def range_transform(sweeps):
    sweep_count = sweeps.shape[1]
    reshaped = sweeps.reshape(2, sweep_count, FIRST_RADIX, SECOND_RADIX)
    product = jnp.einsum(
        "qrk,pskj->qpsrj", dft_tables(FIRST_RADIX), reshaped, preferred_element_type=F32
    )
    inphase_part, quadrature_part = combine(product)
    cosine, sine_part = twiddle(FIRST_RADIX, SECOND_RADIX, FREQUENCIES)
    turned = jnp.stack(
        [
            inphase_part * cosine - quadrature_part * sine_part,
            inphase_part * sine_part + quadrature_part * cosine,
        ]
    ).astype(BF16)
    product = jnp.einsum(
        "quj,psrj->qpsur", dft_tables(SECOND_RADIX), turned, preferred_element_type=F32
    )
    inphase_part, quadrature_part = combine(product)
    factor = 1.0 / math.sqrt(FREQUENCIES)
    return (
        (jnp.stack([inphase_part, quadrature_part]) * factor)
        .astype(BF16)
        .reshape(2, sweep_count, FREQUENCIES)
    )


def phase_tables(angles):
    factor = 1.0 / math.sqrt(SWEEPS)
    return jnp.stack([jnp.cos(angles) * factor, jnp.sin(angles) * factor]).astype(BF16)


def stencil(offsets, fractions):
    weights = [
        -fractions * (fractions - 1.0) * (fractions - 2.0) / 6.0,
        (fractions + 1.0) * (fractions - 1.0) * (fractions - 2.0) / 2.0,
        -(fractions + 1.0) * fractions * (fractions - 2.0) / 2.0,
        (fractions + 1.0) * fractions * (fractions - 1.0) / 6.0,
    ]
    sources = jnp.arange(fractions.shape[-1], dtype=jnp.int32)
    distance = sources - offsets[..., None]
    weights_sum = jnp.zeros(distance.shape, F32)
    for stencil_tap in range(4):
        weights_sum = weights_sum + jnp.where(
            distance == stencil_tap, weights[stencil_tap][..., None], F32(0.0)
        )
    return weights_sum.astype(BF16)


def focus_kernel(slots, tab, z, cu, su, cv, sv, own, other):
    half = own.shape[1]
    own[...] = jnp.zeros_like(own)
    other[...] = jnp.zeros_like(other)
    side = BLOCK_SIDE
    sector = z.shape[-1]
    rows = z.shape[0] * z.shape[2]
    zre = z[:, 0].reshape(rows, sector)
    zim = z[:, 1].reshape(rows, sector)
    for ab in range(tab.shape[1] // side):
        span = slice(ab * side, (ab + 1) * side)
        pc = tab[0, span, :]
        ps = tab[1, span, :]
        dot = functools.partial(jnp.dot, preferred_element_type=F32)
        re = dot(pc, zre) - dot(ps, zim)
        im = dot(pc, zim) + dot(ps, zre)
        for cb in range(sector // side):
            lanes = slice(cb * side, (cb + 1) * side)
            c0 = cu[span, cb : cb + 1]
            s0 = su[span, cb : cb + 1]
            c1 = cv[ab : ab + 1, lanes]
            s1 = sv[ab : ab + 1, lanes]
            cosine = c0 * c1 - s0 * s1
            sine = s0 * c1 + c0 * s1
            r, i = re[:, lanes], im[:, lanes]
            dre = (r * cosine - i * sine).astype(BF16).astype(F32)
            dim = (r * sine + i * cosine).astype(BF16).astype(F32)
            slot = slots[ab * (sector // side) + cb]

            def add(ref, index):
                ref[0, index] = (ref[0, index].astype(F32) + dre).astype(BF16)
                ref[1, index] = (ref[1, index].astype(F32) + dim).astype(BF16)

            @pl.when(slot < half)
            def _():
                add(own, slot)

            @pl.when(slot >= half)
            def _():
                add(other, slot - half)


def focus(slots, tab, z, cu, su, cv, sv, half):
    shape = jax.ShapeDtypeStruct((2, half, BLOCK_SIDE, BLOCK_SIDE), BF16)
    vmem = pl.BlockSpec(memory_space=pltpu.VMEM)
    return pl.pallas_call(
        focus_kernel,
        out_shape=(shape, shape),
        in_specs=[pl.BlockSpec(memory_space=pltpu.SMEM)] + [vmem] * 6,
        out_specs=(vmem, vmem),
        name="focus",
    )(slots, tab, z, cu, su, cv, sv)


def on_device(
    dechirped_echo_matrix,
    bearing_rotation_table,
    patch_subset_holder,
    modulation_slope,
    regrid_lead_cell,
    regrid_weight,
):
    groups = lax.axis_size("sub")
    members = lax.axis_size("mem")
    chips = groups // 2
    sector = FREQUENCIES // members
    ab_count = ANGLES // BLOCK_SIDE
    cb_count = sector // BLOCK_SIDE

    spectrum = range_transform(dechirped_echo_matrix[0])
    sweep_count = spectrum.shape[1]
    by_sector = spectrum.reshape(2, sweep_count, members, sector).transpose(2, 0, 1, 3)
    z = lax.all_to_all(by_sector, "mem", split_axis=0, concat_axis=0, tiled=True)

    tables = phase_tables(bearing_rotation_table[0, 0])
    positions = jnp.arange(BLOCK_SIDE, dtype=F32)
    slope = modulation_slope[0, 0].reshape(2, ab_count, cb_count)
    u_phase = (slope[0][:, None, :] * positions[None, :, None]).reshape(ANGLES, cb_count)
    v_phase = (slope[1][:, :, None] * positions[None, None, :]).reshape(ab_count, sector)

    me = lax.axis_index("sub")
    owners = patch_subset_holder[0, 0]
    apart = owners ^ me
    slots = (apart & 1) * chips + ((apart >> 1) & 1) * (chips // 2) + (owners >> 2)

    own, other = focus(
        slots, tables, z, jnp.cos(u_phase), jnp.sin(u_phase), jnp.cos(v_phase), jnp.sin(v_phase), chips
    )
    core_swap = [(i, i ^ 1) for i in range(groups)]
    held = own + lax.ppermute(other, "sub", core_swap)

    def partner(z, shift):
        w = z + shift
        return ((w ^ 1) - shift) % chips

    def pairing(shift):
        return [(2 * z + c, 2 * partner(z, shift) + c) for z in range(chips) for c in range(2)]

    kept = chips // 2
    first = held[0, :kept] + lax.ppermute(held[0, kept:], "sub", pairing(0))
    second = held[1, :kept] + lax.ppermute(held[1, kept:], "sub", pairing(1))
    alike = [[2 * z + c for z in range(par, chips, 2)] for par in range(2) for c in range(2)]
    arrived = lax.all_to_all(
        jnp.stack([first, second], axis=1),
        "sub",
        split_axis=0,
        concat_axis=0,
        tiled=True,
        axis_index_groups=alike,
    )
    gathered = jnp.sum(arrived.astype(F32), axis=0).astype(BF16)
    own_tables = stencil(regrid_lead_cell[0, 0], regrid_weight[0, 0])
    rows_done = jnp.einsum(
        "ya,pac->pyc", own_tables[0], gathered, preferred_element_type=F32
    ).astype(BF16)
    ground = jnp.einsum("pyc,xc->pyx", rows_done, own_tables[1], preferred_element_type=F32)
    return (0.25 * ground).astype(BF16)[None]


def solution(mesh):
    return jax.shard_map(
        on_device,
        mesh=mesh,
        in_specs=(
            P("sub", None, "mem", None),
            P("sub", "mem", None, None),
            P("sub", "mem", None),
            P("sub", "mem", None, None),
            P("sub", "mem", None, None),
            P("sub", "mem", None, None),
        ),
        out_specs=P(("sub", "mem"), None, None, None),
        check_vma=False,
    )
```

time: 252 us -> 98.9 us (0.39)
  the two profiles are of different devices: /device:TPU:32 before, /device:TPU:65 now
where the time goes in v1:
time: 98.9 us; the launch traced here: 98.4 us
  waiting for transfers between devices  45.1 us (46%)
  starting transfers between devices  30.7 us (31%)
  other arithmetic  9.79 us (10%)
  Pallas kernels  5.8 us (6%)
  local copies, waits for them, and re-layouts  4.94 us (5%)
  matrix products  1.86 us (2%)
    all_to_all x1, waiting for transfers between devices, on_device(): lax.all_to_all(jnp.stack([first, second], axis=1), 'sub', split_axis=0, c...  31.2 us
    all_to_all x1, starting transfers between devices, on_device(): lax.all_to_all(jnp.stack([first, second], axis=1), 'sub', split_axis=0, c...  14.5 us
    all_to_all x1, starting transfers between devices, on_device(): lax.all_to_all(by_sector, 'mem', split_axis=0, concat_axis=0, tiled=True)  6.75 us
    pallas_call x1, Pallas kernels, focus(): pl.pallas_call(focus_kernel, out_shape=(shape, shape), in_specs=[pl.Block...  5.8 us
    ppermute x1, waiting for transfers between devices, on_device(): first = held[0, :kept] + lax.ppermute(held[0, kept:], 'sub', pairing(0))  4.24 us
    all_to_all x1, waiting for transfers between devices, on_device(): lax.all_to_all(by_sector, 'mem', split_axis=0, concat_axis=0, tiled=True)  4.22 us
    ppermute x1, starting transfers between devices, on_device(): held = own + lax.ppermute(other, 'sub', core_swap)  3.97 us
    ppermute x1, starting transfers between devices, on_device(): first = held[0, :kept] + lax.ppermute(held[0, kept:], 'sub', pairing(0))  3.54 us
  transfers between devices with their start and end apart: 5, of which 5 were waited for; matrix products, arithmetic and copies ran while one was open for 6% of the time, Pallas kernels for 0%

profile of v1, /device:TPU:65, one launch (start us, length us, event | category | flops | bytes accessed | tf_op | source)
XLA Modules:
  0.0 98.4 jit_solution(1798387628268794973)
XLA Ops:
  0.3 0.3 sine_convert_fusion
  0.6 1.2 %copy.29 = bf16[4,8,64,128]{3,2,1,0:T(8,128)(2,1)S(1)} copy(bf16[4,8,64,128]{3,1,2,0:T(8,128)(2,1)} %bitcast.129) | data formatting | bytes 1048576
  1.8 0.4 convolution_bitcast_fusion.1
  2.4 0.4 convolution_bitcast_fusion
  3.0 0.3 copy.17
  3.4 0.3 sub.70
  3.7 0.3 copy.19
  4.0 0.3 copy.18
  4.3 0.3 add.168
  4.6 0.3 copy.20
  4.9 0.9 fusion.4
  5.9 6.7 %all-to-all-start = ((bf16[16,2,16,512]{3,2,1,0:T(8,128)(2,1)}), bf16[16,2,16,512]{3,2,1,0:T(8,128)(2,1)S(1)}, u32[]{:S(2)}, u32[]{:S(2)}) async-start(bf16[16,2,16,512]{3,2,1,0:T(8,128)(2,1)} %fusion.4), calls=%async_computation | async-start | bytes 1048576 | tf_op jit(solution)/shard_map/all_to_all | solution.py:160
  12.7 1.9 %fusion.9 = (bf16[1,512,256]{2,1,0:T(8,128)(2,1)S(1)}, bf16[1,512,256]{2,1,0:T(8,128)(2,1)S(1)}) fusion(f32[1,1,512,256]{3,2,1,0:T(8,128)S(1)} %copy-done.1), kind=kLoop, calls=%fused_computation.25 | loop fusion | flops 524288 | bytes 1048576 | tf_op jit(solution)/shard_map/mul | solution.py:68
  14.6 0.9 pad_maximum_fusion.tab
  15.5 0.6 add_bitcast_fusion.slots
  16.2 1.8 %fusion.15 = (f32[512,4]{1,0:T(8,128)}, f32[512,4]{1,0:T(8,128)}) fusion(f32[512]{0:T(512)S(1)} %iota_bitcast_fusion, f32[4,4]{1,0:T(4,128)S(1)} %mul.397), kind=kLoop, calls=%fused_computation.36 | loop fusion | flops 2048 | bytes 18496 | tf_op jit(solution)/shard_map/sin | solution.py:174
  18.1 0.7 fusion.45
  18.8 4.2 %all-to-all-done.z = bf16[16,2,16,512]{3,2,1,0:T(8,128)(2,1)S(1)} async-done(((bf16[16,2,16,512]{3,2,1,0:T(8,128)(2,1)}), bf16[16,2,16,512]{3,2,1,0:T(8,128)(2,1)S(1)}, u32[]{:S(2)}, u32[]{:S(2)}) %all-to-all-start) | async-done | bytes 524320 | tf_op jit(solution)/shard_map/all_to_all | solution.py:160
  23.0 0.8 copy-done
  23.8 5.8 %focus.1 = (bf16[2,16,128,128]{3,2,1,0:T(8,128)(2,1)}, bf16[2,16,128,128]{3,2,1,0:T(8,128)(2,1)}) custom-call(s32[16]{0:T(128)} %add_bitcast_fusion.slots, bf16[2,512,256]{2,1,0:T(8,128)(2,1)} %pad_maximum_fusion.tab, bf16[16,2,16,512]{3,2,1,0:T(8,128)(2,1)} %copy-done, f32[512,4]{1,0:T(8,128)} %get-tuple-element.24.cu, f32[512,4]{1,0:T(8,128)} %get-tuple-element.23.su, ...), custom_call_target="tpu_custom_call" | custom-call | tf_op jit(solution)/shard_map/focus/pallas_call | solution.py:133
  29.6 4.0 %collective-permute-start = (bf16[2,16,128,128]{3,2,1,0:T(8,128)(2,1)}, bf16[2,16,128,128]{3,2,1,0:T(8,128)(2,1)S(1)}, u32[]{:S(2)}, u32[]{:S(2)}) collective-permute-start(bf16[2,16,128,128]{3,2,1,0:T(8,128)(2,1)} %get-tuple-element.8), channel_id=1, source_target_pairs={{0,16},{16,0},{32,48},{48,32},{64,80},{80,64},{96,112},{112,96},{1... | collective-permute-start | bytes 3145736 | tf_op jit(solution)/shard_map/ppermute | solution.py:177
  33.6 2.5 %collective-permute-done = bf16[2,16,128,128]{3,2,1,0:T(8,128)(2,1)S(1)} collective-permute-done((bf16[2,16,128,128]{3,2,1,0:T(8,128)(2,1)}, bf16[2,16,128,128]{3,2,1,0:T(8,128)(2,1)S(1)}, u32[]{:S(2)}, u32[]{:S(2)}) %collective-permute-start) | collective-permute-done | bytes 1048608 | tf_op jit(solution)/shard_map/ppermute | solution.py:177
  36.0 1.6 %add.169 = bf16[2,16,128,128]{3,2,1,0:T(8,128)(2,1)S(1)} add(bf16[2,16,128,128]{3,2,1,0:T(8,128)(2,1)} %get-tuple-element.7, bf16[2,16,128,128]{3,2,1,0:T(8,128)(2,1)S(1)} %collective-permute-done) | non-fusion elementwise | flops 524288 | bytes 3145728 | tf_op jit(solution)/shard_map/add | solution.py:177
  37.7 3.5 %collective-permute-start.1 = (bf16[8,128,128]{2,1,0:T(8,128)(2,1)S(1)}, bf16[8,128,128]{2,1,0:T(8,128)(2,1)S(1)}, u32[]{:S(2)}, u32[]{:S(2)}) collective-permute-start(bf16[8,128,128]{2,1,0:T(8,128)(2,1)S(1)} %get-tuple-element.17), channel_id=1, source_target_pairs={{0,32},{16,48},{32,0},{48,16},{64,96},{80,112},{96,64},{112,80},{1... | collective-permute-start | bytes 786440 | tf_op jit(solution)/shard_map/ppermute | solution.py:187
  41.3 1.9 %collective-permute-start.2 = (bf16[8,128,128]{2,1,0:T(8,128)(2,1)S(1)}, bf16[8,128,128]{2,1,0:T(8,128)(2,1)S(1)}, u32[]{:S(2)}, u32[]{:S(2)}) collective-permute-start(bf16[8,128,128]{2,1,0:T(8,128)(2,1)S(1)} %get-tuple-element.18), channel_id=1, source_target_pairs={{0,480},{16,496},{32,64},{48,80},{64,32},{80,48},{96,128},{112,144... | collective-permute-start | bytes 786440 | tf_op jit(solution)/shard_map/ppermute | solution.py:188
  43.2 4.2 %collective-permute-done.1 = bf16[8,128,128]{2,1,0:T(8,128)(2,1)S(1)} collective-permute-done((bf16[8,128,128]{2,1,0:T(8,128)(2,1)S(1)}, bf16[8,128,128]{2,1,0:T(8,128)(2,1)S(1)}, u32[]{:S(2)}, u32[]{:S(2)}) %collective-permute-start.1) | collective-permute-done | bytes 262176 | tf_op jit(solution)/shard_map/ppermute | solution.py:187
  47.4 2.9 %collective-permute-done.2 = bf16[8,128,128]{2,1,0:T(8,128)(2,1)S(1)} collective-permute-done((bf16[8,128,128]{2,1,0:T(8,128)(2,1)S(1)}, bf16[8,128,128]{2,1,0:T(8,128)(2,1)S(1)}, u32[]{:S(2)}, u32[]{:S(2)}) %collective-permute-start.2) | collective-permute-done | bytes 262176 | tf_op jit(solution)/shard_map/ppermute | solution.py:188
  50.5 0.8 copy.21
  51.3 14.5 %all-to-all-start.1 = ((bf16[8,2,128,128]{3,2,1,0:T(8,128)(2,1)}), bf16[8,2,128,128]{3,2,1,0:T(8,128)(2,1)S(1)}, u32[]{:S(2)}, u32[]{:S(2)}) async-start(bf16[8,2,128,128]{3,2,1,0:T(8,128)(2,1)} %copy.21), calls=%async_computation.1 | async-start | bytes 1048576 | tf_op jit(solution)/shard_map/all_to_all | solution.py:190
  65.9 0.2 add_convert_fusion.1
  66.1 31.2 %all-to-all-done.1 = bf16[8,2,128,128]{3,2,1,0:T(8,128)(2,1)S(1)} async-done(((bf16[8,2,128,128]{3,2,1,0:T(8,128)(2,1)}), bf16[8,2,128,128]{3,2,1,0:T(8,128)(2,1)S(1)}, u32[]{:S(2)}, u32[]{:S(2)}) %all-to-all-start.1) | async-done | bytes 524320 | tf_op jit(solution)/shard_map/all_to_all | solution.py:190
  97.4 1.0 %fusion.1 = bf16[1,2,128,128]{3,2,1,0:T(8,128)(2,1)} fusion(bf16[2,128,128]{2,1,0:T(8,128)(2,1)S(1)} %reduce_sum.12, bf16[2,128,128]{2,1,0:T(8,128)(2,1)S(1)} %add_convert_fusion.1), kind=kOutput, calls=%fused_computation.5 | convolution fusion | flops 16875520 | bytes 196608 | tf_op jit(solution)/shard_map/pyc,xc->pyx/dot_general | solution.py:203
  (25 shorter events, 1.2 us)
Async XLA Ops:
  4.6 8.0 %copy-start.4 = (f32[1,1,2,16]{3,2,1,0:T(2,128)S(1)}, f32[1,1,2,16]{3,2,1,0:T(2,128)}, u32[]{:S(2)}) copy-start(f32[1,1,2,16]{3,2,1,0:T(2,128)} %param.9) | copy-start | bytes 388
  4.6 8.1 %copy-start.1 = (f32[1,1,512,256]{3,2,1,0:T(8,128)S(1)}, f32[1,1,512,256]{3,2,1,0:T(8,128)}, u32[]{:S(2)}) copy-start(f32[1,1,512,256]{3,2,1,0:T(8,128)} %param.7) | copy-start | bytes 1572868
  4.9 10.5 %copy-start.5 = (s32[1,1,16]{2,1,0:T(1,128)S(1)}, s32[1,1,16]{2,1,0:T(1,128)}, u32[]{:S(2)}) copy-start(s32[1,1,16]{2,1,0:T(1,128)} %param.8) | copy-start | bytes 196
  5.9 17.1 %all-to-all-start = ((bf16[16,2,16,512]{3,2,1,0:T(8,128)(2,1)}), bf16[16,2,16,512]{3,2,1,0:T(8,128)(2,1)S(1)}, u32[]{:S(2)}, u32[]{:S(2)}) async-start(bf16[16,2,16,512]{3,2,1,0:T(8,128)(2,1)} %fusion.4), calls=%async_computation | async-start | bytes 1048576 | tf_op jit(solution)/shard_map/all_to_all | solution.py:160
  23.0 0.8 copy-start
  29.6 6.5 %collective-permute-start = (bf16[2,16,128,128]{3,2,1,0:T(8,128)(2,1)}, bf16[2,16,128,128]{3,2,1,0:T(8,128)(2,1)S(1)}, u32[]{:S(2)}, u32[]{:S(2)}) collective-permute-start(bf16[2,16,128,128]{3,2,1,0:T(8,128)(2,1)} %get-tuple-element.8), channel_id=1, source_target_pairs={{0,16},{16,0},{32,48},{48,32},{64,80},{80,64},{96,112},{112,96},{1... | collective-permute-start | bytes 3145736 | tf_op jit(solution)/shard_map/ppermute | solution.py:177
  37.7 9.7 %collective-permute-start.1 = (bf16[8,128,128]{2,1,0:T(8,128)(2,1)S(1)}, bf16[8,128,128]{2,1,0:T(8,128)(2,1)S(1)}, u32[]{:S(2)}, u32[]{:S(2)}) collective-permute-start(bf16[8,128,128]{2,1,0:T(8,128)(2,1)S(1)} %get-tuple-element.17), channel_id=1, source_target_pairs={{0,32},{16,48},{32,0},{48,16},{64,96},{80,112},{96,64},{112,80},{1... | collective-permute-start | bytes 786440 | tf_op jit(solution)/shard_map/ppermute | solution.py:187
  41.2 24.6 %copy-start.3 = (f32[1,1,2,128]{3,2,1,0:T(2,128)S(1)}, f32[1,1,2,128]{3,2,1,0:T(2,128)}, u32[]{:S(2)}) copy-start(f32[1,1,2,128]{3,2,1,0:T(2,128)} %param.11) | copy-start | bytes 3076
  41.2 24.6 %copy-start.2 = (s32[1,1,2,128]{3,2,1,0:T(2,128)S(1)}, s32[1,1,2,128]{3,2,1,0:T(2,128)}, u32[]{:S(2)}) copy-start(s32[1,1,2,128]{3,2,1,0:T(2,128)} %param.10) | copy-start | bytes 3076
  41.3 9.1 %collective-permute-start.2 = (bf16[8,128,128]{2,1,0:T(8,128)(2,1)S(1)}, bf16[8,128,128]{2,1,0:T(8,128)(2,1)S(1)}, u32[]{:S(2)}, u32[]{:S(2)}) collective-permute-start(bf16[8,128,128]{2,1,0:T(8,128)(2,1)S(1)} %get-tuple-element.18), channel_id=1, source_target_pairs={{0,480},{16,496},{32,64},{48,80},{64,32},{80,48},{96,128},{112,144... | collective-permute-start | bytes 786440 | tf_op jit(solution)/shard_map/ppermute | solution.py:188
  51.3 46.0 %all-to-all-start.1 = ((bf16[8,2,128,128]{3,2,1,0:T(8,128)(2,1)}), bf16[8,2,128,128]{3,2,1,0:T(8,128)(2,1)S(1)}, u32[]{:S(2)}, u32[]{:S(2)}) async-start(bf16[8,2,128,128]{3,2,1,0:T(8,128)(2,1)} %copy.21), calls=%async_computation.1 | async-start | bytes 1048576 | tf_op jit(solution)/shard_map/all_to_all | solution.py:190

commit v2 on v1

--- a/solution.py
+++ b/solution.py
@@ -65,7 +65,7 @@
 
 def phase_tables(angles):
     factor = 1.0 / math.sqrt(SWEEPS)
-    return jnp.stack([jnp.cos(angles) * factor, jnp.sin(angles) * factor]).astype(BF16)
+    return jnp.concatenate([jnp.cos(angles) * factor, jnp.sin(angles) * factor], axis=1).astype(BF16)
 
 
 def stencil(offsets, fractions):
@@ -85,58 +85,66 @@
     return weights_sum.astype(BF16)
 
 
-def focus_kernel(slots, tab, z, cu, su, cv, sv, own, other):
-    half = own.shape[1]
+def focus_kernel(row, owners, tab, z, cosines, sines, own, other):
+    half = own.shape[0]
     own[...] = jnp.zeros_like(own)
     other[...] = jnp.zeros_like(other)
     side = BLOCK_SIDE
+    height = own.shape[2]
     sector = z.shape[-1]
+    cb_count = sector // side
     rows = z.shape[0] * z.shape[2]
+    me = owners[0, owners.shape[1] - 1]
     zre = z[:, 0].reshape(rows, sector)
     zim = z[:, 1].reshape(rows, sector)
-    for ab in range(tab.shape[1] // side):
-        span = slice(ab * side, (ab + 1) * side)
-        pc = tab[0, span, :]
-        ps = tab[1, span, :]
-        dot = functools.partial(jnp.dot, preferred_element_type=F32)
-        re = dot(pc, zre) - dot(ps, zim)
-        im = dot(pc, zim) + dot(ps, zre)
-        for cb in range(sector // side):
+    dot = functools.partial(jnp.dot, preferred_element_type=F32)
+    into_re = jnp.concatenate([zre, -zim], axis=0)
+    into_im = jnp.concatenate([zim, zre], axis=0)
+    for ab in range(tab.shape[0] // height):
+        span = slice(ab * height, (ab + 1) * height)
+        re = dot(tab[span, :], into_re)
+        im = dot(tab[span, :], into_im)
+        lines = slice(ab * side, (ab + 1) * side)
+        cu = cosines[:, lines].T[row : row + height]
+        su = sines[:, lines].T[row : row + height]
+        for cb in range(cb_count):
             lanes = slice(cb * side, (cb + 1) * side)
-            c0 = cu[span, cb : cb + 1]
-            s0 = su[span, cb : cb + 1]
-            c1 = cv[ab : ab + 1, lanes]
-            s1 = sv[ab : ab + 1, lanes]
+            c0, s0 = cu[:, cb : cb + 1], su[:, cb : cb + 1]
+            c1 = cosines[cb_count + ab : cb_count + ab + 1, lanes]
+            s1 = sines[cb_count + ab : cb_count + ab + 1, lanes]
             cosine = c0 * c1 - s0 * s1
             sine = s0 * c1 + c0 * s1
             r, i = re[:, lanes], im[:, lanes]
             dre = (r * cosine - i * sine).astype(BF16).astype(F32)
             dim = (r * sine + i * cosine).astype(BF16).astype(F32)
-            slot = slots[ab * (sector // side) + cb]
-
-            def add(ref, index):
-                ref[0, index] = (ref[0, index].astype(F32) + dre).astype(BF16)
-                ref[1, index] = (ref[1, index].astype(F32) + dim).astype(BF16)
-
-            @pl.when(slot < half)
+            owner = owners[0, ab * cb_count + cb]
+            apart = owner ^ me
+            index = ((apart >> 1) & 1) * (half // 2) + (owner >> 2)
+
+            def add(ref):
+                ref[index, 0] = (ref[index, 0].astype(F32) + dre).astype(BF16)
+                ref[index, 1] = (ref[index, 1].astype(F32) + dim).astype(BF16)
+
+            @pl.when((apart & 1) == 0)
             def _():
-                add(own, slot)
-
-            @pl.when(slot >= half)
+                add(own)
+
+            @pl.when((apart & 1) == 1)
             def _():
-                add(other, slot - half)
-
-
-def focus(slots, tab, z, cu, su, cv, sv, half):
-    shape = jax.ShapeDtypeStruct((2, half, BLOCK_SIDE, BLOCK_SIDE), BF16)
+                add(other)
+
+
+def focus(part, owners, tab, z, cosines, sines, slots):
+    height = BLOCK_SIDE // 2
+    shape = pltpu.VMEM((slots, 2, height, BLOCK_SIDE), BF16)
     vmem = pl.BlockSpec(memory_space=pltpu.VMEM)
     return pl.pallas_call(
-        focus_kernel,
+        functools.partial(focus_kernel, part * height),
         out_shape=(shape, shape),
-        in_specs=[pl.BlockSpec(memory_space=pltpu.SMEM)] + [vmem] * 6,
+        in_specs=[pl.BlockSpec(memory_space=pltpu.SMEM)] + [vmem] * 4,
         out_specs=(vmem, vmem),
         name="focus",
-    )(slots, tab, z, cu, su, cv, sv)
+    )(owners, *(pltpu.with_memory_space_constraint(x, pltpu.VMEM) for x in (tab, z, cosines, sines)))
 
 
 def on_device(
@@ -159,36 +167,33 @@
     by_sector = spectrum.reshape(2, sweep_count, members, sector).transpose(2, 0, 1, 3)
     z = lax.all_to_all(by_sector, "mem", split_axis=0, concat_axis=0, tiled=True)
 
-    tables = phase_tables(bearing_rotation_table[0, 0])
+    height = BLOCK_SIDE // 2
+    angles = bearing_rotation_table[0, 0].reshape(ab_count, 2, height, SWEEPS)
+    tables = [phase_tables(angles[:, part].reshape(ANGLES // 2, SWEEPS)) for part in range(2)]
     positions = jnp.arange(BLOCK_SIDE, dtype=F32)
     slope = modulation_slope[0, 0].reshape(2, ab_count, cb_count)
-    u_phase = (slope[0][:, None, :] * positions[None, :, None]).reshape(ANGLES, cb_count)
-    v_phase = (slope[1][:, :, None] * positions[None, None, :]).reshape(ab_count, sector)
-
-    me = lax.axis_index("sub")
-    owners = patch_subset_holder[0, 0]
-    apart = owners ^ me
-    slots = (apart & 1) * chips + ((apart >> 1) & 1) * (chips // 2) + (owners >> 2)
-
-    own, other = focus(
-        slots, tables, z, jnp.cos(u_phase), jnp.sin(u_phase), jnp.cos(v_phase), jnp.sin(v_phase), chips
-    )
+    u_phase = slope[0].T[:, :, None] * positions
+    v_phase = slope[1][:, :, None] * positions
+    phase = jnp.concatenate([u_phase, v_phase]).reshape(cb_count + ab_count, sector)
+    cosines, sines = jnp.cos(phase), jnp.sin(phase)
+
+    me = lax.axis_index("sub").astype(jnp.int32)
+    owners = jnp.concatenate([patch_subset_holder[0], me.reshape(1, 1)], axis=1)
     core_swap = [(i, i ^ 1) for i in range(groups)]
-    held = own + lax.ppermute(other, "sub", core_swap)
-
-    def partner(z, shift):
-        w = z + shift
-        return ((w ^ 1) - shift) % chips
 
     def pairing(shift):
-        return [(2 * z + c, 2 * partner(z, shift) + c) for z in range(chips) for c in range(2)]
+        partner = lambda z: (((z + shift) ^ 1) - shift) % chips
+        return [(2 * z + c, 2 * partner(z) + c) for z in range(chips) for c in range(2)]
 
     kept = chips // 2
-    first = held[0, :kept] + lax.ppermute(held[0, kept:], "sub", pairing(0))
-    second = held[1, :kept] + lax.ppermute(held[1, kept:], "sub", pairing(1))
+    parts = []
+    for part in range(2):
+        own, other = focus(part, owners, tables[part], z, cosines, sines, chips)
+        held = own + lax.ppermute(other, "sub", core_swap)
+        parts.append(held[:kept] + lax.ppermute(held[kept:], "sub", pairing(part)))
     alike = [[2 * z + c for z in range(par, chips, 2)] for par in range(2) for c in range(2)]
     arrived = lax.all_to_all(
-        jnp.stack([first, second], axis=1),
+        jnp.stack(parts, axis=1),
         "sub",
         split_axis=0,
         concat_axis=0,
@@ -196,6 +201,7 @@
         axis_index_groups=alike,
     )
     gathered = jnp.sum(arrived.astype(F32), axis=0).astype(BF16)
+    gathered = gathered.transpose(1, 0, 2, 3).reshape(2, BLOCK_SIDE, BLOCK_SIDE)
     own_tables = stencil(regrid_lead_cell[0, 0], regrid_weight[0, 0])
     rows_done = jnp.einsum(
         "ya,pac->pyc", own_tables[0], gathered, preferred_element_type=F32

time: 98.9 us -> 97.1 us (0.982)
  other arithmetic: 9.79 us -> 5.43 us
  starting transfers between devices: 30.7 us -> 32.6 us
    all_to_all x1, waiting for transfers between devices: 4.22 us -> 7.27 us  [on_device(): lax.all_to_all(by_sector, 'mem', split_axis=0, concat_axis=0, tiled=True)]
    ppermute x1 -> x2, waiting for transfers between devices: 2.48 us -> 0.01 us  [on_device(): held = own + lax.ppermute(other, 'sub', core_swap)]
    sin x2 -> x1, other arithmetic: 2.52 us -> 0.08 us  [on_device(): cosines, sines = (jnp.cos(phase), jnp.sin(phase))]
    ppermute x1 -> x2, starting transfers between devices: 3.97 us -> 5.9 us  [on_device(): held = own + lax.ppermute(other, 'sub', core_swap)]
    mul x1, other arithmetic: 1.92 us -> 0.01 us  [on_device(): u_phase = slope[0].T[:, :, None] * positions]
    add x1 -> x2, other arithmetic: 1.59 us -> 0.39 us  [on_device(): held = own + lax.ppermute(other, 'sub', core_swap)]
    another operation x6 -> x7, other arithmetic: 1.65 us -> 2.73 us  [the longest x1 0.86 us: phase_tables(): jnp.stack([jnp.cos(angles) * factor, jnp.sin(angles) * factor]).astype(BF16)]
    pallas_call x1 -> x2, Pallas kernels: 5.8 us -> 6.66 us  [focus(): pl.pallas_call(functools.partial(focus_kernel, part * height), out_shape=...]
  transfers between devices with their start and end apart: 5 -> 6, of which waited for: 5 -> 4; matrix products, arithmetic and copies ran while one was open for 6% -> 4% of each run, Pallas kernels for 0% -> 3%
where the time goes in v2:
time: 97.1 us; the launch traced here: 96.6 us
  waiting for transfers between devices  45.5 us (47%)
  starting transfers between devices  32.6 us (34%)
  Pallas kernels  6.66 us (7%)
  other arithmetic  5.43 us (6%)
  local copies, waits for them, and re-layouts  4.27 us (4%)
  matrix products  1.86 us (2%)
    all_to_all x1, waiting for transfers between devices, on_device(): lax.all_to_all(jnp.stack(parts, axis=1), 'sub', split_axis=0, concat_axis...  31.2 us
    all_to_all x1, starting transfers between devices, on_device(): lax.all_to_all(jnp.stack(parts, axis=1), 'sub', split_axis=0, concat_axis...  14.5 us
    all_to_all x1, waiting for transfers between devices, on_device(): lax.all_to_all(by_sector, 'mem', split_axis=0, concat_axis=0, tiled=True)  7.27 us
    ppermute x2, waiting for transfers between devices, on_device(): parts.append(held[:kept] + lax.ppermute(held[kept:], 'sub', pairing(part)))  6.99 us
    all_to_all x1, starting transfers between devices, on_device(): lax.all_to_all(by_sector, 'mem', split_axis=0, concat_axis=0, tiled=True)  6.75 us
    pallas_call x2, Pallas kernels, focus(): pl.pallas_call(functools.partial(focus_kernel, part * height), out_shape=...  6.66 us
    ppermute x2, starting transfers between devices, on_device(): held = own + lax.ppermute(other, 'sub', core_swap)  5.9 us
    ppermute x2, starting transfers between devices, on_device(): parts.append(held[:kept] + lax.ppermute(held[kept:], 'sub', pairing(part)))  5.46 us
  transfers between devices with their start and end apart: 6, of which 4 were waited for; matrix products, arithmetic and copies ran while one was open for 4% of the time, Pallas kernels for 3%

profile of v2, /device:TPU:65, one launch (start us, length us, event | category | flops | bytes accessed | tf_op | source)
XLA Modules:
  0.0 96.6 jit_solution(11078233456179365113)
XLA Ops:
  0.3 0.3 sine_convert_fusion
  0.6 1.2 %copy.37 = bf16[4,8,64,128]{3,2,1,0:T(8,128)(2,1)S(1)} copy(bf16[4,8,64,128]{3,1,2,0:T(8,128)(2,1)} %bitcast.123) | data formatting | bytes 1048576
  1.8 0.4 convolution_bitcast_fusion.1
  2.2 0.2 subtract_convert_fusion
  2.4 0.4 convolution_bitcast_fusion
  2.8 0.2 slice_subtract_fusion
  3.0 0.3 copy.18
  3.4 0.3 sub.70
  3.7 0.3 copy.20
  4.0 0.3 copy.19
  4.3 0.3 add.163
  4.6 0.3 copy.21
  4.9 0.9 fusion.4
  5.9 6.7 %all-to-all-start = ((bf16[16,2,16,512]{3,2,1,0:T(8,128)(2,1)}), bf16[16,2,16,512]{3,2,1,0:T(8,128)(2,1)S(1)}, u32[]{:S(2)}, u32[]{:S(2)}) async-start(bf16[16,2,16,512]{3,2,1,0:T(8,128)(2,1)} %fusion.4), calls=%async_computation | async-start | bytes 1048576 | tf_op jit(solution)/shard_map/all_to_all | solution.py:168
  13.0 0.6 pad_add_fusion.owners
  13.7 2.0 %multiply_convert_fusion.3 = (bf16[4,1,64,256]{3,2,0,1:T(8,128)(2,1)S(1)}, bf16[4,1,64,256]{3,2,0,1:T(8,128)(2,1)S(1)}, bf16[4,1,64,256]{3,2,0,1:T(8,128)(2,1)S(1)}, bf16[4,1,64,256]{3,2,0,1:T(8,128)(2,1)S(1)}) fusion(f32[4,2,64,256]{3,2,1,0:T(8,128)S(1)} %bitcast.124), kind=kLoop, calls=%fused_computation.33 | loop fusion | flops 524288 | bytes 1048576 | tf_op jit(solution)/shard_map/convert.14
  15.7 7.3 %all-to-all-done.z = bf16[16,2,16,512]{3,2,1,0:T(8,128)(2,1)S(1)} async-done(((bf16[16,2,16,512]{3,2,1,0:T(8,128)(2,1)}), bf16[16,2,16,512]{3,2,1,0:T(8,128)(2,1)S(1)}, u32[]{:S(2)}, u32[]{:S(2)}) %all-to-all-start) | async-done | bytes 524320 | tf_op jit(solution)/shard_map/all_to_all | solution.py:168
  23.0 3.3 %focus.2 = (bf16[16,2,64,128]{3,2,1,0:T(8,128)(2,1)S(1)}, bf16[16,2,64,128]{3,2,1,0:T(8,128)(2,1)S(1)}) custom-call(s32[1,17]{1,0:T(1,128)} %pad_add_fusion.owners, bf16[256,512]{1,0:T(8,128)(2,1)S(1)} %pad_maximum_fusion.1.tab, bf16[16,2,16,512]{3,2,1,0:T(8,128)(2,1)S(1)} %all-to-all-done.z, f32[8,512]{1,0:T(8,128)S(1)} %get-tuple-element.24.cosines, ...), custom_call_target="tpu_custom_call" | custom-call | tf_op jit(solution)/shard_map/focus/pallas_call | solution.py:141
  26.3 4.0 %collective-permute-start = (bf16[16,2,64,128]{3,2,1,0:T(8,128)(2,1)S(1)}, bf16[16,2,64,128]{3,2,1,0:T(8,128)(2,1)S(1)}, u32[]{:S(2)}, u32[]{:S(2)}) collective-permute-start(bf16[16,2,64,128]{3,2,1,0:T(8,128)(2,1)S(1)} %get-tuple-element.10), channel_id=1, source_target_pairs={{0,16},{16,0},{32,48},{48,32},{64,80},{80,64},{96,112},{112,96},{1... | collective-permute-start | bytes 1572872 | tf_op jit(solution)/shard_map/ppermute | solution.py:192
  30.3 3.4 %focus.3 = (bf16[16,2,64,128]{3,2,1,0:T(8,128)(2,1)S(1)}, bf16[16,2,64,128]{3,2,1,0:T(8,128)(2,1)S(1)}) custom-call(s32[1,17]{1,0:T(1,128)} %pad_add_fusion.owners, bf16[256,512]{1,0:T(8,128)(2,1)S(1)} %pad_maximum_fusion.2.tab, bf16[16,2,16,512]{3,2,1,0:T(8,128)(2,1)S(1)} %all-to-all-done.z, f32[8,512]{1,0:T(8,128)S(1)} %get-tuple-element.24.cosines, ...), custom_call_target="tpu_custom_call" | custom-call | tf_op jit(solution)/shard_map/focus/pallas_call | solution.py:141
  33.7 1.9 %collective-permute-start.2 = (bf16[16,2,64,128]{3,2,1,0:T(8,128)(2,1)S(1)}, bf16[16,2,64,128]{3,2,1,0:T(8,128)(2,1)S(1)}, u32[]{:S(2)}, u32[]{:S(2)}) collective-permute-start(bf16[16,2,64,128]{3,2,1,0:T(8,128)(2,1)S(1)} %get-tuple-element.12), channel_id=1, source_target_pairs={{0,16},{16,0},{32,48},{48,32},{64,80},{80,64},{96,112},{112,96},{1... | collective-permute-start | bytes 1572872 | tf_op jit(solution)/shard_map/ppermute | solution.py:192
  35.6 0.2 add.164
  35.9 3.5 %collective-permute-start.1 = (bf16[8,2,64,128]{3,2,1,0:T(8,128)(2,1)S(1)}, bf16[8,2,64,128]{3,2,1,0:T(8,128)(2,1)S(1)}, u32[]{:S(2)}, u32[]{:S(2)}) collective-permute-start(bf16[8,2,64,128]{3,2,1,0:T(8,128)(2,1)S(1)} %slice.84), channel_id=1, source_target_pairs={{0,32},{16,48},{32,0},{48,16},{64,96},{80,112},{96,64},{112,80},{1... | collective-permute-start | bytes 786440 | tf_op jit(solution)/shard_map/ppermute | solution.py:193
  39.4 0.2 add.166
  39.6 1.9 %collective-permute-start.3 = (bf16[8,2,64,128]{3,2,1,0:T(8,128)(2,1)S(1)}, bf16[8,2,64,128]{3,2,1,0:T(8,128)(2,1)S(1)}, u32[]{:S(2)}, u32[]{:S(2)}) collective-permute-start(bf16[8,2,64,128]{3,2,1,0:T(8,128)(2,1)S(1)} %slice.87), channel_id=1, source_target_pairs={{0,480},{16,496},{32,64},{48,80},{64,32},{80,48},{96,128},{112,144... | collective-permute-start | bytes 786440 | tf_op jit(solution)/shard_map/ppermute | solution.py:193
  41.6 3.9 %collective-permute-done.1 = bf16[8,2,64,128]{3,2,1,0:T(8,128)(2,1)S(1)} collective-permute-done((bf16[8,2,64,128]{3,2,1,0:T(8,128)(2,1)S(1)}, bf16[8,2,64,128]{3,2,1,0:T(8,128)(2,1)S(1)}, u32[]{:S(2)}, u32[]{:S(2)}) %collective-permute-start.1) | collective-permute-done | bytes 262176 | tf_op jit(solution)/shard_map/ppermute | solution.py:193
  45.5 3.1 %collective-permute-done.3 = bf16[8,2,64,128]{3,2,1,0:T(8,128)(2,1)S(1)} collective-permute-done((bf16[8,2,64,128]{3,2,1,0:T(8,128)(2,1)S(1)}, bf16[8,2,64,128]{3,2,1,0:T(8,128)(2,1)S(1)}, u32[]{:S(2)}, u32[]{:S(2)}) %collective-permute-start.3) | collective-permute-done | bytes 262176 | tf_op jit(solution)/shard_map/ppermute | solution.py:193
  48.7 0.8 copy.24
  49.6 14.5 %all-to-all-start.1 = ((bf16[8,2,2,64,128]{4,3,2,1,0:T(8,128)(2,1)}), bf16[8,2,2,64,128]{4,3,2,1,0:T(8,128)(2,1)S(1)}, u32[]{:S(2)}, u32[]{:S(2)}) async-start(bf16[8,2,2,64,128]{4,3,2,1,0:T(8,128)(2,1)} %copy.24), calls=%async_computation.1 | async-start | bytes 1048576 | tf_op jit(solution)/shard_map/all_to_all | solution.py:195
  64.1 0.2 add_convert_fusion.1
  64.3 31.2 %all-to-all-done.1 = bf16[8,2,2,64,128]{4,3,2,1,0:T(8,128)(2,1)S(1)} async-done(((bf16[8,2,2,64,128]{4,3,2,1,0:T(8,128)(2,1)}), bf16[8,2,2,64,128]{4,3,2,1,0:T(8,128)(2,1)S(1)}, u32[]{:S(2)}, u32[]{:S(2)}) %all-to-all-start.1) | async-done | bytes 524320 | tf_op jit(solution)/shard_map/all_to_all | solution.py:195
  95.6 1.0 %fusion.1 = bf16[1,2,128,128]{3,2,1,0:T(8,128)(2,1)} fusion(bf16[2,128,128]{2,1,0:T(8,128)(2,1)S(1)} %bitcast.129, bf16[2,128,128]{2,1,0:T(8,128)(2,1)S(1)} %add_convert_fusion.1), kind=kOutput, calls=%fused_computation.5 | convolution fusion | flops 16875520 | bytes 196608 | tf_op jit(solution)/shard_map/pyc,xc->pyx/dot_general | solution.py:209
  (32 shorter events, 1.1 us)
Async XLA Ops:
  4.6 8.1 %copy-start.3 = (f32[1,1,2,16]{3,2,1,0:T(2,128)S(1)}, f32[1,1,2,16]{3,2,1,0:T(2,128)}, u32[]{:S(2)}) copy-start(f32[1,1,2,16]{3,2,1,0:T(2,128)} %param.9) | copy-start | bytes 388
  4.6 8.4 %copy-start.4 = (s32[1,1,16]{2,1,0:T(1,128)S(1)}, s32[1,1,16]{2,1,0:T(1,128)}, u32[]{:S(2)}) copy-start(s32[1,1,16]{2,1,0:T(1,128)} %param.8) | copy-start | bytes 196
  4.6 9.1 %copy-start = (f32[1,1,512,256]{3,2,1,0:T(8,128)S(1)}, f32[1,1,512,256]{3,2,1,0:T(8,128)}, u32[]{:S(2)}) copy-start(f32[1,1,512,256]{3,2,1,0:T(8,128)} %param.7) | copy-start | bytes 1572868
  5.9 17.1 %all-to-all-start = ((bf16[16,2,16,512]{3,2,1,0:T(8,128)(2,1)}), bf16[16,2,16,512]{3,2,1,0:T(8,128)(2,1)S(1)}, u32[]{:S(2)}, u32[]{:S(2)}) async-start(bf16[16,2,16,512]{3,2,1,0:T(8,128)(2,1)} %fusion.4), calls=%async_computation | async-start | bytes 1048576 | tf_op jit(solution)/shard_map/all_to_all | solution.py:168
  26.3 9.3 %collective-permute-start = (bf16[16,2,64,128]{3,2,1,0:T(8,128)(2,1)S(1)}, bf16[16,2,64,128]{3,2,1,0:T(8,128)(2,1)S(1)}, u32[]{:S(2)}, u32[]{:S(2)}) collective-permute-start(bf16[16,2,64,128]{3,2,1,0:T(8,128)(2,1)S(1)} %get-tuple-element.10), channel_id=1, source_target_pairs={{0,16},{16,0},{32,48},{48,32},{64,80},{80,64},{96,112},{112,96},{1... | collective-permute-start | bytes 1572872 | tf_op jit(solution)/shard_map/ppermute | solution.py:192
  33.7 5.7 %collective-permute-start.2 = (bf16[16,2,64,128]{3,2,1,0:T(8,128)(2,1)S(1)}, bf16[16,2,64,128]{3,2,1,0:T(8,128)(2,1)S(1)}, u32[]{:S(2)}, u32[]{:S(2)}) collective-permute-start(bf16[16,2,64,128]{3,2,1,0:T(8,128)(2,1)S(1)} %get-tuple-element.12), channel_id=1, source_target_pairs={{0,16},{16,0},{32,48},{48,32},{64,80},{80,64},{96,112},{112,96},{1... | collective-permute-start | bytes 1572872 | tf_op jit(solution)/shard_map/ppermute | solution.py:192
  35.9 9.6 %collective-permute-start.1 = (bf16[8,2,64,128]{3,2,1,0:T(8,128)(2,1)S(1)}, bf16[8,2,64,128]{3,2,1,0:T(8,128)(2,1)S(1)}, u32[]{:S(2)}, u32[]{:S(2)}) collective-permute-start(bf16[8,2,64,128]{3,2,1,0:T(8,128)(2,1)S(1)} %slice.84), channel_id=1, source_target_pairs={{0,32},{16,48},{32,0},{48,16},{64,96},{80,112},{96,64},{112,80},{1... | collective-permute-start | bytes 786440 | tf_op jit(solution)/shard_map/ppermute | solution.py:193
  39.6 9.0 %collective-permute-start.3 = (bf16[8,2,64,128]{3,2,1,0:T(8,128)(2,1)S(1)}, bf16[8,2,64,128]{3,2,1,0:T(8,128)(2,1)S(1)}, u32[]{:S(2)}, u32[]{:S(2)}) collective-permute-start(bf16[8,2,64,128]{3,2,1,0:T(8,128)(2,1)S(1)} %slice.87), channel_id=1, source_target_pairs={{0,480},{16,496},{32,64},{48,80},{64,32},{80,48},{96,128},{112,144... | collective-permute-start | bytes 786440 | tf_op jit(solution)/shard_map/ppermute | solution.py:193
  45.5 18.6 %copy-start.2 = (f32[1,1,2,128]{3,2,1,0:T(2,128)S(1)}, f32[1,1,2,128]{3,2,1,0:T(2,128)}, u32[]{:S(2)}) copy-start(f32[1,1,2,128]{3,2,1,0:T(2,128)} %param.11) | copy-start | bytes 3076
  45.5 18.6 %copy-start.1 = (s32[1,1,2,128]{3,2,1,0:T(2,128)S(1)}, s32[1,1,2,128]{3,2,1,0:T(2,128)}, u32[]{:S(2)}) copy-start(s32[1,1,2,128]{3,2,1,0:T(2,128)} %param.10) | copy-start | bytes 3076
  49.6 46.0 %all-to-all-start.1 = ((bf16[8,2,2,64,128]{4,3,2,1,0:T(8,128)(2,1)}), bf16[8,2,2,64,128]{4,3,2,1,0:T(8,128)(2,1)S(1)}, u32[]{:S(2)}, u32[]{:S(2)}) async-start(bf16[8,2,2,64,128]{4,3,2,1,0:T(8,128)(2,1)} %copy.24), calls=%async_computation.1 | async-start | bytes 1048576 | tf_op jit(solution)/shard_map/all_to_all | solution.py:195

commit v3 on v2

v3 whole, which is shorter than its diff:
```python
import functools
import math

import jax
import jax.numpy as jnp
import numpy as np
from jax import lax
from jax.experimental import pallas as pl
from jax.experimental.pallas import tpu as pltpu
from jax.sharding import PartitionSpec as P

FREQUENCIES = 8192
FIRST_RADIX = 64
SECOND_RADIX = 128
SWEEPS = 256
ANGLES = 512
BLOCK_SIDE = 128
F32 = jnp.float32
BF16 = jnp.bfloat16


def range_constants():
    def table(length, rows):
        turns = np.outer(rows, np.arange(length)) % length
        angle = turns * (2.0 * np.pi / length)
        c, s = np.cos(angle), np.sin(angle)
        return np.concatenate([c, -s], axis=1), np.concatenate([s, c], axis=1)

    first = np.concatenate(table(FIRST_RADIX, np.arange(FIRST_RADIX)))
    second = np.concatenate(
        [part for odd in range(2) for part in table(SECOND_RADIX, np.arange(odd, SECOND_RADIX, 2))]
    )
    turns = np.outer(np.arange(FIRST_RADIX), np.arange(SECOND_RADIX)) % FREQUENCIES
    angle = turns * (2.0 * np.pi / FREQUENCIES)
    return (
        jnp.asarray(first.astype(np.float32)).astype(BF16),
        jnp.asarray(second.astype(np.float32)).astype(BF16),
        jnp.asarray(np.stack([np.cos(angle), np.sin(angle)]).astype(np.float32)),
    )


def range_kernel(x, first, second, turn, out, rows, turned, moved):
    sweeps = x.shape[1]
    lanes = SECOND_RADIX
    height = 2 * FIRST_RADIX
    for p in range(2):
        for k2 in range(FIRST_RADIX):
            tile = x[p, :, k2 * lanes : (k2 + 1) * lanes].astype(F32)
            rows[pl.ds(p * FIRST_RADIX + k2, sweeps, stride=height), :] = tile
    cosine, sine = turn[0], turn[1]
    for s in range(0, sweeps, 2):
        pair = [rows[(s + i) * height : (s + i + 1) * height, :].astype(BF16) for i in range(2)]
        product = jnp.dot(first[...], jnp.concatenate(pair, axis=1), preferred_element_type=F32)
        for i in range(2):
            re = product[:FIRST_RADIX, i * lanes : (i + 1) * lanes]
            im = product[FIRST_RADIX:, i * lanes : (i + 1) * lanes]
            span = slice((s + i) * FIRST_RADIX, (s + i + 1) * FIRST_RADIX)
            turned[span, :lanes] = (re * cosine - im * sine).astype(BF16)
            turned[span, lanes:] = (re * sine + im * cosine).astype(BF16)
    factor = 1.0 / math.sqrt(FREQUENCIES)
    low = lax.broadcasted_iota(jnp.int32, (lanes, lanes), 1) < FIRST_RADIX
    for s in range(0, sweeps, 2):
        span = slice(s * FIRST_RADIX, (s + 2) * FIRST_RADIX)
        product = factor * lax.dot_general(
            second[...], turned[span, :], (((1,), (1,)), ((), ())), preferred_element_type=F32
        )
        even, odd = product[:lanes], product[lanes:]
        here = jnp.where(low, even, pltpu.roll(odd, FIRST_RADIX, 1))
        after = jnp.where(low, pltpu.roll(even, FIRST_RADIX, 1), odd)
        moved[pl.ds(s, lanes, stride=sweeps), :] = here
        moved[pl.ds(s + 1, lanes, stride=sweeps), :] = after
    members = out.shape[0]
    cb_count = out.shape[3] // lanes
    for q in range(2):
        for m in range(members):
            for cb in range(cb_count):
                row = ((q * members + m) * cb_count + cb) * sweeps
                out[m, q, :, cb * lanes : (cb + 1) * lanes] = moved[row : row + sweeps, :].astype(BF16)


def range_messages(sweeps, members):
    count = sweeps.shape[1]
    vmem = pl.BlockSpec(memory_space=pltpu.VMEM)
    return pl.pallas_call(
        range_kernel,
        out_shape=jax.ShapeDtypeStruct((members, 2, count, FREQUENCIES // members), BF16),
        in_specs=[vmem] * 4,
        out_specs=vmem,
        scratch_shapes=[
            pltpu.VMEM((count * 2 * FIRST_RADIX, SECOND_RADIX), F32),
            pltpu.VMEM((count * FIRST_RADIX, 2 * SECOND_RADIX), BF16),
            pltpu.VMEM((count * 2 * FIRST_RADIX, SECOND_RADIX), F32),
        ],
        name="range_transform",
    )(sweeps, *range_constants())


def phase_tables(angles):
    factor = 1.0 / math.sqrt(SWEEPS)
    return jnp.concatenate([jnp.cos(angles) * factor, jnp.sin(angles) * factor], axis=1).astype(BF16)


def stencil(offsets, fractions):
    weights = [
        -fractions * (fractions - 1.0) * (fractions - 2.0) / 6.0,
        (fractions + 1.0) * (fractions - 1.0) * (fractions - 2.0) / 2.0,
        -(fractions + 1.0) * fractions * (fractions - 2.0) / 2.0,
        (fractions + 1.0) * fractions * (fractions - 1.0) / 6.0,
    ]
    sources = jnp.arange(fractions.shape[-1], dtype=jnp.int32)
    distance = sources - offsets[..., None]
    weights_sum = jnp.zeros(distance.shape, F32)
    for stencil_tap in range(4):
        weights_sum = weights_sum + jnp.where(
            distance == stencil_tap, weights[stencil_tap][..., None], F32(0.0)
        )
    return weights_sum.astype(BF16)


def focus_kernel(row, owners, tab, z, cosines, sines, own, other, clean, sums):
    side = BLOCK_SIDE
    height = own.shape[2]
    sector = z.shape[-1]
    cb_count = sector // side
    rows = z.shape[0] * z.shape[2]
    zre = z[:, 0].reshape(rows, sector)
    zim = z[:, 1].reshape(rows, sector)
    dot = functools.partial(jnp.dot, preferred_element_type=F32)
    re_all = dot(tab[...], jnp.concatenate([zre, -zim], axis=0))
    im_all = dot(tab[...], jnp.concatenate([zim, zre], axis=0))
    ab_count = tab.shape[0] // height
    for ab in range(ab_count):
        span = slice(ab * height, (ab + 1) * height)
        lines = slice(ab * side, (ab + 1) * side)
        cu = cosines[:, lines].T[row : row + height]
        su = sines[:, lines].T[row : row + height]
        for cb in range(cb_count):
            lanes = slice(cb * side, (cb + 1) * side)
            c0, s0 = cu[:, cb : cb + 1], su[:, cb : cb + 1]
            c1 = cosines[cb_count + ab : cb_count + ab + 1, lanes]
            s1 = sines[cb_count + ab : cb_count + ab + 1, lanes]
            cosine = c0 * c1 - s0 * s1
            sine = s0 * c1 + c0 * s1
            r, i = re_all[span, lanes], im_all[span, lanes]
            clean[ab * cb_count + cb, 0] = (r * cosine - i * sine).astype(BF16)
            clean[ab * cb_count + cb, 1] = (r * sine + i * cosine).astype(BF16)
    sums[...] = jnp.zeros_like(sums)
    blocks = ab_count * cb_count
    me = owners[0, blocks]
    chips = own.shape[0]
    for b in range(blocks):
        owner = owners[0, b]
        apart = owner ^ me
        slot = (apart & 1) * chips + ((apart >> 1) & 1) * (chips // 2) + (owner >> 2)
        sums[slot] = (sums[slot].astype(F32) + clean[b].astype(F32)).astype(BF16)
    own[...] = sums[:chips]
    other[...] = sums[chips:]


def focus(part, owners, tab, z, cosines, sines, slots):
    height = BLOCK_SIDE // 2
    vmem = pl.BlockSpec(memory_space=pltpu.VMEM)
    blocks = owners.shape[1] - 1
    operands = [pltpu.with_memory_space_constraint(x, pltpu.VMEM) for x in (tab, z, cosines, sines)]
    shape = pltpu.VMEM((slots // 2, 2, height, BLOCK_SIDE), BF16)
    return pl.pallas_call(
        functools.partial(focus_kernel, part * height),
        out_shape=(shape, shape),
        in_specs=[pl.BlockSpec(memory_space=pltpu.SMEM)] + [vmem] * 4,
        out_specs=(vmem, vmem),
        scratch_shapes=[pltpu.VMEM((n, 2, height, BLOCK_SIDE), BF16) for n in (blocks, slots)],
        name="focus",
    )(owners, *operands)


def on_device(
    dechirped_echo_matrix,
    bearing_rotation_table,
    patch_subset_holder,
    modulation_slope,
    regrid_lead_cell,
    regrid_weight,
):
    groups = lax.axis_size("sub")
    members = lax.axis_size("mem")
    chips = groups // 2
    sector = FREQUENCIES // members
    ab_count = ANGLES // BLOCK_SIDE
    cb_count = sector // BLOCK_SIDE

    by_sector = range_messages(dechirped_echo_matrix[0], members)
    z = lax.all_to_all(by_sector, "mem", split_axis=0, concat_axis=0, tiled=True)

    height = BLOCK_SIDE // 2
    angles = bearing_rotation_table[0, 0].reshape(ab_count, 2, height, SWEEPS)
    tables = [phase_tables(angles[:, part].reshape(ANGLES // 2, SWEEPS)) for part in range(2)]
    positions = jnp.arange(BLOCK_SIDE, dtype=F32)
    slope = modulation_slope[0, 0].reshape(2, ab_count, cb_count)
    u_phase = slope[0].T[:, :, None] * positions
    v_phase = slope[1][:, :, None] * positions
    phase = jnp.concatenate([u_phase, v_phase]).reshape(cb_count + ab_count, sector)
    cosines, sines = jnp.cos(phase), jnp.sin(phase)

    me = lax.axis_index("sub").astype(jnp.int32)
    owners = jnp.concatenate([patch_subset_holder[0], me.reshape(1, 1)], axis=1)
    core_swap = [(i, i ^ 1) for i in range(groups)]

    def pairing(shift):
        partner = lambda z: (((z + shift) ^ 1) - shift) % chips
        return [(2 * z + c, 2 * partner(z) + c) for z in range(chips) for c in range(2)]

    kept = chips // 2
    parts = []
    for part in range(2):
        own, other = focus(part, owners, tables[part], z, cosines, sines, groups)
        held = own + lax.ppermute(other, "sub", core_swap)
        parts.append(held[:kept] + lax.ppermute(held[kept:], "sub", pairing(part)))
    alike = [[2 * z + c for z in range(par, chips, 2)] for par in range(2) for c in range(2)]
    arrived = lax.all_to_all(
        jnp.concatenate(parts, axis=2),
        "sub",
        split_axis=0,
        concat_axis=0,
        tiled=True,
        axis_index_groups=alike,
    )
    gathered = jnp.sum(arrived.astype(F32), axis=0).astype(BF16)
    own_tables = stencil(regrid_lead_cell[0, 0], regrid_weight[0, 0])
    rows_done = jnp.einsum(
        "ya,pac->pyc", own_tables[0], gathered, preferred_element_type=F32
    ).astype(BF16)
    ground = jnp.einsum("pyc,xc->pyx", rows_done, own_tables[1], preferred_element_type=F32)
    return (0.25 * ground).astype(BF16)[None]


def solution(mesh):
    return jax.shard_map(
        on_device,
        mesh=mesh,
        in_specs=(
            P("sub", None, "mem", None),
            P("sub", "mem", None, None),
            P("sub", "mem", None),
            P("sub", "mem", None, None),
            P("sub", "mem", None, None),
            P("sub", "mem", None, None),
        ),
        out_specs=P(("sub", "mem"), None, None, None),
        check_vma=False,
    )
```

time: 97.1 us -> 90.1 us (0.928)
  the two profiles are of different devices: /device:TPU:65 before, /device:TPU:32 now
where the time goes in v3:
time: 90.1 us; the launch traced here: 89.6 us
  waiting for transfers between devices  42.8 us (48%)
  starting transfers between devices  32.4 us (36%)
  Pallas kernels  6.52 us (7%)
  other arithmetic  4.29 us (5%)
  local copies, waits for them, and re-layouts  2.41 us (3%)
  matrix products  0.93 us (1%)
    all_to_all x1, waiting for transfers between devices, on_device(): lax.all_to_all(jnp.concatenate(parts, axis=2), 'sub', split_axis=0, conca...  29.6 us
    ppermute x2, starting transfers between devices, on_device(): parts.append(held[:kept] + lax.ppermute(held[kept:], 'sub', pairing(part)))  13.4 us
    all_to_all x1, starting transfers between devices, on_device(): lax.all_to_all(jnp.concatenate(parts, axis=2), 'sub', split_axis=0, conca...  7.48 us
    all_to_all x1, starting transfers between devices, on_device(): lax.all_to_all(by_sector, 'mem', split_axis=0, concat_axis=0, tiled=True)  7.17 us
    all_to_all x1, waiting for transfers between devices, on_device(): lax.all_to_all(by_sector, 'mem', split_axis=0, concat_axis=0, tiled=True)  7.08 us
    ppermute x2, waiting for transfers between devices, on_device(): parts.append(held[:kept] + lax.ppermute(held[kept:], 'sub', pairing(part)))  6.15 us
    ppermute x2, starting transfers between devices, on_device(): held = own + lax.ppermute(other, 'sub', core_swap)  4.32 us
    pallas_call x1, Pallas kernels, range_messages(): pl.pallas_call(range_kernel, out_shape=jax.ShapeDtypeStruct((members, 2,...  3.42 us
  transfers between devices with their start and end apart: 6, of which 3 were waited for; matrix products, arithmetic and copies ran while one was open for 4% of the time, Pallas kernels for 2%

profile of v3, /device:TPU:32, one launch (start us, length us, event | category | flops | bytes accessed | tf_op | source)
XLA Modules:
  0.0 89.6 jit_solution(3152264265010986041)
XLA Ops:
  0.0 3.4 %range_transform.1 = bf16[16,2,16,512]{3,2,1,0:T(8,128)(2,1)} custom-call(bf16[2,16,8192]{2,1,0:T(8,128)(2,1)} %bitcast.73, bf16[128,128]{1,0:T(8,128)(2,1)} %constant.51.first, bf16[256,256]{1,0:T(8,128)(2,1)} %constant.52.second, f32[2,64,128]{2,1,0:T(8,128)} %constant.44.clone.turn), custom_call_target="tpu_custom_call" | custom-call | tf_op jit(solution)/shard_map/range_transform/pallas_call | solution.py:84
  3.4 7.2 %all-to-all-start = ((bf16[16,2,16,512]{3,2,1,0:T(8,128)(2,1)}), bf16[16,2,16,512]{3,2,1,0:T(8,128)(2,1)S(1)}, u32[]{:S(2)}, u32[]{:S(2)}) async-start(bf16[16,2,16,512]{3,2,1,0:T(8,128)(2,1)} %range_transform.1), calls=%async_computation | async-start | bytes 1048576 | tf_op jit(solution)/shard_map/all_to_all | solution.py:192
  10.6 0.0 copy-start.3
  10.6 0.7 copy-done.3
  11.3 0.1 mul.138
  11.4 0.1 squeeze.20
  11.5 0.1 copy.11
  11.6 0.1 broadcast_bitcast_fusion
  11.7 0.0 copy-start.4
  11.7 0.6 copy-done.4
  12.3 0.6 pad_add_fusion.owners
  12.9 0.1 fusion.7
  13.0 2.0 %multiply_convert_fusion.3 = (bf16[4,1,64,256]{3,2,0,1:T(8,128)(2,1)S(1)}, bf16[4,1,64,256]{3,2,0,1:T(8,128)(2,1)S(1)}, bf16[4,1,64,256]{3,2,0,1:T(8,128)(2,1)S(1)}, bf16[4,1,64,256]{3,2,0,1:T(8,128)(2,1)S(1)}) fusion(f32[4,2,64,256]{3,2,1,0:T(8,128)S(1)} %bitcast.74), kind=kLoop, calls=%fused_computation.15 | loop fusion | flops 524288 | bytes 1048576 | tf_op jit(solution)/shard_map/convert.8
  15.0 7.1 %all-to-all-done.z = bf16[16,2,16,512]{3,2,1,0:T(8,128)(2,1)S(1)} async-done(((bf16[16,2,16,512]{3,2,1,0:T(8,128)(2,1)}), bf16[16,2,16,512]{3,2,1,0:T(8,128)(2,1)S(1)}, u32[]{:S(2)}, u32[]{:S(2)}) %all-to-all-start) | async-done | bytes 524320 | tf_op jit(solution)/shard_map/all_to_all | solution.py:192
  22.1 1.6 %focus.3 = (bf16[16,2,64,128]{3,2,1,0:T(8,128)(2,1)S(1)}, bf16[16,2,64,128]{3,2,1,0:T(8,128)(2,1)S(1)}) custom-call(s32[1,17]{1,0:T(1,128)} %pad_add_fusion.owners, bf16[256,512]{1,0:T(8,128)(2,1)S(1)} %pad_maximum_fusion.2.tab, bf16[16,2,16,512]{3,2,1,0:T(8,128)(2,1)S(1)} %all-to-all-done.z, f32[8,512]{1,0:T(8,128)S(1)} %get-tuple-element.20.cosines, ...), custom_call_target="tpu_custom_call" | custom-call | tf_op jit(solution)/shard_map/focus/pallas_call | solution.py:166
  23.7 1.9 %collective-permute-start.2 = (bf16[16,2,64,128]{3,2,1,0:T(8,128)(2,1)S(1)}, bf16[16,2,64,128]{3,2,1,0:T(8,128)(2,1)S(1)}, u32[]{:S(2)}, u32[]{:S(2)}) collective-permute-start(bf16[16,2,64,128]{3,2,1,0:T(8,128)(2,1)S(1)} %get-tuple-element.12), channel_id=1, source_target_pairs={{0,16},{16,0},{32,48},{48,32},{64,80},{80,64},{96,112},{112,96},{1... | collective-permute-start | bytes 1572872 | tf_op jit(solution)/shard_map/ppermute | solution.py:216
  25.6 1.5 %focus.2 = (bf16[16,2,64,128]{3,2,1,0:T(8,128)(2,1)S(1)}, bf16[16,2,64,128]{3,2,1,0:T(8,128)(2,1)S(1)}) custom-call(s32[1,17]{1,0:T(1,128)} %pad_add_fusion.owners, bf16[256,512]{1,0:T(8,128)(2,1)S(1)} %pad_maximum_fusion.1.tab, bf16[16,2,16,512]{3,2,1,0:T(8,128)(2,1)S(1)} %all-to-all-done.z, f32[8,512]{1,0:T(8,128)S(1)} %get-tuple-element.20.cosines, ...), custom_call_target="tpu_custom_call" | custom-call | tf_op jit(solution)/shard_map/focus/pallas_call | solution.py:166
  27.2 2.4 %collective-permute-start = (bf16[16,2,64,128]{3,2,1,0:T(8,128)(2,1)S(1)}, bf16[16,2,64,128]{3,2,1,0:T(8,128)(2,1)S(1)}, u32[]{:S(2)}, u32[]{:S(2)}) collective-permute-start(bf16[16,2,64,128]{3,2,1,0:T(8,128)(2,1)S(1)} %get-tuple-element.10), channel_id=1, source_target_pairs={{0,16},{16,0},{32,48},{48,32},{64,80},{80,64},{96,112},{112,96},{1... | collective-permute-start | bytes 1572872 | tf_op jit(solution)/shard_map/ppermute | solution.py:216
  29.6 0.0 collective-permute-done.2
  29.6 0.2 add.60
  29.8 3.8 %collective-permute-start.3 = (bf16[8,2,64,128]{3,2,1,0:T(8,128)(2,1)S(1)}, bf16[8,2,64,128]{3,2,1,0:T(8,128)(2,1)S(1)}, u32[]{:S(2)}, u32[]{:S(2)}) collective-permute-start(bf16[8,2,64,128]{3,2,1,0:T(8,128)(2,1)S(1)} %slice.48), channel_id=1, source_target_pairs={{0,480},{16,496},{32,64},{48,80},{64,32},{80,48},{96,128},{112,144... | collective-permute-start | bytes 786440 | tf_op jit(solution)/shard_map/ppermute | solution.py:217
  33.7 0.2 add.58
  33.9 9.6 %collective-permute-start.1 = (bf16[8,2,64,128]{3,2,1,0:T(8,128)(2,1)S(1)}, bf16[8,2,64,128]{3,2,1,0:T(8,128)(2,1)S(1)}, u32[]{:S(2)}, u32[]{:S(2)}) collective-permute-start(bf16[8,2,64,128]{3,2,1,0:T(8,128)(2,1)S(1)} %slice.45), channel_id=1, source_target_pairs={{0,32},{16,48},{32,0},{48,16},{64,96},{80,112},{96,64},{112,80},{1... | collective-permute-start | bytes 786440 | tf_op jit(solution)/shard_map/ppermute | solution.py:217
  43.5 6.1 %collective-permute-done.1 = bf16[8,2,64,128]{3,2,1,0:T(8,128)(2,1)S(1)} collective-permute-done((bf16[8,2,64,128]{3,2,1,0:T(8,128)(2,1)S(1)}, bf16[8,2,64,128]{3,2,1,0:T(8,128)(2,1)S(1)}, u32[]{:S(2)}, u32[]{:S(2)}) %collective-permute-start.1) | collective-permute-done | bytes 262176 | tf_op jit(solution)/shard_map/ppermute | solution.py:217
  49.7 0.8 pad_maximum_fusion
  50.6 7.5 %all-to-all-start.1 = ((bf16[8,2,128,128]{3,2,1,0:T(8,128)(2,1)}), bf16[8,2,128,128]{3,2,1,0:T(8,128)(2,1)S(1)}, u32[]{:S(2)}, u32[]{:S(2)}) async-start(bf16[8,2,128,128]{3,2,1,0:T(8,128)(2,1)} %pad_maximum_fusion), calls=%async_computation.1 | async-start | bytes 1048576 | tf_op jit(solution)/shard_map/all_to_all | solution.py:219
  58.1 0.0 copy-start.1
  58.1 0.7 copy-done.1
  58.7 0.2 add_convert_fusion
  59.0 29.6 %all-to-all-done.1 = bf16[8,2,128,128]{3,2,1,0:T(8,128)(2,1)S(1)} async-done(((bf16[8,2,128,128]{3,2,1,0:T(8,128)(2,1)}), bf16[8,2,128,128]{3,2,1,0:T(8,128)(2,1)S(1)}, u32[]{:S(2)}, u32[]{:S(2)}) %all-to-all-start.1) | async-done | bytes 524320 | tf_op jit(solution)/shard_map/all_to_all | solution.py:219
  88.6 0.1 reduce_sum.12
  88.6 0.9 %fusion.1 = bf16[1,2,128,128]{3,2,1,0:T(8,128)(2,1)} fusion(bf16[2,128,128]{2,1,0:T(8,128)(2,1)S(1)} %reduce_sum.12, bf16[2,128,128]{2,1,0:T(8,128)(2,1)S(1)} %add_convert_fusion), kind=kOutput, calls=%fused_computation.3 | convolution fusion | flops 16875520 | bytes 196608 | tf_op jit(solution)/shard_map/pyc,xc->pyx/dot_general | solution.py:232
  (16 shorter events, 0.2 us)
Async XLA Ops:
  3.4 9.6 %copy-start = (f32[1,1,512,256]{3,2,1,0:T(8,128)S(1)}, f32[1,1,512,256]{3,2,1,0:T(8,128)}, u32[]{:S(2)}) copy-start(f32[1,1,512,256]{3,2,1,0:T(8,128)} %param.10) | copy-start | bytes 1572868
  3.4 18.7 %all-to-all-start = ((bf16[16,2,16,512]{3,2,1,0:T(8,128)(2,1)}), bf16[16,2,16,512]{3,2,1,0:T(8,128)(2,1)S(1)}, u32[]{:S(2)}, u32[]{:S(2)}) async-start(bf16[16,2,16,512]{3,2,1,0:T(8,128)(2,1)} %range_transform.1), calls=%async_computation | async-start | bytes 1048576 | tf_op jit(solution)/shard_map/all_to_all | solution.py:192
  10.6 0.7 copy-start.3
  11.7 0.7 copy-start.4
  23.7 5.9 %collective-permute-start.2 = (bf16[16,2,64,128]{3,2,1,0:T(8,128)(2,1)S(1)}, bf16[16,2,64,128]{3,2,1,0:T(8,128)(2,1)S(1)}, u32[]{:S(2)}, u32[]{:S(2)}) collective-permute-start(bf16[16,2,64,128]{3,2,1,0:T(8,128)(2,1)S(1)} %get-tuple-element.12), channel_id=1, source_target_pairs={{0,16},{16,0},{32,48},{48,32},{64,80},{80,64},{96,112},{112,96},{1... | collective-permute-start | bytes 1572872 | tf_op jit(solution)/shard_map/ppermute | solution.py:216
  27.2 6.5 %collective-permute-start = (bf16[16,2,64,128]{3,2,1,0:T(8,128)(2,1)S(1)}, bf16[16,2,64,128]{3,2,1,0:T(8,128)(2,1)S(1)}, u32[]{:S(2)}, u32[]{:S(2)}) collective-permute-start(bf16[16,2,64,128]{3,2,1,0:T(8,128)(2,1)S(1)} %get-tuple-element.10), channel_id=1, source_target_pairs={{0,16},{16,0},{32,48},{48,32},{64,80},{80,64},{96,112},{112,96},{1... | collective-permute-start | bytes 1572872 | tf_op jit(solution)/shard_map/ppermute | solution.py:216
  29.8 13.7 %collective-permute-start.3 = (bf16[8,2,64,128]{3,2,1,0:T(8,128)(2,1)S(1)}, bf16[8,2,64,128]{3,2,1,0:T(8,128)(2,1)S(1)}, u32[]{:S(2)}, u32[]{:S(2)}) collective-permute-start(bf16[8,2,64,128]{3,2,1,0:T(8,128)(2,1)S(1)} %slice.48), channel_id=1, source_target_pairs={{0,480},{16,496},{32,64},{48,80},{64,32},{80,48},{96,128},{112,144... | collective-permute-start | bytes 786440 | tf_op jit(solution)/shard_map/ppermute | solution.py:217
  33.9 15.8 %collective-permute-start.1 = (bf16[8,2,64,128]{3,2,1,0:T(8,128)(2,1)S(1)}, bf16[8,2,64,128]{3,2,1,0:T(8,128)(2,1)S(1)}, u32[]{:S(2)}, u32[]{:S(2)}) collective-permute-start(bf16[8,2,64,128]{3,2,1,0:T(8,128)(2,1)S(1)} %slice.45), channel_id=1, source_target_pairs={{0,32},{16,48},{32,0},{48,16},{64,96},{80,112},{96,64},{112,80},{1... | collective-permute-start | bytes 786440 | tf_op jit(solution)/shard_map/ppermute | solution.py:217
  50.6 7.5 %copy-start.2 = (f32[1,1,2,128]{3,2,1,0:T(2,128)S(1)}, f32[1,1,2,128]{3,2,1,0:T(2,128)}, u32[]{:S(2)}) copy-start(f32[1,1,2,128]{3,2,1,0:T(2,128)} %param.14) | copy-start | bytes 3076
  50.6 38.0 %all-to-all-start.1 = ((bf16[8,2,128,128]{3,2,1,0:T(8,128)(2,1)}), bf16[8,2,128,128]{3,2,1,0:T(8,128)(2,1)S(1)}, u32[]{:S(2)}, u32[]{:S(2)}) async-start(bf16[8,2,128,128]{3,2,1,0:T(8,128)(2,1)} %pad_maximum_fusion), calls=%async_computation.1 | async-start | bytes 1048576 | tf_op jit(solution)/shard_map/all_to_all | solution.py:219
  58.1 0.7 copy-start.1

commit v4 on v3

--- a/solution.py
+++ b/solution.py
@@ -117,7 +117,7 @@
     return weights_sum.astype(BF16)
 
 
-def focus_kernel(row, owners, tab, z, cosines, sines, own, other, clean, sums):
+def focus_kernel(part, row, owners, tab, z, cosines, sines, own, other, clean, sums):
     side = BLOCK_SIDE
     height = own.shape[2]
     sector = z.shape[-1]
@@ -151,7 +151,10 @@
     for b in range(blocks):
         owner = owners[0, b]
         apart = owner ^ me
-        slot = (apart & 1) * chips + ((apart >> 1) & 1) * (chips // 2) + (owner >> 2)
+        x = (apart >> 1) & 3
+        gray = x ^ (x >> 1)
+        order = gray if part else ((gray & 1) << 1) | (x >> 1)
+        slot = (apart & 1) * chips + order * (chips // 4) + (owner >> 3)
         sums[slot] = (sums[slot].astype(F32) + clean[b].astype(F32)).astype(BF16)
     own[...] = sums[:chips]
     other[...] = sums[chips:]
@@ -164,7 +167,7 @@
     operands = [pltpu.with_memory_space_constraint(x, pltpu.VMEM) for x in (tab, z, cosines, sines)]
     shape = pltpu.VMEM((slots // 2, 2, height, BLOCK_SIDE), BF16)
     return pl.pallas_call(
-        functools.partial(focus_kernel, part * height),
+        functools.partial(focus_kernel, part, part * height),
         out_shape=(shape, shape),
         in_specs=[pl.BlockSpec(memory_space=pltpu.SMEM)] + [vmem] * 4,
         out_specs=(vmem, vmem),
@@ -209,13 +212,15 @@
         partner = lambda z: (((z + shift) ^ 1) - shift) % chips
         return [(2 * z + c, 2 * partner(z) + c) for z in range(chips) for c in range(2)]
 
-    kept = chips // 2
     parts = []
     for part in range(2):
         own, other = focus(part, owners, tables[part], z, cosines, sines, groups)
         held = own + lax.ppermute(other, "sub", core_swap)
-        parts.append(held[:kept] + lax.ppermute(held[kept:], "sub", pairing(part)))
-    alike = [[2 * z + c for z in range(par, chips, 2)] for par in range(2) for c in range(2)]
+        for shift in (part, 1 - part):
+            kept = held.shape[0] // 2
+            held = held[:kept] + lax.ppermute(held[kept:], "sub", pairing(shift))
+        parts.append(held)
+    alike = [[2 * z + c for z in range(k, chips, 4)] for k in range(4) for c in range(2)]
     arrived = lax.all_to_all(
         jnp.concatenate(parts, axis=2),
         "sub",

time: 90.1 us -> 85.6 us (0.950)
  the two profiles are of different devices: /device:TPU:32 before, /device:TPU:8 now
where the time goes in v4:
time: 85.6 us; the launch traced here: 85 us
  starting transfers between devices  38.7 us (45%)
  waiting for transfers between devices  32.1 us (38%)
  Pallas kernels  6.51 us (8%)
  other arithmetic  4.11 us (5%)
  local copies, waits for them, and re-layouts  2.43 us (3%)
  matrix products  0.93 us (1%)
    ppermute x4, starting transfers between devices, on_device(): held = held[:kept] + lax.ppermute(held[kept:], 'sub', pairing(shift))  18 us
    all_to_all x1, waiting for transfers between devices, on_device(): lax.all_to_all(jnp.concatenate(parts, axis=2), 'sub', split_axis=0, conca...  16.9 us
    ppermute x4, waiting for transfers between devices, on_device(): held = held[:kept] + lax.ppermute(held[kept:], 'sub', pairing(shift))  10.7 us
    all_to_all x1, starting transfers between devices, on_device(): lax.all_to_all(by_sector, 'mem', split_axis=0, concat_axis=0, tiled=True)  9.29 us
    all_to_all x1, starting transfers between devices, on_device(): lax.all_to_all(jnp.concatenate(parts, axis=2), 'sub', split_axis=0, conca...  7.08 us
    all_to_all x1, waiting for transfers between devices, on_device(): lax.all_to_all(by_sector, 'mem', split_axis=0, concat_axis=0, tiled=True)  4.46 us
    ppermute x2, starting transfers between devices, on_device(): held = own + lax.ppermute(other, 'sub', core_swap)  4.32 us
    pallas_call x1, Pallas kernels, range_messages(): pl.pallas_call(range_kernel, out_shape=jax.ShapeDtypeStruct((members, 2,...  3.41 us
  transfers between devices with their start and end apart: 8, of which 5 were waited for; matrix products, arithmetic and copies ran while one was open for 4% of the time, Pallas kernels for 2%

profile of v4, /device:TPU:8, one launch (start us, length us, event | category | flops | bytes accessed | tf_op | source)
XLA Modules:
  0.0 85.0 jit_solution(1909929116960878483)
XLA Ops:
  0.0 3.4 %range_transform.1 = bf16[16,2,16,512]{3,2,1,0:T(8,128)(2,1)} custom-call(bf16[2,16,8192]{2,1,0:T(8,128)(2,1)} %bitcast.73, bf16[128,128]{1,0:T(8,128)(2,1)} %constant.51.first, bf16[256,256]{1,0:T(8,128)(2,1)} %constant.52.second, f32[2,64,128]{2,1,0:T(8,128)} %constant.44.clone.turn), custom_call_target="tpu_custom_call" | custom-call | tf_op jit(solution)/shard_map/range_transform/pallas_call | solution.py:84
  3.4 9.3 %all-to-all-start = ((bf16[16,2,16,512]{3,2,1,0:T(8,128)(2,1)}), bf16[16,2,16,512]{3,2,1,0:T(8,128)(2,1)S(1)}, u32[]{:S(2)}, u32[]{:S(2)}) async-start(bf16[16,2,16,512]{3,2,1,0:T(8,128)(2,1)} %range_transform.1), calls=%async_computation | async-start | bytes 1048576 | tf_op jit(solution)/shard_map/all_to_all | solution.py:195
  12.7 0.7 copy-done.3
  13.4 0.1 mul.138
  13.5 0.1 squeeze.20
  13.6 0.1 copy.11
  13.7 0.1 broadcast_bitcast_fusion
  13.8 0.6 copy-done.4
  14.4 0.6 pad_add_fusion.owners
  15.0 0.1 fusion.7
  15.1 2.0 %multiply_convert_fusion.3 = (bf16[4,1,64,256]{3,2,0,1:T(8,128)(2,1)S(1)}, bf16[4,1,64,256]{3,2,0,1:T(8,128)(2,1)S(1)}, bf16[4,1,64,256]{3,2,0,1:T(8,128)(2,1)S(1)}, bf16[4,1,64,256]{3,2,0,1:T(8,128)(2,1)S(1)}) fusion(f32[4,2,64,256]{3,2,1,0:T(8,128)S(1)} %bitcast.74), kind=kLoop, calls=%fused_computation.15 | loop fusion | flops 524288 | bytes 1048576 | tf_op jit(solution)/shard_map/convert.8
  17.1 4.5 %all-to-all-done.z = bf16[16,2,16,512]{3,2,1,0:T(8,128)(2,1)S(1)} async-done(((bf16[16,2,16,512]{3,2,1,0:T(8,128)(2,1)}), bf16[16,2,16,512]{3,2,1,0:T(8,128)(2,1)S(1)}, u32[]{:S(2)}, u32[]{:S(2)}) %all-to-all-start) | async-done | bytes 524320 | tf_op jit(solution)/shard_map/all_to_all | solution.py:195
  21.5 1.6 %focus.3 = (bf16[16,2,64,128]{3,2,1,0:T(8,128)(2,1)S(1)}, bf16[16,2,64,128]{3,2,1,0:T(8,128)(2,1)S(1)}) custom-call(s32[1,17]{1,0:T(1,128)} %pad_add_fusion.owners, bf16[256,512]{1,0:T(8,128)(2,1)S(1)} %pad_maximum_fusion.1.tab, bf16[16,2,16,512]{3,2,1,0:T(8,128)(2,1)S(1)} %all-to-all-done.z, f32[8,512]{1,0:T(8,128)S(1)} %get-tuple-element.20.cosines, ...), custom_call_target="tpu_custom_call" | custom-call | tf_op jit(solution)/shard_map/focus/pallas_call | solution.py:169
  23.1 1.9 %collective-permute-start.3 = (bf16[16,2,64,128]{3,2,1,0:T(8,128)(2,1)S(1)}, bf16[16,2,64,128]{3,2,1,0:T(8,128)(2,1)S(1)}, u32[]{:S(2)}, u32[]{:S(2)}) collective-permute-start(bf16[16,2,64,128]{3,2,1,0:T(8,128)(2,1)S(1)} %get-tuple-element.12), channel_id=1, source_target_pairs={{0,16},{16,0},{32,48},{48,32},{64,80},{80,64},{96,112},{112,96},{1... | collective-permute-start | bytes 1572872 | tf_op jit(solution)/shard_map/ppermute | solution.py:218
  25.1 1.5 %focus.2 = (bf16[16,2,64,128]{3,2,1,0:T(8,128)(2,1)S(1)}, bf16[16,2,64,128]{3,2,1,0:T(8,128)(2,1)S(1)}) custom-call(s32[1,17]{1,0:T(1,128)} %pad_add_fusion.owners, bf16[256,512]{1,0:T(8,128)(2,1)S(1)} %pad_maximum_fusion.tab, bf16[16,2,16,512]{3,2,1,0:T(8,128)(2,1)S(1)} %all-to-all-done.z, f32[8,512]{1,0:T(8,128)S(1)} %get-tuple-element.20.cosines, ...), custom_call_target="tpu_custom_call" | custom-call | tf_op jit(solution)/shard_map/focus/pallas_call | solution.py:169
  26.6 2.4 %collective-permute-start = (bf16[16,2,64,128]{3,2,1,0:T(8,128)(2,1)S(1)}, bf16[16,2,64,128]{3,2,1,0:T(8,128)(2,1)S(1)}, u32[]{:S(2)}, u32[]{:S(2)}) collective-permute-start(bf16[16,2,64,128]{3,2,1,0:T(8,128)(2,1)S(1)} %get-tuple-element.10), channel_id=1, source_target_pairs={{0,16},{16,0},{32,48},{48,32},{64,80},{80,64},{96,112},{112,96},{1... | collective-permute-start | bytes 1572872 | tf_op jit(solution)/shard_map/ppermute | solution.py:218
  29.0 0.2 add.67
  29.2 10.9 %collective-permute-start.4 = (bf16[8,2,64,128]{3,2,1,0:T(8,128)(2,1)S(1)}, bf16[8,2,64,128]{3,2,1,0:T(8,128)(2,1)S(1)}, u32[]{:S(2)}, u32[]{:S(2)}) collective-permute-start(bf16[8,2,64,128]{3,2,1,0:T(8,128)(2,1)S(1)} %slice.66), channel_id=1, source_target_pairs={{0,480},{16,496},{32,64},{48,80},{64,32},{80,48},{96,128},{112,144... | collective-permute-start | bytes 786440 | tf_op jit(solution)/shard_map/ppermute | solution.py:221
  40.2 0.2 add.64
  40.4 1.9 %collective-permute-start.1 = (bf16[8,2,64,128]{3,2,1,0:T(8,128)(2,1)S(1)}, bf16[8,2,64,128]{3,2,1,0:T(8,128)(2,1)S(1)}, u32[]{:S(2)}, u32[]{:S(2)}) collective-permute-start(bf16[8,2,64,128]{3,2,1,0:T(8,128)(2,1)S(1)} %slice.61), channel_id=1, source_target_pairs={{0,32},{16,48},{32,0},{48,16},{64,96},{80,112},{96,64},{112,80},{1... | collective-permute-start | bytes 786440 | tf_op jit(solution)/shard_map/ppermute | solution.py:221
  42.3 4.3 %collective-permute-done.4 = bf16[8,2,64,128]{3,2,1,0:T(8,128)(2,1)S(1)} collective-permute-done((bf16[8,2,64,128]{3,2,1,0:T(8,128)(2,1)S(1)}, bf16[8,2,64,128]{3,2,1,0:T(8,128)(2,1)S(1)}, u32[]{:S(2)}, u32[]{:S(2)}) %collective-permute-start.4) | collective-permute-done | bytes 262176 | tf_op jit(solution)/shard_map/ppermute | solution.py:221
  46.7 1.9 %collective-permute-start.5 = (bf16[4,2,64,128]{3,2,1,0:T(8,128)(2,1)S(1)}, bf16[4,2,64,128]{3,2,1,0:T(8,128)(2,1)S(1)}, u32[]{:S(2)}, u32[]{:S(2)}) collective-permute-start(bf16[4,2,64,128]{3,2,1,0:T(8,128)(2,1)S(1)} %slice.68), channel_id=1, source_target_pairs={{0,32},{16,48},{32,0},{48,16},{64,96},{80,112},{96,64},{112,80},{1... | collective-permute-start | bytes 393224 | tf_op jit(solution)/shard_map/ppermute | solution.py:221
  48.6 1.6 %collective-permute-done.1 = bf16[8,2,64,128]{3,2,1,0:T(8,128)(2,1)S(1)} collective-permute-done((bf16[8,2,64,128]{3,2,1,0:T(8,128)(2,1)S(1)}, bf16[8,2,64,128]{3,2,1,0:T(8,128)(2,1)S(1)}, u32[]{:S(2)}, u32[]{:S(2)}) %collective-permute-start.1) | collective-permute-done | bytes 262176 | tf_op jit(solution)/shard_map/ppermute | solution.py:221
  50.3 3.2 %collective-permute-start.2 = (bf16[4,2,64,128]{3,2,1,0:T(8,128)(2,1)S(1)}, bf16[4,2,64,128]{3,2,1,0:T(8,128)(2,1)S(1)}, u32[]{:S(2)}, u32[]{:S(2)}) collective-permute-start(bf16[4,2,64,128]{3,2,1,0:T(8,128)(2,1)S(1)} %slice.63), channel_id=1, source_target_pairs={{0,480},{16,496},{32,64},{48,80},{64,32},{80,48},{96,128},{112,144... | collective-permute-start | bytes 393224 | tf_op jit(solution)/shard_map/ppermute | solution.py:221
  53.6 0.0 collective-permute-done.5
  53.6 4.8 %collective-permute-done.2 = bf16[4,2,64,128]{3,2,1,0:T(8,128)(2,1)S(1)} collective-permute-done((bf16[4,2,64,128]{3,2,1,0:T(8,128)(2,1)S(1)}, bf16[4,2,64,128]{3,2,1,0:T(8,128)(2,1)S(1)}, u32[]{:S(2)}, u32[]{:S(2)}) %collective-permute-start.2) | collective-permute-done | bytes 131104 | tf_op jit(solution)/shard_map/ppermute | solution.py:221
  58.4 0.7 pad_maximum_fusion.2
  59.1 7.1 %all-to-all-start.1 = ((bf16[4,2,128,128]{3,2,1,0:T(8,128)(2,1)}), bf16[4,2,128,128]{3,2,1,0:T(8,128)(2,1)S(1)}, u32[]{:S(2)}, u32[]{:S(2)}) async-start(bf16[4,2,128,128]{3,2,1,0:T(8,128)(2,1)} %pad_maximum_fusion.2), calls=%async_computation.1 | async-start | bytes 524288 | tf_op jit(solution)/shard_map/all_to_all | solution.py:224
  66.2 0.7 copy-done.1
  66.9 0.2 add_convert_fusion
  67.1 16.9 %all-to-all-done.1 = bf16[4,2,128,128]{3,2,1,0:T(8,128)(2,1)S(1)} async-done(((bf16[4,2,128,128]{3,2,1,0:T(8,128)(2,1)}), bf16[4,2,128,128]{3,2,1,0:T(8,128)(2,1)S(1)}, u32[]{:S(2)}, u32[]{:S(2)}) %all-to-all-start.1) | async-done | bytes 262176 | tf_op jit(solution)/shard_map/all_to_all | solution.py:224
  84.1 0.9 %fusion.1 = bf16[1,2,128,128]{3,2,1,0:T(8,128)(2,1)} fusion(bf16[2,128,128]{2,1,0:T(8,128)(2,1)S(1)} %reduce_sum.12, bf16[2,128,128]{2,1,0:T(8,128)(2,1)S(1)} %add_convert_fusion), kind=kOutput, calls=%fused_computation.3 | convolution fusion | flops 16875520 | bytes 196608 | tf_op jit(solution)/shard_map/pyc,xc->pyx/dot_general | solution.py:237
  (24 shorter events, 0.3 us)
Async XLA Ops:
  3.4 11.7 %copy-start = (f32[1,1,512,256]{3,2,1,0:T(8,128)S(1)}, f32[1,1,512,256]{3,2,1,0:T(8,128)}, u32[]{:S(2)}) copy-start(f32[1,1,512,256]{3,2,1,0:T(8,128)} %param.10) | copy-start | bytes 1572868
  3.4 18.1 %all-to-all-start = ((bf16[16,2,16,512]{3,2,1,0:T(8,128)(2,1)}), bf16[16,2,16,512]{3,2,1,0:T(8,128)(2,1)S(1)}, u32[]{:S(2)}, u32[]{:S(2)}) async-start(bf16[16,2,16,512]{3,2,1,0:T(8,128)(2,1)} %range_transform.1), calls=%async_computation | async-start | bytes 1048576 | tf_op jit(solution)/shard_map/all_to_all | solution.py:195
  12.7 0.7 copy-start.3
  13.8 0.7 copy-start.4
  23.1 5.9 %collective-permute-start.3 = (bf16[16,2,64,128]{3,2,1,0:T(8,128)(2,1)S(1)}, bf16[16,2,64,128]{3,2,1,0:T(8,128)(2,1)S(1)}, u32[]{:S(2)}, u32[]{:S(2)}) collective-permute-start(bf16[16,2,64,128]{3,2,1,0:T(8,128)(2,1)S(1)} %get-tuple-element.12), channel_id=1, source_target_pairs={{0,16},{16,0},{32,48},{48,32},{64,80},{80,64},{96,112},{112,96},{1... | collective-permute-start | bytes 1572872 | tf_op jit(solution)/shard_map/ppermute | solution.py:218
  26.6 13.6 %collective-permute-start = (bf16[16,2,64,128]{3,2,1,0:T(8,128)(2,1)S(1)}, bf16[16,2,64,128]{3,2,1,0:T(8,128)(2,1)S(1)}, u32[]{:S(2)}, u32[]{:S(2)}) collective-permute-start(bf16[16,2,64,128]{3,2,1,0:T(8,128)(2,1)S(1)} %get-tuple-element.10), channel_id=1, source_target_pairs={{0,16},{16,0},{32,48},{48,32},{64,80},{80,64},{96,112},{112,96},{1... | collective-permute-start | bytes 1572872 | tf_op jit(solution)/shard_map/ppermute | solution.py:218
  29.2 17.4 %collective-permute-start.4 = (bf16[8,2,64,128]{3,2,1,0:T(8,128)(2,1)S(1)}, bf16[8,2,64,128]{3,2,1,0:T(8,128)(2,1)S(1)}, u32[]{:S(2)}, u32[]{:S(2)}) collective-permute-start(bf16[8,2,64,128]{3,2,1,0:T(8,128)(2,1)S(1)} %slice.66), channel_id=1, source_target_pairs={{0,480},{16,496},{32,64},{48,80},{64,32},{80,48},{96,128},{112,144... | collective-permute-start | bytes 786440 | tf_op jit(solution)/shard_map/ppermute | solution.py:221
  40.4 9.8 %collective-permute-start.1 = (bf16[8,2,64,128]{3,2,1,0:T(8,128)(2,1)S(1)}, bf16[8,2,64,128]{3,2,1,0:T(8,128)(2,1)S(1)}, u32[]{:S(2)}, u32[]{:S(2)}) collective-permute-start(bf16[8,2,64,128]{3,2,1,0:T(8,128)(2,1)S(1)} %slice.61), channel_id=1, source_target_pairs={{0,32},{16,48},{32,0},{48,16},{64,96},{80,112},{96,64},{112,80},{1... | collective-permute-start | bytes 786440 | tf_op jit(solution)/shard_map/ppermute | solution.py:221
  46.7 6.9 %collective-permute-start.5 = (bf16[4,2,64,128]{3,2,1,0:T(8,128)(2,1)S(1)}, bf16[4,2,64,128]{3,2,1,0:T(8,128)(2,1)S(1)}, u32[]{:S(2)}, u32[]{:S(2)}) collective-permute-start(bf16[4,2,64,128]{3,2,1,0:T(8,128)(2,1)S(1)} %slice.68), channel_id=1, source_target_pairs={{0,32},{16,48},{32,0},{48,16},{64,96},{80,112},{96,64},{112,80},{1... | collective-permute-start | bytes 393224 | tf_op jit(solution)/shard_map/ppermute | solution.py:221
  50.3 8.1 %collective-permute-start.2 = (bf16[4,2,64,128]{3,2,1,0:T(8,128)(2,1)S(1)}, bf16[4,2,64,128]{3,2,1,0:T(8,128)(2,1)S(1)}, u32[]{:S(2)}, u32[]{:S(2)}) collective-permute-start(bf16[4,2,64,128]{3,2,1,0:T(8,128)(2,1)S(1)} %slice.63), channel_id=1, source_target_pairs={{0,480},{16,496},{32,64},{48,80},{64,32},{80,48},{96,128},{112,144... | collective-permute-start | bytes 393224 | tf_op jit(solution)/shard_map/ppermute | solution.py:221
  59.1 7.1 %copy-start.2 = (f32[1,1,2,128]{3,2,1,0:T(2,128)S(1)}, f32[1,1,2,128]{3,2,1,0:T(2,128)}, u32[]{:S(2)}) copy-start(f32[1,1,2,128]{3,2,1,0:T(2,128)} %param.14) | copy-start | bytes 3076
  59.1 24.9 %all-to-all-start.1 = ((bf16[4,2,128,128]{3,2,1,0:T(8,128)(2,1)}), bf16[4,2,128,128]{3,2,1,0:T(8,128)(2,1)S(1)}, u32[]{:S(2)}, u32[]{:S(2)}) async-start(bf16[4,2,128,128]{3,2,1,0:T(8,128)(2,1)} %pad_maximum_fusion.2), calls=%async_computation.1 | async-start | bytes 524288 | tf_op jit(solution)/shard_map/all_to_all | solution.py:224
  66.2 0.7 copy-start.1

commit v5 on v4

--- a/solution.py
+++ b/solution.py
@@ -15,6 +15,7 @@
 SWEEPS = 256
 ANGLES = 512
 BLOCK_SIDE = 128
+PARTS = ((0, 64), (64, 128))
 F32 = jnp.float32
 BF16 = jnp.bfloat16
 
@@ -117,23 +118,22 @@
     return weights_sum.astype(BF16)
 
 
-def focus_kernel(part, row, owners, tab, z, cosines, sines, own, other, clean, sums):
+def focus_kernel(owners, tab, z, cosines, sines, own, other, clean, sums):
     side = BLOCK_SIDE
-    height = own.shape[2]
+    chips = own.shape[0]
     sector = z.shape[-1]
     cb_count = sector // side
+    ab_count = tab.shape[0] // side
     rows = z.shape[0] * z.shape[2]
     zre = z[:, 0].reshape(rows, sector)
     zim = z[:, 1].reshape(rows, sector)
     dot = functools.partial(jnp.dot, preferred_element_type=F32)
     re_all = dot(tab[...], jnp.concatenate([zre, -zim], axis=0))
     im_all = dot(tab[...], jnp.concatenate([zim, zre], axis=0))
-    ab_count = tab.shape[0] // height
     for ab in range(ab_count):
-        span = slice(ab * height, (ab + 1) * height)
-        lines = slice(ab * side, (ab + 1) * side)
-        cu = cosines[:, lines].T[row : row + height]
-        su = sines[:, lines].T[row : row + height]
+        span = slice(ab * side, (ab + 1) * side)
+        cu = cosines[:, span].T
+        su = sines[:, span].T
         for cb in range(cb_count):
             lanes = slice(cb * side, (cb + 1) * side)
             c0, s0 = cu[:, cb : cb + 1], su[:, cb : cb + 1]
@@ -147,33 +147,61 @@
     sums[...] = jnp.zeros_like(sums)
     blocks = ab_count * cb_count
     me = owners[0, blocks]
-    chips = own.shape[0]
     for b in range(blocks):
         owner = owners[0, b]
         apart = owner ^ me
         x = (apart >> 1) & 3
         gray = x ^ (x >> 1)
-        order = gray if part else ((gray & 1) << 1) | (x >> 1)
-        slot = (apart & 1) * chips + order * (chips // 4) + (owner >> 3)
-        sums[slot] = (sums[slot].astype(F32) + clean[b].astype(F32)).astype(BF16)
+        for part, order in enumerate((((gray & 1) << 1) | (x >> 1), gray)):
+            slot = (apart & 1) * chips + order * (chips // 4) + (owner >> 3)
+            lines = slice(*PARTS[part])
+            total = sums[slot, :, lines].astype(F32) + clean[b, :, lines].astype(F32)
+            sums[slot, :, lines] = total.astype(BF16)
     own[...] = sums[:chips]
     other[...] = sums[chips:]
 
 
-def focus(part, owners, tab, z, cosines, sines, slots):
-    height = BLOCK_SIDE // 2
+def focus(owners, tab, z, cosines, sines, slots):
     vmem = pl.BlockSpec(memory_space=pltpu.VMEM)
     blocks = owners.shape[1] - 1
     operands = [pltpu.with_memory_space_constraint(x, pltpu.VMEM) for x in (tab, z, cosines, sines)]
-    shape = pltpu.VMEM((slots // 2, 2, height, BLOCK_SIDE), BF16)
+    shape = pltpu.VMEM((slots // 2, 2, BLOCK_SIDE, BLOCK_SIDE), BF16)
     return pl.pallas_call(
-        functools.partial(focus_kernel, part, part * height),
+        focus_kernel,
         out_shape=(shape, shape),
         in_specs=[pl.BlockSpec(memory_space=pltpu.SMEM)] + [vmem] * 4,
         out_specs=(vmem, vmem),
-        scratch_shapes=[pltpu.VMEM((n, 2, height, BLOCK_SIDE), BF16) for n in (blocks, slots)],
+        scratch_shapes=[
+            pltpu.VMEM((n, 2, BLOCK_SIDE, BLOCK_SIDE), BF16) for n in (blocks, slots)
+        ],
+        compiler_params=pltpu.CompilerParams(vmem_limit_bytes=20 << 20),
         name="focus",
     )(owners, *operands)
+
+
+def regrid_kernel(arrived, tables, out):
+    total = arrived[0].astype(F32)
+    for i in range(1, arrived.shape[0]):
+        total = total + arrived[i].astype(F32)
+    total = total.astype(BF16)
+    for p in range(2):
+        rows_done = jnp.dot(tables[0], total[p], preferred_element_type=F32).astype(BF16)
+        ground = lax.dot_general(
+            rows_done, tables[1], (((1,), (1,)), ((), ())), preferred_element_type=F32
+        )
+        out[p] = (0.25 * ground).astype(BF16)
+
+
+def regrid(arrived, tables):
+    vmem = pl.BlockSpec(memory_space=pltpu.VMEM)
+    return pl.pallas_call(
+        regrid_kernel,
+        out_shape=jax.ShapeDtypeStruct(arrived.shape[1:], BF16),
+        in_specs=[vmem] * 2,
+        out_specs=vmem,
+        compiler_params=pltpu.CompilerParams(vmem_limit_bytes=4 << 20),
+        name="regrid",
+    )(*(pltpu.with_memory_space_constraint(x, pltpu.VMEM) for x in (arrived, tables)))
 
 
 def on_device(
@@ -194,9 +222,7 @@
     by_sector = range_messages(dechirped_echo_matrix[0], members)
     z = lax.all_to_all(by_sector, "mem", split_axis=0, concat_axis=0, tiled=True)
 
-    height = BLOCK_SIDE // 2
-    angles = bearing_rotation_table[0, 0].reshape(ab_count, 2, height, SWEEPS)
-    tables = [phase_tables(angles[:, part].reshape(ANGLES // 2, SWEEPS)) for part in range(2)]
+    tables = phase_tables(bearing_rotation_table[0, 0])
     positions = jnp.arange(BLOCK_SIDE, dtype=F32)
     slope = modulation_slope[0, 0].reshape(2, ab_count, cb_count)
     u_phase = slope[0].T[:, :, None] * positions
@@ -212,10 +238,12 @@
         partner = lambda z: (((z + shift) ^ 1) - shift) % chips
         return [(2 * z + c, 2 * partner(z) + c) for z in range(chips) for c in range(2)]
 
+    own, other = focus(owners, tables, z, cosines, sines, groups)
+    arriving = lax.ppermute(other, "sub", core_swap)
     parts = []
     for part in range(2):
-        own, other = focus(part, owners, tables[part], z, cosines, sines, groups)
-        held = own + lax.ppermute(other, "sub", core_swap)
+        lines = slice(*PARTS[part])
+        held = own[:, :, lines] + arriving[:, :, lines]
         for shift in (part, 1 - part):
             kept = held.shape[0] // 2
             held = held[:kept] + lax.ppermute(held[kept:], "sub", pairing(shift))
@@ -229,13 +257,8 @@
         tiled=True,
         axis_index_groups=alike,
     )
-    gathered = jnp.sum(arrived.astype(F32), axis=0).astype(BF16)
     own_tables = stencil(regrid_lead_cell[0, 0], regrid_weight[0, 0])
-    rows_done = jnp.einsum(
-        "ya,pac->pyc", own_tables[0], gathered, preferred_element_type=F32
-    ).astype(BF16)
-    ground = jnp.einsum("pyc,xc->pyx", rows_done, own_tables[1], preferred_element_type=F32)
-    return (0.25 * ground).astype(BF16)[None]
+    return regrid(arrived, own_tables)[None]
 
 
 def solution(mesh):

time: 85.6 us -> 84.6 us (0.988)
  starting transfers between devices: 38.7 us -> 41.9 us
  waiting for transfers between devices: 32.1 us -> 29.7 us
  matrix products: 0.93 us -> 0 us
    ppermute x4, waiting for transfers between devices: 10.7 us -> 4.92 us  [on_device(): held = held[:kept] + lax.ppermute(held[kept:], 'sub', pairing(shift))]
    ppermute x4, starting transfers between devices: 18 us -> 23 us  [on_device(): held = held[:kept] + lax.ppermute(held[kept:], 'sub', pairing(shift))]
    ppermute x2 -> x1, waiting for transfers between devices: 0.01 us -> 2.63 us  [on_device(): arriving = lax.ppermute(other, 'sub', core_swap)]
    ppermute x2 -> x1, starting transfers between devices: 4.32 us -> 1.92 us  [on_device(): arriving = lax.ppermute(other, 'sub', core_swap)]
    another operation x1 -> x0, other arithmetic: 1.96 us -> none
    mul x0 -> x1, other arithmetic: none -> 1.92 us  [phase_tables(): jnp.cos(angles) * factor]
    dot_general x1 -> x0, matrix products: 0.93 us -> none  [on_device(): jnp.einsum('pyc,xc->pyx', rows_done, own_tables[1], preferred_element_typ...]
  transfers between devices with their start and end apart: 8 -> 7, of which waited for: 5 -> 5; matrix products, arithmetic and copies ran while one was open for 4% -> 3% of each run, Pallas kernels for 2% -> 0%
where the time goes in v5:
time: 84.6 us; the launch traced here: 84.1 us
  starting transfers between devices  41.9 us (50%)
  waiting for transfers between devices  29.7 us (35%)
  Pallas kernels  6.55 us (8%)
  other arithmetic  3.3 us (4%)
  local copies, waits for them, and re-layouts  2.43 us (3%)
    ppermute x4, starting transfers between devices, on_device(): held = held[:kept] + lax.ppermute(held[kept:], 'sub', pairing(shift))  23 us
    all_to_all x1, waiting for transfers between devices, on_device(): lax.all_to_all(jnp.concatenate(parts, axis=2), 'sub', split_axis=0, conca...  17.2 us
    all_to_all x1, starting transfers between devices, on_device(): lax.all_to_all(by_sector, 'mem', split_axis=0, concat_axis=0, tiled=True)  9.29 us
    all_to_all x1, starting transfers between devices, on_device(): lax.all_to_all(jnp.concatenate(parts, axis=2), 'sub', split_axis=0, conca...  7.64 us
    all_to_all x1, waiting for transfers between devices, on_device(): lax.all_to_all(by_sector, 'mem', split_axis=0, concat_axis=0, tiled=True)  4.97 us
    ppermute x4, waiting for transfers between devices, on_device(): held = held[:kept] + lax.ppermute(held[kept:], 'sub', pairing(shift))  4.92 us
    pallas_call x1, Pallas kernels, range_messages(): pl.pallas_call(range_kernel, out_shape=jax.ShapeDtypeStruct((members, 2,...  3.41 us
    ppermute x1, waiting for transfers between devices, on_device(): arriving = lax.ppermute(other, 'sub', core_swap)  2.63 us
  transfers between devices with their start and end apart: 7, of which 5 were waited for; matrix products, arithmetic and copies ran while one was open for 3% of the time, Pallas kernels for 0%

profile of v5, /device:TPU:8, one launch (start us, length us, event | category | flops | bytes accessed | tf_op | source)
XLA Modules:
  0.0 84.1 jit_solution(7016358687839936057)
XLA Ops:
  0.0 3.4 %range_transform.1 = bf16[16,2,16,512]{3,2,1,0:T(8,128)(2,1)} custom-call(bf16[2,16,8192]{2,1,0:T(8,128)(2,1)} %bitcast.45, bf16[128,128]{1,0:T(8,128)(2,1)} %constant.47.first, bf16[256,256]{1,0:T(8,128)(2,1)} %constant.48.second, f32[2,64,128]{2,1,0:T(8,128)} %constant.40.clone.turn), custom_call_target="tpu_custom_call" | custom-call | tf_op jit(solution)/shard_map/range_transform/pallas_call | solution.py:85
  3.4 9.3 %all-to-all-start = ((bf16[16,2,16,512]{3,2,1,0:T(8,128)(2,1)}), bf16[16,2,16,512]{3,2,1,0:T(8,128)(2,1)S(1)}, u32[]{:S(2)}, u32[]{:S(2)}) async-start(bf16[16,2,16,512]{3,2,1,0:T(8,128)(2,1)} %range_transform.1), calls=%async_computation | async-start | bytes 1048576 | tf_op jit(solution)/shard_map/all_to_all | solution.py:223
  12.7 0.0 copy-start.3
  12.7 0.7 copy-done.3
  13.4 0.1 squeeze.15
  13.5 0.1 copy.10
  13.6 0.1 mul.120
  13.7 0.1 broadcast_bitcast_fusion
  13.8 0.0 copy-start.4
  13.8 0.6 copy-done.4
  14.4 0.1 pad_add_fusion.owners
  14.5 0.1 fusion.6
  14.6 1.9 %fusion = (bf16[512,256]{1,0:T(8,128)(2,1)S(1)}, bf16[512,256]{1,0:T(8,128)(2,1)S(1)}) fusion(f32[1,1,512,256]{3,2,1,0:T(8,128)S(1)} %copy-done), kind=kLoop, calls=%fused_computation.5 | loop fusion | flops 524288 | bytes 1048576 | tf_op jit(solution)/shard_map/mul | solution.py:101
  16.6 5.0 %all-to-all-done.z = bf16[16,2,16,512]{3,2,1,0:T(8,128)(2,1)S(1)} async-done(((bf16[16,2,16,512]{3,2,1,0:T(8,128)(2,1)}), bf16[16,2,16,512]{3,2,1,0:T(8,128)(2,1)S(1)}, u32[]{:S(2)}, u32[]{:S(2)}) %all-to-all-start) | async-done | bytes 524320 | tf_op jit(solution)/shard_map/all_to_all | solution.py:223
  21.5 2.2 %focus.1 = (bf16[16,2,128,128]{3,2,1,0:T(8,128)(2,1)S(1)}, bf16[16,2,128,128]{3,2,1,0:T(8,128)(2,1)S(1)}) custom-call(s32[1,17]{1,0:T(1,128)S(1)} %pad_add_fusion.owners, bf16[512,512]{1,0:T(8,128)(2,1)S(1)} %pad_maximum_fusion.tab, bf16[16,2,16,512]{3,2,1,0:T(8,128)(2,1)S(1)} %all-to-all-done.z, f32[8,512]{1,0:T(8,128)S(1)} %get-tuple-element.16.cosines, ...), custom_call_target="tpu_custom_call" | custom-call | tf_op jit(solution)/shard_map/focus/pallas_call | solution.py:169
  23.7 1.9 %collective-permute-start = (bf16[16,2,128,128]{3,2,1,0:T(8,128)(2,1)S(1)}, bf16[16,2,128,128]{3,2,1,0:T(8,128)(2,1)S(1)}, u32[]{:S(2)}, u32[]{:S(2)}) collective-permute-start(bf16[16,2,128,128]{3,2,1,0:T(8,128)(2,1)S(1)} %get-tuple-element.8), channel_id=1, source_target_pairs={{0,16},{16,0},{32,48},{48,32},{64,80},{80,64},{96,112},{112,96},{1... | collective-permute-start | bytes 3145736 | tf_op jit(solution)/shard_map/ppermute | solution.py:242
  25.7 2.6 %collective-permute-done = bf16[16,2,128,128]{3,2,1,0:T(8,128)(2,1)S(1)} collective-permute-done((bf16[16,2,128,128]{3,2,1,0:T(8,128)(2,1)S(1)}, bf16[16,2,128,128]{3,2,1,0:T(8,128)(2,1)S(1)}, u32[]{:S(2)}, u32[]{:S(2)}) %collective-permute-start) | collective-permute-done | bytes 1048608 | tf_op jit(solution)/shard_map/ppermute | solution.py:242
  28.3 0.1 slice_add_fusion.1
  28.5 3.4 %collective-permute-start.1 = (bf16[8,2,64,128]{3,2,1,0:T(8,128)(2,1)S(1)}, bf16[8,2,64,128]{3,2,1,0:T(8,128)(2,1)S(1)}, u32[]{:S(2)}, u32[]{:S(2)}) collective-permute-start(bf16[8,2,64,128]{3,2,1,0:T(8,128)(2,1)S(1)} %slice.60), channel_id=1, source_target_pairs={{0,32},{16,48},{32,0},{48,16},{64,96},{80,112},{96,64},{112,80},{1... | collective-permute-start | bytes 786440 | tf_op jit(solution)/shard_map/ppermute | solution.py:249
  31.9 10.5 %collective-permute-start.3 = (bf16[8,2,64,128]{3,2,1,0:T(8,128)(2,1)S(1)}, bf16[8,2,64,128]{3,2,1,0:T(8,128)(2,1)S(1)}, u32[]{:S(2)}, u32[]{:S(2)}) collective-permute-start(bf16[8,2,64,128]{3,2,1,0:T(8,128)(2,1)S(1)} %slice.65), channel_id=1, source_target_pairs={{0,480},{16,496},{32,64},{48,80},{64,32},{80,48},{96,128},{112,144... | collective-permute-start | bytes 786440 | tf_op jit(solution)/shard_map/ppermute | solution.py:249
  42.4 0.0 collective-permute-done.1
  42.4 7.3 %collective-permute-start.2 = (bf16[4,2,64,128]{3,2,1,0:T(8,128)(2,1)S(1)}, bf16[4,2,64,128]{3,2,1,0:T(8,128)(2,1)S(1)}, u32[]{:S(2)}, u32[]{:S(2)}) collective-permute-start(bf16[4,2,64,128]{3,2,1,0:T(8,128)(2,1)S(1)} %slice.62), channel_id=1, source_target_pairs={{0,480},{16,496},{32,64},{48,80},{64,32},{80,48},{96,128},{112,144... | collective-permute-start | bytes 393224 | tf_op jit(solution)/shard_map/ppermute | solution.py:249
  49.8 1.9 %collective-permute-start.4 = (bf16[4,2,64,128]{3,2,1,0:T(8,128)(2,1)S(1)}, bf16[4,2,64,128]{3,2,1,0:T(8,128)(2,1)S(1)}, u32[]{:S(2)}, u32[]{:S(2)}) collective-permute-start(bf16[4,2,64,128]{3,2,1,0:T(8,128)(2,1)S(1)} %slice.67), channel_id=1, source_target_pairs={{0,32},{16,48},{32,0},{48,16},{64,96},{80,112},{96,64},{112,80},{1... | collective-permute-start | bytes 393224 | tf_op jit(solution)/shard_map/ppermute | solution.py:249
  51.7 0.9 %collective-permute-done.2 = bf16[4,2,64,128]{3,2,1,0:T(8,128)(2,1)S(1)} collective-permute-done((bf16[4,2,64,128]{3,2,1,0:T(8,128)(2,1)S(1)}, bf16[4,2,64,128]{3,2,1,0:T(8,128)(2,1)S(1)}, u32[]{:S(2)}, u32[]{:S(2)}) %collective-permute-start.2) | collective-permute-done | bytes 131104 | tf_op jit(solution)/shard_map/ppermute | solution.py:249
  52.7 4.0 %collective-permute-done.4 = bf16[4,2,64,128]{3,2,1,0:T(8,128)(2,1)S(1)} collective-permute-done((bf16[4,2,64,128]{3,2,1,0:T(8,128)(2,1)S(1)}, bf16[4,2,64,128]{3,2,1,0:T(8,128)(2,1)S(1)}, u32[]{:S(2)}, u32[]{:S(2)}) %collective-permute-start.4) | collective-permute-done | bytes 131104 | tf_op jit(solution)/shard_map/ppermute | solution.py:249
  56.6 0.7 pad_maximum_fusion.1
  57.4 7.6 %all-to-all-start.1 = ((bf16[4,2,128,128]{3,2,1,0:T(8,128)(2,1)}), bf16[4,2,128,128]{3,2,1,0:T(8,128)(2,1)S(1)}, u32[]{:S(2)}, u32[]{:S(2)}) async-start(bf16[4,2,128,128]{3,2,1,0:T(8,128)(2,1)} %pad_maximum_fusion.1), calls=%async_computation.1 | async-start | bytes 524288 | tf_op jit(solution)/shard_map/all_to_all | solution.py:252
  65.0 0.0 copy-start.1
  65.0 0.7 copy-done.1
  65.7 0.2 add_convert_fusion.tables
  65.9 17.2 %all-to-all-done.1.arrived = bf16[4,2,128,128]{3,2,1,0:T(8,128)(2,1)S(1)} async-done(((bf16[4,2,128,128]{3,2,1,0:T(8,128)(2,1)}), bf16[4,2,128,128]{3,2,1,0:T(8,128)(2,1)S(1)}, u32[]{:S(2)}, u32[]{:S(2)}) %all-to-all-start.1) | async-done | bytes 262176 | tf_op jit(solution)/shard_map/all_to_all | solution.py:252
  83.1 0.9 %regrid.1 = bf16[2,128,128]{2,1,0:T(8,128)(2,1)} custom-call(bf16[4,2,128,128]{3,2,1,0:T(8,128)(2,1)S(1)} %all-to-all-done.1.arrived, bf16[2,128,128]{2,1,0:T(8,128)(2,1)S(1)} %add_convert_fusion.tables), custom_call_target="tpu_custom_call" | custom-call | tf_op jit(solution)/shard_map/regrid/pallas_call | solution.py:197
  (18 shorter events, 0.3 us)
Async XLA Ops:
  3.4 11.2 %copy-start = (f32[1,1,512,256]{3,2,1,0:T(8,128)S(1)}, f32[1,1,512,256]{3,2,1,0:T(8,128)}, u32[]{:S(2)}) copy-start(f32[1,1,512,256]{3,2,1,0:T(8,128)} %param.10) | copy-start | bytes 1572868
  3.4 18.1 %all-to-all-start = ((bf16[16,2,16,512]{3,2,1,0:T(8,128)(2,1)}), bf16[16,2,16,512]{3,2,1,0:T(8,128)(2,1)S(1)}, u32[]{:S(2)}, u32[]{:S(2)}) async-start(bf16[16,2,16,512]{3,2,1,0:T(8,128)(2,1)} %range_transform.1), calls=%async_computation | async-start | bytes 1048576 | tf_op jit(solution)/shard_map/all_to_all | solution.py:223
  12.7 0.7 copy-start.3
  13.8 0.7 copy-start.4
  23.7 4.6 %collective-permute-start = (bf16[16,2,128,128]{3,2,1,0:T(8,128)(2,1)S(1)}, bf16[16,2,128,128]{3,2,1,0:T(8,128)(2,1)S(1)}, u32[]{:S(2)}, u32[]{:S(2)}) collective-permute-start(bf16[16,2,128,128]{3,2,1,0:T(8,128)(2,1)S(1)} %get-tuple-element.8), channel_id=1, source_target_pairs={{0,16},{16,0},{32,48},{48,32},{64,80},{80,64},{96,112},{112,96},{1... | collective-permute-start | bytes 3145736 | tf_op jit(solution)/shard_map/ppermute | solution.py:242
  28.5 13.9 %collective-permute-start.1 = (bf16[8,2,64,128]{3,2,1,0:T(8,128)(2,1)S(1)}, bf16[8,2,64,128]{3,2,1,0:T(8,128)(2,1)S(1)}, u32[]{:S(2)}, u32[]{:S(2)}) collective-permute-start(bf16[8,2,64,128]{3,2,1,0:T(8,128)(2,1)S(1)} %slice.60), channel_id=1, source_target_pairs={{0,32},{16,48},{32,0},{48,16},{64,96},{80,112},{96,64},{112,80},{1... | collective-permute-start | bytes 786440 | tf_op jit(solution)/shard_map/ppermute | solution.py:249
  31.9 17.8 %collective-permute-start.3 = (bf16[8,2,64,128]{3,2,1,0:T(8,128)(2,1)S(1)}, bf16[8,2,64,128]{3,2,1,0:T(8,128)(2,1)S(1)}, u32[]{:S(2)}, u32[]{:S(2)}) collective-permute-start(bf16[8,2,64,128]{3,2,1,0:T(8,128)(2,1)S(1)} %slice.65), channel_id=1, source_target_pairs={{0,480},{16,496},{32,64},{48,80},{64,32},{80,48},{96,128},{112,144... | collective-permute-start | bytes 786440 | tf_op jit(solution)/shard_map/ppermute | solution.py:249
  42.4 10.2 %collective-permute-start.2 = (bf16[4,2,64,128]{3,2,1,0:T(8,128)(2,1)S(1)}, bf16[4,2,64,128]{3,2,1,0:T(8,128)(2,1)S(1)}, u32[]{:S(2)}, u32[]{:S(2)}) collective-permute-start(bf16[4,2,64,128]{3,2,1,0:T(8,128)(2,1)S(1)} %slice.62), channel_id=1, source_target_pairs={{0,480},{16,496},{32,64},{48,80},{64,32},{80,48},{96,128},{112,144... | collective-permute-start | bytes 393224 | tf_op jit(solution)/shard_map/ppermute | solution.py:249
  49.8 6.9 %collective-permute-start.4 = (bf16[4,2,64,128]{3,2,1,0:T(8,128)(2,1)S(1)}, bf16[4,2,64,128]{3,2,1,0:T(8,128)(2,1)S(1)}, u32[]{:S(2)}, u32[]{:S(2)}) collective-permute-start(bf16[4,2,64,128]{3,2,1,0:T(8,128)(2,1)S(1)} %slice.67), channel_id=1, source_target_pairs={{0,32},{16,48},{32,0},{48,16},{64,96},{80,112},{96,64},{112,80},{1... | collective-permute-start | bytes 393224 | tf_op jit(solution)/shard_map/ppermute | solution.py:249
  57.4 7.6 %copy-start.2 = (f32[1,1,2,128]{3,2,1,0:T(2,128)S(1)}, f32[1,1,2,128]{3,2,1,0:T(2,128)}, u32[]{:S(2)}) copy-start(f32[1,1,2,128]{3,2,1,0:T(2,128)} %param.14) | copy-start | bytes 3076
  57.4 25.8 %all-to-all-start.1 = ((bf16[4,2,128,128]{3,2,1,0:T(8,128)(2,1)}), bf16[4,2,128,128]{3,2,1,0:T(8,128)(2,1)S(1)}, u32[]{:S(2)}, u32[]{:S(2)}) async-start(bf16[4,2,128,128]{3,2,1,0:T(8,128)(2,1)} %pad_maximum_fusion.1), calls=%async_computation.1 | async-start | bytes 524288 | tf_op jit(solution)/shard_map/all_to_all | solution.py:252
  65.0 0.7 copy-start.1

commit v6 on v5

--- a/solution.py
+++ b/solution.py
@@ -179,10 +179,11 @@
     )(owners, *operands)
 
 
-def regrid_kernel(arrived, tables, out):
-    total = arrived[0].astype(F32)
-    for i in range(1, arrived.shape[0]):
-        total = total + arrived[i].astype(F32)
+def regrid_kernel(*refs):
+    *arrived, tables, out = refs
+    total = arrived[0][...].astype(F32)
+    for part in arrived[1:]:
+        total = total + part[...].astype(F32)
     total = total.astype(BF16)
     for p in range(2):
         rows_done = jnp.dot(tables[0], total[p], preferred_element_type=F32).astype(BF16)
@@ -196,12 +197,12 @@
     vmem = pl.BlockSpec(memory_space=pltpu.VMEM)
     return pl.pallas_call(
         regrid_kernel,
-        out_shape=jax.ShapeDtypeStruct(arrived.shape[1:], BF16),
-        in_specs=[vmem] * 2,
+        out_shape=jax.ShapeDtypeStruct(arrived[0].shape, BF16),
+        in_specs=[vmem] * (len(arrived) + 1),
         out_specs=vmem,
         compiler_params=pltpu.CompilerParams(vmem_limit_bytes=4 << 20),
         name="regrid",
-    )(*(pltpu.with_memory_space_constraint(x, pltpu.VMEM) for x in (arrived, tables)))
+    )(*(pltpu.with_memory_space_constraint(x, pltpu.VMEM) for x in (*arrived, tables)))
 
 
 def on_device(
@@ -248,15 +249,11 @@
             kept = held.shape[0] // 2
             held = held[:kept] + lax.ppermute(held[kept:], "sub", pairing(shift))
         parts.append(held)
-    alike = [[2 * z + c for z in range(k, chips, 4)] for k in range(4) for c in range(2)]
-    arrived = lax.all_to_all(
-        jnp.concatenate(parts, axis=2),
-        "sub",
-        split_axis=0,
-        concat_axis=0,
-        tiled=True,
-        axis_index_groups=alike,
-    )
+    held = jnp.concatenate(parts, axis=2)
+    quarter = me >> 3
+    chunk = lambda k: lax.dynamic_index_in_dim(held, (quarter + k) & 3, 0, keepdims=False)
+    along = lambda k: [(i, (i + 8 * k) % groups) for i in range(groups)]
+    arrived = [lax.ppermute(chunk(k), "sub", along(k)) for k in (2, 1, 3)] + [chunk(0)]
     own_tables = stencil(regrid_lead_cell[0, 0], regrid_weight[0, 0])
     return regrid(arrived, own_tables)[None]
 

time: 84.6 us -> 83.5 us (0.987)
  waiting for transfers between devices: 29.7 us -> 24.2 us
  starting transfers between devices: 41.9 us -> 46.9 us
    ppermute x0 -> x3, starting transfers between devices: none -> 17.5 us  [on_device(): lax.ppermute(chunk(k), 'sub', along(k))]
    all_to_all x1 -> x0, waiting for transfers between devices: 17.2 us -> none  [on_device(): lax.all_to_all(jnp.concatenate(parts, axis=2), 'sub', split_axis=0, conca...]
    all_to_all x1 -> x0, starting transfers between devices: 7.64 us -> none  [on_device(): lax.all_to_all(jnp.concatenate(parts, axis=2), 'sub', split_axis=0, conca...]
    ppermute x0 -> x3, waiting for transfers between devices: none -> 5.99 us  [on_device(): lax.ppermute(chunk(k), 'sub', along(k))]
    ppermute x4, waiting for transfers between devices: 4.92 us -> 10.6 us  [on_device(): held = held[:kept] + lax.ppermute(held[kept:], 'sub', pairing(shift))]
    ppermute x4, starting transfers between devices: 23 us -> 18.2 us  [on_device(): held = held[:kept] + lax.ppermute(held[kept:], 'sub', pairing(shift))]
  transfers between devices with their start and end apart: 7 -> 9, of which waited for: 5 -> 7; matrix products, arithmetic and copies ran while one was open for 3% -> 3% of each run, Pallas kernels for 0% -> 0%
where the time goes in v6:
time: 83.5 us; the launch traced here: 83 us
  starting transfers between devices  46.9 us (56%)
  waiting for transfers between devices  24.2 us (29%)
  Pallas kernels  6.56 us (8%)
  other arithmetic  2.6 us (3%)
  local copies, waits for them, and re-layouts  2.43 us (3%)
    ppermute x4, starting transfers between devices, on_device(): held = held[:kept] + lax.ppermute(held[kept:], 'sub', pairing(shift))  18.2 us
    ppermute x3, starting transfers between devices, on_device(): lax.ppermute(chunk(k), 'sub', along(k))  17.5 us
    ppermute x4, waiting for transfers between devices, on_device(): held = held[:kept] + lax.ppermute(held[kept:], 'sub', pairing(shift))  10.6 us
    all_to_all x1, starting transfers between devices, on_device(): lax.all_to_all(by_sector, 'mem', split_axis=0, concat_axis=0, tiled=True)  9.29 us
    ppermute x3, waiting for transfers between devices, on_device(): lax.ppermute(chunk(k), 'sub', along(k))  5.99 us
    all_to_all x1, waiting for transfers between devices, on_device(): lax.all_to_all(by_sector, 'mem', split_axis=0, concat_axis=0, tiled=True)  4.97 us
    pallas_call x1, Pallas kernels, range_messages(): pl.pallas_call(range_kernel, out_shape=jax.ShapeDtypeStruct((members, 2,...  3.42 us
    ppermute x1, waiting for transfers between devices, on_device(): arriving = lax.ppermute(other, 'sub', core_swap)  2.63 us
  transfers between devices with their start and end apart: 9, of which 7 were waited for; matrix products, arithmetic and copies ran while one was open for 3% of the time, Pallas kernels for 0%

profile of v6, /device:TPU:8, one launch (start us, length us, event | category | flops | bytes accessed | tf_op | source)
XLA Modules:
  0.0 83.0 jit_solution(186146629035469040)
XLA Ops:
  0.0 3.4 %range_transform.1 = bf16[16,2,16,512]{3,2,1,0:T(8,128)(2,1)} custom-call(bf16[2,16,8192]{2,1,0:T(8,128)(2,1)} %bitcast.53, bf16[128,128]{1,0:T(8,128)(2,1)} %constant.61.first, bf16[256,256]{1,0:T(8,128)(2,1)} %constant.62.second, f32[2,64,128]{2,1,0:T(8,128)} %constant.54.clone.turn), custom_call_target="tpu_custom_call" | custom-call | tf_op jit(solution)/shard_map/range_transform/pallas_call | solution.py:85
  3.4 9.3 %all-to-all-start = ((bf16[16,2,16,512]{3,2,1,0:T(8,128)(2,1)}), bf16[16,2,16,512]{3,2,1,0:T(8,128)(2,1)S(1)}, u32[]{:S(2)}, u32[]{:S(2)}) async-start(bf16[16,2,16,512]{3,2,1,0:T(8,128)(2,1)} %range_transform.1), calls=%async_computation | async-start | bytes 1048576 | tf_op jit(solution)/shard_map/all_to_all | solution.py:224
  12.7 0.7 copy-done.3
  13.4 0.1 squeeze.28
  13.5 0.1 copy.10
  13.6 0.1 mul.120
  13.7 0.1 broadcast_bitcast_fusion
  13.8 0.6 copy-done.4
  14.4 0.1 pad_add_fusion.owners
  14.5 0.1 fusion.14
  14.6 1.9 %fusion = (bf16[512,256]{1,0:T(8,128)(2,1)S(1)}, bf16[512,256]{1,0:T(8,128)(2,1)S(1)}) fusion(f32[1,1,512,256]{3,2,1,0:T(8,128)S(1)} %copy-done), kind=kLoop, calls=%fused_computation.13 | loop fusion | flops 524288 | bytes 1048576 | tf_op jit(solution)/shard_map/mul | solution.py:101
  16.6 5.0 %all-to-all-done.z = bf16[16,2,16,512]{3,2,1,0:T(8,128)(2,1)S(1)} async-done(((bf16[16,2,16,512]{3,2,1,0:T(8,128)(2,1)}), bf16[16,2,16,512]{3,2,1,0:T(8,128)(2,1)S(1)}, u32[]{:S(2)}, u32[]{:S(2)}) %all-to-all-start) | async-done | bytes 524320 | tf_op jit(solution)/shard_map/all_to_all | solution.py:224
  21.5 2.2 %focus.1 = (bf16[16,2,128,128]{3,2,1,0:T(8,128)(2,1)S(1)}, bf16[16,2,128,128]{3,2,1,0:T(8,128)(2,1)S(1)}) custom-call(s32[1,17]{1,0:T(1,128)S(1)} %pad_add_fusion.owners, bf16[512,512]{1,0:T(8,128)(2,1)S(1)} %pad_maximum_fusion.tab, bf16[16,2,16,512]{3,2,1,0:T(8,128)(2,1)S(1)} %all-to-all-done.z, f32[8,512]{1,0:T(8,128)S(1)} %get-tuple-element.20.cosines, ...), custom_call_target="tpu_custom_call" | custom-call | tf_op jit(solution)/shard_map/focus/pallas_call | solution.py:169
  23.8 1.9 %collective-permute-start = (bf16[16,2,128,128]{3,2,1,0:T(8,128)(2,1)S(1)}, bf16[16,2,128,128]{3,2,1,0:T(8,128)(2,1)S(1)}, u32[]{:S(2)}, u32[]{:S(2)}) collective-permute-start(bf16[16,2,128,128]{3,2,1,0:T(8,128)(2,1)S(1)} %get-tuple-element.8), channel_id=1, source_target_pairs={{0,16},{16,0},{32,48},{48,32},{64,80},{80,64},{96,112},{112,96},{1... | collective-permute-start | bytes 3145736 | tf_op jit(solution)/shard_map/ppermute | solution.py:243
  25.7 2.6 %collective-permute-done = bf16[16,2,128,128]{3,2,1,0:T(8,128)(2,1)S(1)} collective-permute-done((bf16[16,2,128,128]{3,2,1,0:T(8,128)(2,1)S(1)}, bf16[16,2,128,128]{3,2,1,0:T(8,128)(2,1)S(1)}, u32[]{:S(2)}, u32[]{:S(2)}) %collective-permute-start) | collective-permute-done | bytes 1048608 | tf_op jit(solution)/shard_map/ppermute | solution.py:243
  28.3 0.1 slice_add_fusion
  28.5 10.9 %collective-permute-start.3 = (bf16[8,2,64,128]{3,2,1,0:T(8,128)(2,1)S(1)}, bf16[8,2,64,128]{3,2,1,0:T(8,128)(2,1)S(1)}, u32[]{:S(2)}, u32[]{:S(2)}) collective-permute-start(bf16[8,2,64,128]{3,2,1,0:T(8,128)(2,1)S(1)} %slice.65), channel_id=1, source_target_pairs={{0,480},{16,496},{32,64},{48,80},{64,32},{80,48},{96,128},{112,144... | collective-permute-start | bytes 786440 | tf_op jit(solution)/shard_map/ppermute | solution.py:250
  39.5 1.9 %collective-permute-start.1 = (bf16[8,2,64,128]{3,2,1,0:T(8,128)(2,1)S(1)}, bf16[8,2,64,128]{3,2,1,0:T(8,128)(2,1)S(1)}, u32[]{:S(2)}, u32[]{:S(2)}) collective-permute-start(bf16[8,2,64,128]{3,2,1,0:T(8,128)(2,1)S(1)} %slice.60), channel_id=1, source_target_pairs={{0,32},{16,48},{32,0},{48,16},{64,96},{80,112},{96,64},{112,80},{1... | collective-permute-start | bytes 786440 | tf_op jit(solution)/shard_map/ppermute | solution.py:250
  41.4 4.6 %collective-permute-done.3 = bf16[8,2,64,128]{3,2,1,0:T(8,128)(2,1)S(1)} collective-permute-done((bf16[8,2,64,128]{3,2,1,0:T(8,128)(2,1)S(1)}, bf16[8,2,64,128]{3,2,1,0:T(8,128)(2,1)S(1)}, u32[]{:S(2)}, u32[]{:S(2)}) %collective-permute-start.3) | collective-permute-done | bytes 262176 | tf_op jit(solution)/shard_map/ppermute | solution.py:250
  46.1 1.9 %collective-permute-start.4 = (bf16[4,2,64,128]{3,2,1,0:T(8,128)(2,1)S(1)}, bf16[4,2,64,128]{3,2,1,0:T(8,128)(2,1)S(1)}, u32[]{:S(2)}, u32[]{:S(2)}) collective-permute-start(bf16[4,2,64,128]{3,2,1,0:T(8,128)(2,1)S(1)} %slice.67), channel_id=1, source_target_pairs={{0,32},{16,48},{32,0},{48,16},{64,96},{80,112},{96,64},{112,80},{1... | collective-permute-start | bytes 393224 | tf_op jit(solution)/shard_map/ppermute | solution.py:250
  48.0 1.4 %collective-permute-done.1 = bf16[8,2,64,128]{3,2,1,0:T(8,128)(2,1)S(1)} collective-permute-done((bf16[8,2,64,128]{3,2,1,0:T(8,128)(2,1)S(1)}, bf16[8,2,64,128]{3,2,1,0:T(8,128)(2,1)S(1)}, u32[]{:S(2)}, u32[]{:S(2)}) %collective-permute-start.1) | collective-permute-done | bytes 262176 | tf_op jit(solution)/shard_map/ppermute | solution.py:250
  49.5 3.4 %collective-permute-start.2 = (bf16[4,2,64,128]{3,2,1,0:T(8,128)(2,1)S(1)}, bf16[4,2,64,128]{3,2,1,0:T(8,128)(2,1)S(1)}, u32[]{:S(2)}, u32[]{:S(2)}) collective-permute-start(bf16[4,2,64,128]{3,2,1,0:T(8,128)(2,1)S(1)} %slice.62), channel_id=1, source_target_pairs={{0,480},{16,496},{32,64},{48,80},{64,32},{80,48},{96,128},{112,144... | collective-permute-start | bytes 393224 | tf_op jit(solution)/shard_map/ppermute | solution.py:250
  52.9 0.0 collective-permute-done.4
  52.9 4.6 %collective-permute-done.2 = bf16[4,2,64,128]{3,2,1,0:T(8,128)(2,1)S(1)} collective-permute-done((bf16[4,2,64,128]{3,2,1,0:T(8,128)(2,1)S(1)}, bf16[4,2,64,128]{3,2,1,0:T(8,128)(2,1)S(1)}, u32[]{:S(2)}, u32[]{:S(2)}) %collective-permute-start.2) | collective-permute-done | bytes 131104 | tf_op jit(solution)/shard_map/ppermute | solution.py:250
  57.6 7.8 %collective-permute-start.5 = (bf16[2,128,128]{2,1,0:T(8,128)(2,1)S(1)}, bf16[2,128,128]{2,1,0:T(8,128)(2,1)S(1)}, u32[]{:S(2)}, u32[]{:S(2)}) collective-permute-start(bf16[2,128,128]{2,1,0:T(8,128)(2,1)S(1)} %get-tuple-element.16), channel_id=1, source_target_pairs={{0,256},{16,272},{32,288},{48,304},{64,320},{80,336},{96,352},{112... | collective-permute-start | bytes 196616 | tf_op jit(solution)/shard_map/ppermute | solution.py:256
  65.4 5.0 %collective-permute-start.6 = (bf16[2,128,128]{2,1,0:T(8,128)(2,1)S(1)}, bf16[2,128,128]{2,1,0:T(8,128)(2,1)S(1)}, u32[]{:S(2)}, u32[]{:S(2)}) collective-permute-start(bf16[2,128,128]{2,1,0:T(8,128)(2,1)S(1)} %get-tuple-element.17), channel_id=1, source_target_pairs={{0,128},{16,144},{32,160},{48,176},{64,192},{80,208},{96,224},{112... | collective-permute-start | bytes 196616 | tf_op jit(solution)/shard_map/ppermute | solution.py:256
  70.3 4.8 %collective-permute-start.7 = (bf16[2,128,128]{2,1,0:T(8,128)(2,1)S(1)}, bf16[2,128,128]{2,1,0:T(8,128)(2,1)S(1)}, u32[]{:S(2)}, u32[]{:S(2)}) collective-permute-start(bf16[2,128,128]{2,1,0:T(8,128)(2,1)S(1)} %get-tuple-element.18), channel_id=1, source_target_pairs={{0,384},{16,400},{32,416},{48,432},{64,448},{80,464},{96,480},{112... | collective-permute-start | bytes 196616 | tf_op jit(solution)/shard_map/ppermute | solution.py:256
  75.1 0.7 copy-done.1
  75.8 0.2 add_convert_fusion.refs_4_
  76.1 0.6 collective-permute-done.6.refs_1_
  76.7 5.4 %collective-permute-done.7.refs_2_ = bf16[2,128,128]{2,1,0:T(8,128)(2,1)S(1)} collective-permute-done((bf16[2,128,128]{2,1,0:T(8,128)(2,1)S(1)}, bf16[2,128,128]{2,1,0:T(8,128)(2,1)S(1)}, u32[]{:S(2)}, u32[]{:S(2)}) %collective-permute-start.7) | collective-permute-done | bytes 65568 | tf_op jit(solution)/shard_map/ppermute | solution.py:256
  82.1 0.9 %regrid.1 = bf16[2,128,128]{2,1,0:T(8,128)(2,1)} custom-call(bf16[2,128,128]{2,1,0:T(8,128)(2,1)S(1)} %collective-permute-done.5.refs_0_, bf16[2,128,128]{2,1,0:T(8,128)(2,1)S(1)} %collective-permute-done.6.refs_1_, bf16[2,128,128]{2,1,0:T(8,128)(2,1)S(1)} %collective-permute-done.7.refs_2_, bf16[2,128,128]{2,1,0:T(8,128)(2,1)S(1)} %get-tuple-element.15.refs_3_, ...), custom_call_target="tpu_custom_call" | custom-call | tf_op jit(solution)/shard_map/regrid/pallas_call | solution.py:198
  (22 shorter events, 0.3 us)
Async XLA Ops:
  3.4 11.2 %copy-start = (f32[1,1,512,256]{3,2,1,0:T(8,128)S(1)}, f32[1,1,512,256]{3,2,1,0:T(8,128)}, u32[]{:S(2)}) copy-start(f32[1,1,512,256]{3,2,1,0:T(8,128)} %param.10) | copy-start | bytes 1572868
  3.4 18.1 %all-to-all-start = ((bf16[16,2,16,512]{3,2,1,0:T(8,128)(2,1)}), bf16[16,2,16,512]{3,2,1,0:T(8,128)(2,1)S(1)}, u32[]{:S(2)}, u32[]{:S(2)}) async-start(bf16[16,2,16,512]{3,2,1,0:T(8,128)(2,1)} %range_transform.1), calls=%async_computation | async-start | bytes 1048576 | tf_op jit(solution)/shard_map/all_to_all | solution.py:224
  12.7 0.7 copy-start.3
  13.8 0.7 copy-start.4
  23.8 4.6 %collective-permute-start = (bf16[16,2,128,128]{3,2,1,0:T(8,128)(2,1)S(1)}, bf16[16,2,128,128]{3,2,1,0:T(8,128)(2,1)S(1)}, u32[]{:S(2)}, u32[]{:S(2)}) collective-permute-start(bf16[16,2,128,128]{3,2,1,0:T(8,128)(2,1)S(1)} %get-tuple-element.8), channel_id=1, source_target_pairs={{0,16},{16,0},{32,48},{48,32},{64,80},{80,64},{96,112},{112,96},{1... | collective-permute-start | bytes 3145736 | tf_op jit(solution)/shard_map/ppermute | solution.py:243
  28.5 17.5 %collective-permute-start.3 = (bf16[8,2,64,128]{3,2,1,0:T(8,128)(2,1)S(1)}, bf16[8,2,64,128]{3,2,1,0:T(8,128)(2,1)S(1)}, u32[]{:S(2)}, u32[]{:S(2)}) collective-permute-start(bf16[8,2,64,128]{3,2,1,0:T(8,128)(2,1)S(1)} %slice.65), channel_id=1, source_target_pairs={{0,480},{16,496},{32,64},{48,80},{64,32},{80,48},{96,128},{112,144... | collective-permute-start | bytes 786440 | tf_op jit(solution)/shard_map/ppermute | solution.py:250
  39.4 2.0 %copy-start.2 = (f32[1,1,2,128]{3,2,1,0:T(2,128)S(1)}, f32[1,1,2,128]{3,2,1,0:T(2,128)}, u32[]{:S(2)}) copy-start(f32[1,1,2,128]{3,2,1,0:T(2,128)} %param.14) | copy-start | bytes 3076
  39.5 10.0 %collective-permute-start.1 = (bf16[8,2,64,128]{3,2,1,0:T(8,128)(2,1)S(1)}, bf16[8,2,64,128]{3,2,1,0:T(8,128)(2,1)S(1)}, u32[]{:S(2)}, u32[]{:S(2)}) collective-permute-start(bf16[8,2,64,128]{3,2,1,0:T(8,128)(2,1)S(1)} %slice.60), channel_id=1, source_target_pairs={{0,32},{16,48},{32,0},{48,16},{64,96},{80,112},{96,64},{112,80},{1... | collective-permute-start | bytes 786440 | tf_op jit(solution)/shard_map/ppermute | solution.py:250
  46.1 6.9 %collective-permute-start.4 = (bf16[4,2,64,128]{3,2,1,0:T(8,128)(2,1)S(1)}, bf16[4,2,64,128]{3,2,1,0:T(8,128)(2,1)S(1)}, u32[]{:S(2)}, u32[]{:S(2)}) collective-permute-start(bf16[4,2,64,128]{3,2,1,0:T(8,128)(2,1)S(1)} %slice.67), channel_id=1, source_target_pairs={{0,32},{16,48},{32,0},{48,16},{64,96},{80,112},{96,64},{112,80},{1... | collective-permute-start | bytes 393224 | tf_op jit(solution)/shard_map/ppermute | solution.py:250
  49.5 8.1 %collective-permute-start.2 = (bf16[4,2,64,128]{3,2,1,0:T(8,128)(2,1)S(1)}, bf16[4,2,64,128]{3,2,1,0:T(8,128)(2,1)S(1)}, u32[]{:S(2)}, u32[]{:S(2)}) collective-permute-start(bf16[4,2,64,128]{3,2,1,0:T(8,128)(2,1)S(1)} %slice.62), channel_id=1, source_target_pairs={{0,480},{16,496},{32,64},{48,80},{64,32},{80,48},{96,128},{112,144... | collective-permute-start | bytes 393224 | tf_op jit(solution)/shard_map/ppermute | solution.py:250
  57.6 18.5 %collective-permute-start.5 = (bf16[2,128,128]{2,1,0:T(8,128)(2,1)S(1)}, bf16[2,128,128]{2,1,0:T(8,128)(2,1)S(1)}, u32[]{:S(2)}, u32[]{:S(2)}) collective-permute-start(bf16[2,128,128]{2,1,0:T(8,128)(2,1)S(1)} %get-tuple-element.16), channel_id=1, source_target_pairs={{0,256},{16,272},{32,288},{48,304},{64,320},{80,336},{96,352},{112... | collective-permute-start | bytes 196616 | tf_op jit(solution)/shard_map/ppermute | solution.py:256
  65.4 11.3 %collective-permute-start.6 = (bf16[2,128,128]{2,1,0:T(8,128)(2,1)S(1)}, bf16[2,128,128]{2,1,0:T(8,128)(2,1)S(1)}, u32[]{:S(2)}, u32[]{:S(2)}) collective-permute-start(bf16[2,128,128]{2,1,0:T(8,128)(2,1)S(1)} %get-tuple-element.17), channel_id=1, source_target_pairs={{0,128},{16,144},{32,160},{48,176},{64,192},{80,208},{96,224},{112... | collective-permute-start | bytes 196616 | tf_op jit(solution)/shard_map/ppermute | solution.py:256
  70.3 11.7 %collective-permute-start.7 = (bf16[2,128,128]{2,1,0:T(8,128)(2,1)S(1)}, bf16[2,128,128]{2,1,0:T(8,128)(2,1)S(1)}, u32[]{:S(2)}, u32[]{:S(2)}) collective-permute-start(bf16[2,128,128]{2,1,0:T(8,128)(2,1)S(1)} %get-tuple-element.18), channel_id=1, source_target_pairs={{0,384},{16,400},{32,416},{48,432},{64,448},{80,464},{96,480},{112... | collective-permute-start | bytes 196616 | tf_op jit(solution)/shard_map/ppermute | solution.py:256
  75.1 0.7 copy-start.1

commit v7 on v6

--- a/solution.py
+++ b/solution.py
@@ -253,7 +253,7 @@
     quarter = me >> 3
     chunk = lambda k: lax.dynamic_index_in_dim(held, (quarter + k) & 3, 0, keepdims=False)
     along = lambda k: [(i, (i + 8 * k) % groups) for i in range(groups)]
-    arrived = [lax.ppermute(chunk(k), "sub", along(k)) for k in (2, 1, 3)] + [chunk(0)]
+    arrived = [lax.ppermute(chunk(k), "sub", along(k)) for k in (2, 3, 1)] + [chunk(0)]
     own_tables = stencil(regrid_lead_cell[0, 0], regrid_weight[0, 0])
     return regrid(arrived, own_tables)[None]
 

time: 83.5 us -> 81 us (0.970)
  the two profiles are of different devices: /device:TPU:8 before, /device:TPU:32 now
where the time goes in v7:
time: 81 us; the launch traced here: 80.5 us
  starting transfers between devices  49.8 us (61%)
  waiting for transfers between devices  18.8 us (23%)
  Pallas kernels  6.57 us (8%)
  other arithmetic  2.61 us (3%)
  local copies, waits for them, and re-layouts  2.43 us (3%)
    ppermute x4, starting transfers between devices, on_device(): held = held[:kept] + lax.ppermute(held[kept:], 'sub', pairing(shift))  21.8 us
    ppermute x3, starting transfers between devices, on_device(): lax.ppermute(chunk(k), 'sub', along(k))  18.9 us
    all_to_all x1, waiting for transfers between devices, on_device(): lax.all_to_all(by_sector, 'mem', split_axis=0, concat_axis=0, tiled=True)  7.63 us
    all_to_all x1, starting transfers between devices, on_device(): lax.all_to_all(by_sector, 'mem', split_axis=0, concat_axis=0, tiled=True)  7.17 us
    ppermute x4, waiting for transfers between devices, on_device(): held = held[:kept] + lax.ppermute(held[kept:], 'sub', pairing(shift))  4.92 us
    ppermute x3, waiting for transfers between devices, on_device(): lax.ppermute(chunk(k), 'sub', along(k))  3.62 us
    pallas_call x1, Pallas kernels, range_messages(): pl.pallas_call(range_kernel, out_shape=jax.ShapeDtypeStruct((members, 2,...  3.42 us
    ppermute x1, waiting for transfers between devices, on_device(): arriving = lax.ppermute(other, 'sub', core_swap)  2.63 us
  transfers between devices with their start and end apart: 9, of which 6 were waited for; matrix products, arithmetic and copies ran while one was open for 4% of the time, Pallas kernels for 0%

profile of v7, /device:TPU:32, one launch (start us, length us, event | category | flops | bytes accessed | tf_op | source)
XLA Modules:
  0.0 80.5 jit_solution(4805740758918447981)
XLA Ops:
  0.0 3.4 %range_transform.1 = bf16[16,2,16,512]{3,2,1,0:T(8,128)(2,1)} custom-call(bf16[2,16,8192]{2,1,0:T(8,128)(2,1)} %bitcast.53, bf16[128,128]{1,0:T(8,128)(2,1)} %constant.61.first, bf16[256,256]{1,0:T(8,128)(2,1)} %constant.62.second, f32[2,64,128]{2,1,0:T(8,128)} %constant.54.clone.turn), custom_call_target="tpu_custom_call" | custom-call | tf_op jit(solution)/shard_map/range_transform/pallas_call | solution.py:85
  3.4 7.2 %all-to-all-start = ((bf16[16,2,16,512]{3,2,1,0:T(8,128)(2,1)}), bf16[16,2,16,512]{3,2,1,0:T(8,128)(2,1)S(1)}, u32[]{:S(2)}, u32[]{:S(2)}) async-start(bf16[16,2,16,512]{3,2,1,0:T(8,128)(2,1)} %range_transform.1), calls=%async_computation | async-start | bytes 1048576 | tf_op jit(solution)/shard_map/all_to_all | solution.py:224
  10.6 0.0 copy-start.3
  10.6 0.7 copy-done.3
  11.3 0.1 squeeze.28
  11.4 0.1 copy.10
  11.5 0.1 mul.120
  11.6 0.1 broadcast_bitcast_fusion
  11.7 0.0 copy-start.4
  11.7 0.6 copy-done.4
  12.3 0.1 pad_add_fusion.owners
  12.4 0.1 fusion.14
  12.5 1.9 %fusion = (bf16[512,256]{1,0:T(8,128)(2,1)S(1)}, bf16[512,256]{1,0:T(8,128)(2,1)S(1)}) fusion(f32[1,1,512,256]{3,2,1,0:T(8,128)S(1)} %copy-done), kind=kLoop, calls=%fused_computation.13 | loop fusion | flops 524288 | bytes 1048576 | tf_op jit(solution)/shard_map/mul | solution.py:101
  14.5 7.6 %all-to-all-done.z = bf16[16,2,16,512]{3,2,1,0:T(8,128)(2,1)S(1)} async-done(((bf16[16,2,16,512]{3,2,1,0:T(8,128)(2,1)}), bf16[16,2,16,512]{3,2,1,0:T(8,128)(2,1)S(1)}, u32[]{:S(2)}, u32[]{:S(2)}) %all-to-all-start) | async-done | bytes 524320 | tf_op jit(solution)/shard_map/all_to_all | solution.py:224
  22.1 2.2 %focus.1 = (bf16[16,2,128,128]{3,2,1,0:T(8,128)(2,1)S(1)}, bf16[16,2,128,128]{3,2,1,0:T(8,128)(2,1)S(1)}) custom-call(s32[1,17]{1,0:T(1,128)S(1)} %pad_add_fusion.owners, bf16[512,512]{1,0:T(8,128)(2,1)S(1)} %pad_maximum_fusion.tab, bf16[16,2,16,512]{3,2,1,0:T(8,128)(2,1)S(1)} %all-to-all-done.z, f32[8,512]{1,0:T(8,128)S(1)} %get-tuple-element.20.cosines, ...), custom_call_target="tpu_custom_call" | custom-call | tf_op jit(solution)/shard_map/focus/pallas_call | solution.py:169
  24.3 1.9 %collective-permute-start = (bf16[16,2,128,128]{3,2,1,0:T(8,128)(2,1)S(1)}, bf16[16,2,128,128]{3,2,1,0:T(8,128)(2,1)S(1)}, u32[]{:S(2)}, u32[]{:S(2)}) collective-permute-start(bf16[16,2,128,128]{3,2,1,0:T(8,128)(2,1)S(1)} %get-tuple-element.8), channel_id=1, source_target_pairs={{0,16},{16,0},{32,48},{48,32},{64,80},{80,64},{96,112},{112,96},{1... | collective-permute-start | bytes 3145736 | tf_op jit(solution)/shard_map/ppermute | solution.py:243
  26.2 2.6 %collective-permute-done = bf16[16,2,128,128]{3,2,1,0:T(8,128)(2,1)S(1)} collective-permute-done((bf16[16,2,128,128]{3,2,1,0:T(8,128)(2,1)S(1)}, bf16[16,2,128,128]{3,2,1,0:T(8,128)(2,1)S(1)}, u32[]{:S(2)}, u32[]{:S(2)}) %collective-permute-start) | collective-permute-done | bytes 1048608 | tf_op jit(solution)/shard_map/ppermute | solution.py:243
  28.9 0.1 slice_add_fusion
  29.0 3.8 %collective-permute-start.3 = (bf16[8,2,64,128]{3,2,1,0:T(8,128)(2,1)S(1)}, bf16[8,2,64,128]{3,2,1,0:T(8,128)(2,1)S(1)}, u32[]{:S(2)}, u32[]{:S(2)}) collective-permute-start(bf16[8,2,64,128]{3,2,1,0:T(8,128)(2,1)S(1)} %slice.65), channel_id=1, source_target_pairs={{0,480},{16,496},{32,64},{48,80},{64,32},{80,48},{96,128},{112,144... | collective-permute-start | bytes 786440 | tf_op jit(solution)/shard_map/ppermute | solution.py:250
  32.9 9.6 %collective-permute-start.1 = (bf16[8,2,64,128]{3,2,1,0:T(8,128)(2,1)S(1)}, bf16[8,2,64,128]{3,2,1,0:T(8,128)(2,1)S(1)}, u32[]{:S(2)}, u32[]{:S(2)}) collective-permute-start(bf16[8,2,64,128]{3,2,1,0:T(8,128)(2,1)S(1)} %slice.60), channel_id=1, source_target_pairs={{0,32},{16,48},{32,0},{48,16},{64,96},{80,112},{96,64},{112,80},{1... | collective-permute-start | bytes 786440 | tf_op jit(solution)/shard_map/ppermute | solution.py:250
  42.6 6.5 %collective-permute-start.4 = (bf16[4,2,64,128]{3,2,1,0:T(8,128)(2,1)S(1)}, bf16[4,2,64,128]{3,2,1,0:T(8,128)(2,1)S(1)}, u32[]{:S(2)}, u32[]{:S(2)}) collective-permute-start(bf16[4,2,64,128]{3,2,1,0:T(8,128)(2,1)S(1)} %slice.67), channel_id=1, source_target_pairs={{0,32},{16,48},{32,0},{48,16},{64,96},{80,112},{96,64},{112,80},{1... | collective-permute-start | bytes 393224 | tf_op jit(solution)/shard_map/ppermute | solution.py:250
  49.2 1.9 %collective-permute-start.2 = (bf16[4,2,64,128]{3,2,1,0:T(8,128)(2,1)S(1)}, bf16[4,2,64,128]{3,2,1,0:T(8,128)(2,1)S(1)}, u32[]{:S(2)}, u32[]{:S(2)}) collective-permute-start(bf16[4,2,64,128]{3,2,1,0:T(8,128)(2,1)S(1)} %slice.62), channel_id=1, source_target_pairs={{0,480},{16,496},{32,64},{48,80},{64,32},{80,48},{96,128},{112,144... | collective-permute-start | bytes 393224 | tf_op jit(solution)/shard_map/ppermute | solution.py:250
  51.1 1.2 %collective-permute-done.4 = bf16[4,2,64,128]{3,2,1,0:T(8,128)(2,1)S(1)} collective-permute-done((bf16[4,2,64,128]{3,2,1,0:T(8,128)(2,1)S(1)}, bf16[4,2,64,128]{3,2,1,0:T(8,128)(2,1)S(1)}, u32[]{:S(2)}, u32[]{:S(2)}) %collective-permute-start.4) | collective-permute-done | bytes 131104 | tf_op jit(solution)/shard_map/ppermute | solution.py:250
  52.3 3.7 %collective-permute-done.2 = bf16[4,2,64,128]{3,2,1,0:T(8,128)(2,1)S(1)} collective-permute-done((bf16[4,2,64,128]{3,2,1,0:T(8,128)(2,1)S(1)}, bf16[4,2,64,128]{3,2,1,0:T(8,128)(2,1)S(1)}, u32[]{:S(2)}, u32[]{:S(2)}) %collective-permute-start.2) | collective-permute-done | bytes 131104 | tf_op jit(solution)/shard_map/ppermute | solution.py:250
  56.1 9.2 %collective-permute-start.5 = (bf16[2,128,128]{2,1,0:T(8,128)(2,1)S(1)}, bf16[2,128,128]{2,1,0:T(8,128)(2,1)S(1)}, u32[]{:S(2)}, u32[]{:S(2)}) collective-permute-start(bf16[2,128,128]{2,1,0:T(8,128)(2,1)S(1)} %get-tuple-element.16), channel_id=1, source_target_pairs={{0,256},{16,272},{32,288},{48,304},{64,320},{80,336},{96,352},{112... | collective-permute-start | bytes 196616 | tf_op jit(solution)/shard_map/ppermute | solution.py:256
  65.3 2.5 %collective-permute-start.6 = (bf16[2,128,128]{2,1,0:T(8,128)(2,1)S(1)}, bf16[2,128,128]{2,1,0:T(8,128)(2,1)S(1)}, u32[]{:S(2)}, u32[]{:S(2)}) collective-permute-start(bf16[2,128,128]{2,1,0:T(8,128)(2,1)S(1)} %get-tuple-element.17), channel_id=1, source_target_pairs={{0,384},{16,400},{32,416},{48,432},{64,448},{80,464},{96,480},{112... | collective-permute-start | bytes 196616 | tf_op jit(solution)/shard_map/ppermute | solution.py:256
  67.8 7.2 %collective-permute-start.7 = (bf16[2,128,128]{2,1,0:T(8,128)(2,1)S(1)}, bf16[2,128,128]{2,1,0:T(8,128)(2,1)S(1)}, u32[]{:S(2)}, u32[]{:S(2)}) collective-permute-start(bf16[2,128,128]{2,1,0:T(8,128)(2,1)S(1)} %get-tuple-element.18), channel_id=1, source_target_pairs={{0,128},{16,144},{32,160},{48,176},{64,192},{80,208},{96,224},{112... | collective-permute-start | bytes 196616 | tf_op jit(solution)/shard_map/ppermute | solution.py:256
  75.0 0.7 copy-done.1
  75.7 0.2 add_convert_fusion.refs_4_
  76.0 1.0 %collective-permute-done.6.refs_1_ = bf16[2,128,128]{2,1,0:T(8,128)(2,1)S(1)} collective-permute-done((bf16[2,128,128]{2,1,0:T(8,128)(2,1)S(1)}, bf16[2,128,128]{2,1,0:T(8,128)(2,1)S(1)}, u32[]{:S(2)}, u32[]{:S(2)}) %collective-permute-start.6) | collective-permute-done | bytes 65568 | tf_op jit(solution)/shard_map/ppermute | solution.py:256
  76.9 2.7 %collective-permute-done.7.refs_2_ = bf16[2,128,128]{2,1,0:T(8,128)(2,1)S(1)} collective-permute-done((bf16[2,128,128]{2,1,0:T(8,128)(2,1)S(1)}, bf16[2,128,128]{2,1,0:T(8,128)(2,1)S(1)}, u32[]{:S(2)}, u32[]{:S(2)}) %collective-permute-start.7) | collective-permute-done | bytes 65568 | tf_op jit(solution)/shard_map/ppermute | solution.py:256
  79.6 0.9 %regrid.1 = bf16[2,128,128]{2,1,0:T(8,128)(2,1)} custom-call(bf16[2,128,128]{2,1,0:T(8,128)(2,1)S(1)} %collective-permute-done.5.refs_0_, bf16[2,128,128]{2,1,0:T(8,128)(2,1)S(1)} %collective-permute-done.6.refs_1_, bf16[2,128,128]{2,1,0:T(8,128)(2,1)S(1)} %collective-permute-done.7.refs_2_, bf16[2,128,128]{2,1,0:T(8,128)(2,1)S(1)} %get-tuple-element.15.refs_3_, ...), custom_call_target="tpu_custom_call" | custom-call | tf_op jit(solution)/shard_map/regrid/pallas_call | solution.py:198
  (22 shorter events, 0.3 us)
Async XLA Ops:
  3.4 9.1 %copy-start = (f32[1,1,512,256]{3,2,1,0:T(8,128)S(1)}, f32[1,1,512,256]{3,2,1,0:T(8,128)}, u32[]{:S(2)}) copy-start(f32[1,1,512,256]{3,2,1,0:T(8,128)} %param.10) | copy-start | bytes 1572868
  3.4 18.7 %all-to-all-start = ((bf16[16,2,16,512]{3,2,1,0:T(8,128)(2,1)}), bf16[16,2,16,512]{3,2,1,0:T(8,128)(2,1)S(1)}, u32[]{:S(2)}, u32[]{:S(2)}) async-start(bf16[16,2,16,512]{3,2,1,0:T(8,128)(2,1)} %range_transform.1), calls=%async_computation | async-start | bytes 1048576 | tf_op jit(solution)/shard_map/all_to_all | solution.py:224
  10.6 0.7 copy-start.3
  11.7 0.7 copy-start.4
  24.3 4.6 %collective-permute-start = (bf16[16,2,128,128]{3,2,1,0:T(8,128)(2,1)S(1)}, bf16[16,2,128,128]{3,2,1,0:T(8,128)(2,1)S(1)}, u32[]{:S(2)}, u32[]{:S(2)}) collective-permute-start(bf16[16,2,128,128]{3,2,1,0:T(8,128)(2,1)S(1)} %get-tuple-element.8), channel_id=1, source_target_pairs={{0,16},{16,0},{32,48},{48,32},{64,80},{80,64},{96,112},{112,96},{1... | collective-permute-start | bytes 3145736 | tf_op jit(solution)/shard_map/ppermute | solution.py:243
  29.0 13.5 %collective-permute-start.3 = (bf16[8,2,64,128]{3,2,1,0:T(8,128)(2,1)S(1)}, bf16[8,2,64,128]{3,2,1,0:T(8,128)(2,1)S(1)}, u32[]{:S(2)}, u32[]{:S(2)}) collective-permute-start(bf16[8,2,64,128]{3,2,1,0:T(8,128)(2,1)S(1)} %slice.65), channel_id=1, source_target_pairs={{0,480},{16,496},{32,64},{48,80},{64,32},{80,48},{96,128},{112,144... | collective-permute-start | bytes 786440 | tf_op jit(solution)/shard_map/ppermute | solution.py:250
  32.9 9.6 %copy-start.2 = (f32[1,1,2,128]{3,2,1,0:T(2,128)S(1)}, f32[1,1,2,128]{3,2,1,0:T(2,128)}, u32[]{:S(2)}) copy-start(f32[1,1,2,128]{3,2,1,0:T(2,128)} %param.14) | copy-start | bytes 3076
  32.9 16.2 %collective-permute-start.1 = (bf16[8,2,64,128]{3,2,1,0:T(8,128)(2,1)S(1)}, bf16[8,2,64,128]{3,2,1,0:T(8,128)(2,1)S(1)}, u32[]{:S(2)}, u32[]{:S(2)}) collective-permute-start(bf16[8,2,64,128]{3,2,1,0:T(8,128)(2,1)S(1)} %slice.60), channel_id=1, source_target_pairs={{0,32},{16,48},{32,0},{48,16},{64,96},{80,112},{96,64},{112,80},{1... | collective-permute-start | bytes 786440 | tf_op jit(solution)/shard_map/ppermute | solution.py:250
  42.6 9.7 %collective-permute-start.4 = (bf16[4,2,64,128]{3,2,1,0:T(8,128)(2,1)S(1)}, bf16[4,2,64,128]{3,2,1,0:T(8,128)(2,1)S(1)}, u32[]{:S(2)}, u32[]{:S(2)}) collective-permute-start(bf16[4,2,64,128]{3,2,1,0:T(8,128)(2,1)S(1)} %slice.67), channel_id=1, source_target_pairs={{0,32},{16,48},{32,0},{48,16},{64,96},{80,112},{96,64},{112,80},{1... | collective-permute-start | bytes 393224 | tf_op jit(solution)/shard_map/ppermute | solution.py:250
  49.2 6.9 %collective-permute-start.2 = (bf16[4,2,64,128]{3,2,1,0:T(8,128)(2,1)S(1)}, bf16[4,2,64,128]{3,2,1,0:T(8,128)(2,1)S(1)}, u32[]{:S(2)}, u32[]{:S(2)}) collective-permute-start(bf16[4,2,64,128]{3,2,1,0:T(8,128)(2,1)S(1)} %slice.62), channel_id=1, source_target_pairs={{0,480},{16,496},{32,64},{48,80},{64,32},{80,48},{96,128},{112,144... | collective-permute-start | bytes 393224 | tf_op jit(solution)/shard_map/ppermute | solution.py:250
  56.1 19.9 %collective-permute-start.5 = (bf16[2,128,128]{2,1,0:T(8,128)(2,1)S(1)}, bf16[2,128,128]{2,1,0:T(8,128)(2,1)S(1)}, u32[]{:S(2)}, u32[]{:S(2)}) collective-permute-start(bf16[2,128,128]{2,1,0:T(8,128)(2,1)S(1)} %get-tuple-element.16), channel_id=1, source_target_pairs={{0,256},{16,272},{32,288},{48,304},{64,320},{80,336},{96,352},{112... | collective-permute-start | bytes 196616 | tf_op jit(solution)/shard_map/ppermute | solution.py:256
  65.3 11.7 %collective-permute-start.6 = (bf16[2,128,128]{2,1,0:T(8,128)(2,1)S(1)}, bf16[2,128,128]{2,1,0:T(8,128)(2,1)S(1)}, u32[]{:S(2)}, u32[]{:S(2)}) collective-permute-start(bf16[2,128,128]{2,1,0:T(8,128)(2,1)S(1)} %get-tuple-element.17), channel_id=1, source_target_pairs={{0,384},{16,400},{32,416},{48,432},{64,448},{80,464},{96,480},{112... | collective-permute-start | bytes 196616 | tf_op jit(solution)/shard_map/ppermute | solution.py:256
  67.8 11.8 %collective-permute-start.7 = (bf16[2,128,128]{2,1,0:T(8,128)(2,1)S(1)}, bf16[2,128,128]{2,1,0:T(8,128)(2,1)S(1)}, u32[]{:S(2)}, u32[]{:S(2)}) collective-permute-start(bf16[2,128,128]{2,1,0:T(8,128)(2,1)S(1)} %get-tuple-element.18), channel_id=1, source_target_pairs={{0,128},{16,144},{32,160},{48,176},{64,192},{80,208},{96,224},{112... | collective-permute-start | bytes 196616 | tf_op jit(solution)/shard_map/ppermute | solution.py:256
  75.0 0.7 copy-start.1

commit v8 on v7

--- a/solution.py
+++ b/solution.py
@@ -253,7 +253,7 @@
     quarter = me >> 3
     chunk = lambda k: lax.dynamic_index_in_dim(held, (quarter + k) & 3, 0, keepdims=False)
     along = lambda k: [(i, (i + 8 * k) % groups) for i in range(groups)]
-    arrived = [lax.ppermute(chunk(k), "sub", along(k)) for k in (2, 3, 1)] + [chunk(0)]
+    arrived = [lax.ppermute(chunk(k), "sub", along(k)) for k in (3, 2, 1)] + [chunk(0)]
     own_tables = stencil(regrid_lead_cell[0, 0], regrid_weight[0, 0])
     return regrid(arrived, own_tables)[None]
 

time: 81 us -> 84.1 us (1.038)
  waiting for transfers between devices: 18.8 us -> 21.9 us
    ppermute x3, waiting for transfers between devices: 3.62 us -> 6.69 us  [on_device(): lax.ppermute(chunk(k), 'sub', along(k))]
  transfers between devices with their start and end apart: 9 -> 9, of which waited for: 6 -> 6; matrix products, arithmetic and copies ran while one was open for 4% -> 3% of each run, Pallas kernels for 0% -> 0%
where the time goes in v8:
time: 84.1 us; the launch traced here: 83.6 us
  starting transfers between devices  49.8 us (59%)
  waiting for transfers between devices  21.9 us (26%)
  Pallas kernels  6.57 us (8%)
  other arithmetic  2.61 us (3%)
  local copies, waits for them, and re-layouts  2.43 us (3%)
    ppermute x4, starting transfers between devices, on_device(): held = held[:kept] + lax.ppermute(held[kept:], 'sub', pairing(shift))  21.8 us
    ppermute x3, starting transfers between devices, on_device(): lax.ppermute(chunk(k), 'sub', along(k))  18.9 us
    all_to_all x1, waiting for transfers between devices, on_device(): lax.all_to_all(by_sector, 'mem', split_axis=0, concat_axis=0, tiled=True)  7.63 us
    all_to_all x1, starting transfers between devices, on_device(): lax.all_to_all(by_sector, 'mem', split_axis=0, concat_axis=0, tiled=True)  7.17 us
    ppermute x3, waiting for transfers between devices, on_device(): lax.ppermute(chunk(k), 'sub', along(k))  6.69 us
    ppermute x4, waiting for transfers between devices, on_device(): held = held[:kept] + lax.ppermute(held[kept:], 'sub', pairing(shift))  4.92 us
    pallas_call x1, Pallas kernels, range_messages(): pl.pallas_call(range_kernel, out_shape=jax.ShapeDtypeStruct((members, 2,...  3.42 us
    ppermute x1, waiting for transfers between devices, on_device(): arriving = lax.ppermute(other, 'sub', core_swap)  2.63 us
  transfers between devices with their start and end apart: 9, of which 6 were waited for; matrix products, arithmetic and copies ran while one was open for 3% of the time, Pallas kernels for 0%

profile of v8, /device:TPU:32, one launch (start us, length us, event | category | flops | bytes accessed | tf_op | source)
XLA Modules:
  0.0 83.6 jit_solution(17354032885907906294)
XLA Ops:
  0.0 3.4 %range_transform.1 = bf16[16,2,16,512]{3,2,1,0:T(8,128)(2,1)} custom-call(bf16[2,16,8192]{2,1,0:T(8,128)(2,1)} %bitcast.53, bf16[128,128]{1,0:T(8,128)(2,1)} %constant.61.first, bf16[256,256]{1,0:T(8,128)(2,1)} %constant.62.second, f32[2,64,128]{2,1,0:T(8,128)} %constant.54.clone.turn), custom_call_target="tpu_custom_call" | custom-call | tf_op jit(solution)/shard_map/range_transform/pallas_call | solution.py:85
  3.4 7.2 %all-to-all-start = ((bf16[16,2,16,512]{3,2,1,0:T(8,128)(2,1)}), bf16[16,2,16,512]{3,2,1,0:T(8,128)(2,1)S(1)}, u32[]{:S(2)}, u32[]{:S(2)}) async-start(bf16[16,2,16,512]{3,2,1,0:T(8,128)(2,1)} %range_transform.1), calls=%async_computation | async-start | bytes 1048576 | tf_op jit(solution)/shard_map/all_to_all | solution.py:224
  10.6 0.7 copy-done.3
  11.3 0.1 squeeze.28
  11.4 0.1 copy.10
  11.5 0.1 mul.120
  11.6 0.1 broadcast_bitcast_fusion
  11.7 0.0 copy-start.4
  11.7 0.6 copy-done.4
  12.3 0.1 pad_add_fusion.owners
  12.4 0.1 fusion.14
  12.5 1.9 %fusion = (bf16[512,256]{1,0:T(8,128)(2,1)S(1)}, bf16[512,256]{1,0:T(8,128)(2,1)S(1)}) fusion(f32[1,1,512,256]{3,2,1,0:T(8,128)S(1)} %copy-done), kind=kLoop, calls=%fused_computation.13 | loop fusion | flops 524288 | bytes 1048576 | tf_op jit(solution)/shard_map/mul | solution.py:101
  14.5 7.6 %all-to-all-done.z = bf16[16,2,16,512]{3,2,1,0:T(8,128)(2,1)S(1)} async-done(((bf16[16,2,16,512]{3,2,1,0:T(8,128)(2,1)}), bf16[16,2,16,512]{3,2,1,0:T(8,128)(2,1)S(1)}, u32[]{:S(2)}, u32[]{:S(2)}) %all-to-all-start) | async-done | bytes 524320 | tf_op jit(solution)/shard_map/all_to_all | solution.py:224
  22.1 2.2 %focus.1 = (bf16[16,2,128,128]{3,2,1,0:T(8,128)(2,1)S(1)}, bf16[16,2,128,128]{3,2,1,0:T(8,128)(2,1)S(1)}) custom-call(s32[1,17]{1,0:T(1,128)S(1)} %pad_add_fusion.owners, bf16[512,512]{1,0:T(8,128)(2,1)S(1)} %pad_maximum_fusion.tab, bf16[16,2,16,512]{3,2,1,0:T(8,128)(2,1)S(1)} %all-to-all-done.z, f32[8,512]{1,0:T(8,128)S(1)} %get-tuple-element.20.cosines, ...), custom_call_target="tpu_custom_call" | custom-call | tf_op jit(solution)/shard_map/focus/pallas_call | solution.py:169
  24.3 1.9 %collective-permute-start = (bf16[16,2,128,128]{3,2,1,0:T(8,128)(2,1)S(1)}, bf16[16,2,128,128]{3,2,1,0:T(8,128)(2,1)S(1)}, u32[]{:S(2)}, u32[]{:S(2)}) collective-permute-start(bf16[16,2,128,128]{3,2,1,0:T(8,128)(2,1)S(1)} %get-tuple-element.8), channel_id=1, source_target_pairs={{0,16},{16,0},{32,48},{48,32},{64,80},{80,64},{96,112},{112,96},{1... | collective-permute-start | bytes 3145736 | tf_op jit(solution)/shard_map/ppermute | solution.py:243
  26.2 2.6 %collective-permute-done = bf16[16,2,128,128]{3,2,1,0:T(8,128)(2,1)S(1)} collective-permute-done((bf16[16,2,128,128]{3,2,1,0:T(8,128)(2,1)S(1)}, bf16[16,2,128,128]{3,2,1,0:T(8,128)(2,1)S(1)}, u32[]{:S(2)}, u32[]{:S(2)}) %collective-permute-start) | collective-permute-done | bytes 1048608 | tf_op jit(solution)/shard_map/ppermute | solution.py:243
  28.9 0.1 slice_add_fusion
  29.0 3.8 %collective-permute-start.3 = (bf16[8,2,64,128]{3,2,1,0:T(8,128)(2,1)S(1)}, bf16[8,2,64,128]{3,2,1,0:T(8,128)(2,1)S(1)}, u32[]{:S(2)}, u32[]{:S(2)}) collective-permute-start(bf16[8,2,64,128]{3,2,1,0:T(8,128)(2,1)S(1)} %slice.65), channel_id=1, source_target_pairs={{0,480},{16,496},{32,64},{48,80},{64,32},{80,48},{96,128},{112,144... | collective-permute-start | bytes 786440 | tf_op jit(solution)/shard_map/ppermute | solution.py:250
  32.9 0.0 copy-start.2
  32.9 9.6 %collective-permute-start.1 = (bf16[8,2,64,128]{3,2,1,0:T(8,128)(2,1)S(1)}, bf16[8,2,64,128]{3,2,1,0:T(8,128)(2,1)S(1)}, u32[]{:S(2)}, u32[]{:S(2)}) collective-permute-start(bf16[8,2,64,128]{3,2,1,0:T(8,128)(2,1)S(1)} %slice.60), channel_id=1, source_target_pairs={{0,32},{16,48},{32,0},{48,16},{64,96},{80,112},{96,64},{112,80},{1... | collective-permute-start | bytes 786440 | tf_op jit(solution)/shard_map/ppermute | solution.py:250
  42.6 6.5 %collective-permute-start.4 = (bf16[4,2,64,128]{3,2,1,0:T(8,128)(2,1)S(1)}, bf16[4,2,64,128]{3,2,1,0:T(8,128)(2,1)S(1)}, u32[]{:S(2)}, u32[]{:S(2)}) collective-permute-start(bf16[4,2,64,128]{3,2,1,0:T(8,128)(2,1)S(1)} %slice.67), channel_id=1, source_target_pairs={{0,32},{16,48},{32,0},{48,16},{64,96},{80,112},{96,64},{112,80},{1... | collective-permute-start | bytes 393224 | tf_op jit(solution)/shard_map/ppermute | solution.py:250
  49.2 1.9 %collective-permute-start.2 = (bf16[4,2,64,128]{3,2,1,0:T(8,128)(2,1)S(1)}, bf16[4,2,64,128]{3,2,1,0:T(8,128)(2,1)S(1)}, u32[]{:S(2)}, u32[]{:S(2)}) collective-permute-start(bf16[4,2,64,128]{3,2,1,0:T(8,128)(2,1)S(1)} %slice.62), channel_id=1, source_target_pairs={{0,480},{16,496},{32,64},{48,80},{64,32},{80,48},{96,128},{112,144... | collective-permute-start | bytes 393224 | tf_op jit(solution)/shard_map/ppermute | solution.py:250
  51.1 1.2 %collective-permute-done.4 = bf16[4,2,64,128]{3,2,1,0:T(8,128)(2,1)S(1)} collective-permute-done((bf16[4,2,64,128]{3,2,1,0:T(8,128)(2,1)S(1)}, bf16[4,2,64,128]{3,2,1,0:T(8,128)(2,1)S(1)}, u32[]{:S(2)}, u32[]{:S(2)}) %collective-permute-start.4) | collective-permute-done | bytes 131104 | tf_op jit(solution)/shard_map/ppermute | solution.py:250
  52.3 3.7 %collective-permute-done.2 = bf16[4,2,64,128]{3,2,1,0:T(8,128)(2,1)S(1)} collective-permute-done((bf16[4,2,64,128]{3,2,1,0:T(8,128)(2,1)S(1)}, bf16[4,2,64,128]{3,2,1,0:T(8,128)(2,1)S(1)}, u32[]{:S(2)}, u32[]{:S(2)}) %collective-permute-start.2) | collective-permute-done | bytes 131104 | tf_op jit(solution)/shard_map/ppermute | solution.py:250
  56.1 6.2 %collective-permute-start.5 = (bf16[2,128,128]{2,1,0:T(8,128)(2,1)S(1)}, bf16[2,128,128]{2,1,0:T(8,128)(2,1)S(1)}, u32[]{:S(2)}, u32[]{:S(2)}) collective-permute-start(bf16[2,128,128]{2,1,0:T(8,128)(2,1)S(1)} %get-tuple-element.16), channel_id=1, source_target_pairs={{0,384},{16,400},{32,416},{48,432},{64,448},{80,464},{96,480},{112... | collective-permute-start | bytes 196616 | tf_op jit(solution)/shard_map/ppermute | solution.py:256
  62.3 5.5 %collective-permute-start.6 = (bf16[2,128,128]{2,1,0:T(8,128)(2,1)S(1)}, bf16[2,128,128]{2,1,0:T(8,128)(2,1)S(1)}, u32[]{:S(2)}, u32[]{:S(2)}) collective-permute-start(bf16[2,128,128]{2,1,0:T(8,128)(2,1)S(1)} %get-tuple-element.17), channel_id=1, source_target_pairs={{0,256},{16,272},{32,288},{48,304},{64,320},{80,336},{96,352},{112... | collective-permute-start | bytes 196616 | tf_op jit(solution)/shard_map/ppermute | solution.py:256
  67.8 7.2 %collective-permute-start.7 = (bf16[2,128,128]{2,1,0:T(8,128)(2,1)S(1)}, bf16[2,128,128]{2,1,0:T(8,128)(2,1)S(1)}, u32[]{:S(2)}, u32[]{:S(2)}) collective-permute-start(bf16[2,128,128]{2,1,0:T(8,128)(2,1)S(1)} %get-tuple-element.18), channel_id=1, source_target_pairs={{0,128},{16,144},{32,160},{48,176},{64,192},{80,208},{96,224},{112... | collective-permute-start | bytes 196616 | tf_op jit(solution)/shard_map/ppermute | solution.py:256
  75.0 0.7 copy-done.1
  75.7 0.2 add_convert_fusion.refs_4_
  76.0 2.1 %collective-permute-done.6.refs_1_ = bf16[2,128,128]{2,1,0:T(8,128)(2,1)S(1)} collective-permute-done((bf16[2,128,128]{2,1,0:T(8,128)(2,1)S(1)}, bf16[2,128,128]{2,1,0:T(8,128)(2,1)S(1)}, u32[]{:S(2)}, u32[]{:S(2)}) %collective-permute-start.6) | collective-permute-done | bytes 65568 | tf_op jit(solution)/shard_map/ppermute | solution.py:256
  78.1 4.5 %collective-permute-done.7.refs_2_ = bf16[2,128,128]{2,1,0:T(8,128)(2,1)S(1)} collective-permute-done((bf16[2,128,128]{2,1,0:T(8,128)(2,1)S(1)}, bf16[2,128,128]{2,1,0:T(8,128)(2,1)S(1)}, u32[]{:S(2)}, u32[]{:S(2)}) %collective-permute-start.7) | collective-permute-done | bytes 65568 | tf_op jit(solution)/shard_map/ppermute | solution.py:256
  82.7 0.9 %regrid.1 = bf16[2,128,128]{2,1,0:T(8,128)(2,1)} custom-call(bf16[2,128,128]{2,1,0:T(8,128)(2,1)S(1)} %collective-permute-done.5.refs_0_, bf16[2,128,128]{2,1,0:T(8,128)(2,1)S(1)} %collective-permute-done.6.refs_1_, bf16[2,128,128]{2,1,0:T(8,128)(2,1)S(1)} %collective-permute-done.7.refs_2_, bf16[2,128,128]{2,1,0:T(8,128)(2,1)S(1)} %get-tuple-element.15.refs_3_, ...), custom_call_target="tpu_custom_call" | custom-call | tf_op jit(solution)/shard_map/regrid/pallas_call | solution.py:198
  (22 shorter events, 0.3 us)
Async XLA Ops:
  3.4 9.1 %copy-start = (f32[1,1,512,256]{3,2,1,0:T(8,128)S(1)}, f32[1,1,512,256]{3,2,1,0:T(8,128)}, u32[]{:S(2)}) copy-start(f32[1,1,512,256]{3,2,1,0:T(8,128)} %param.10) | copy-start | bytes 1572868
  3.4 18.7 %all-to-all-start = ((bf16[16,2,16,512]{3,2,1,0:T(8,128)(2,1)}), bf16[16,2,16,512]{3,2,1,0:T(8,128)(2,1)S(1)}, u32[]{:S(2)}, u32[]{:S(2)}) async-start(bf16[16,2,16,512]{3,2,1,0:T(8,128)(2,1)} %range_transform.1), calls=%async_computation | async-start | bytes 1048576 | tf_op jit(solution)/shard_map/all_to_all | solution.py:224
  10.6 0.7 copy-start.3
  11.7 0.7 copy-start.4
  24.3 4.6 %collective-permute-start = (bf16[16,2,128,128]{3,2,1,0:T(8,128)(2,1)S(1)}, bf16[16,2,128,128]{3,2,1,0:T(8,128)(2,1)S(1)}, u32[]{:S(2)}, u32[]{:S(2)}) collective-permute-start(bf16[16,2,128,128]{3,2,1,0:T(8,128)(2,1)S(1)} %get-tuple-element.8), channel_id=1, source_target_pairs={{0,16},{16,0},{32,48},{48,32},{64,80},{80,64},{96,112},{112,96},{1... | collective-permute-start | bytes 3145736 | tf_op jit(solution)/shard_map/ppermute | solution.py:243
  29.0 13.5 %collective-permute-start.3 = (bf16[8,2,64,128]{3,2,1,0:T(8,128)(2,1)S(1)}, bf16[8,2,64,128]{3,2,1,0:T(8,128)(2,1)S(1)}, u32[]{:S(2)}, u32[]{:S(2)}) collective-permute-start(bf16[8,2,64,128]{3,2,1,0:T(8,128)(2,1)S(1)} %slice.65), channel_id=1, source_target_pairs={{0,480},{16,496},{32,64},{48,80},{64,32},{80,48},{96,128},{112,144... | collective-permute-start | bytes 786440 | tf_op jit(solution)/shard_map/ppermute | solution.py:250
  32.9 9.6 %copy-start.2 = (f32[1,1,2,128]{3,2,1,0:T(2,128)S(1)}, f32[1,1,2,128]{3,2,1,0:T(2,128)}, u32[]{:S(2)}) copy-start(f32[1,1,2,128]{3,2,1,0:T(2,128)} %param.14) | copy-start | bytes 3076
  32.9 16.2 %collective-permute-start.1 = (bf16[8,2,64,128]{3,2,1,0:T(8,128)(2,1)S(1)}, bf16[8,2,64,128]{3,2,1,0:T(8,128)(2,1)S(1)}, u32[]{:S(2)}, u32[]{:S(2)}) collective-permute-start(bf16[8,2,64,128]{3,2,1,0:T(8,128)(2,1)S(1)} %slice.60), channel_id=1, source_target_pairs={{0,32},{16,48},{32,0},{48,16},{64,96},{80,112},{96,64},{112,80},{1... | collective-permute-start | bytes 786440 | tf_op jit(solution)/shard_map/ppermute | solution.py:250
  42.6 9.7 %collective-permute-start.4 = (bf16[4,2,64,128]{3,2,1,0:T(8,128)(2,1)S(1)}, bf16[4,2,64,128]{3,2,1,0:T(8,128)(2,1)S(1)}, u32[]{:S(2)}, u32[]{:S(2)}) collective-permute-start(bf16[4,2,64,128]{3,2,1,0:T(8,128)(2,1)S(1)} %slice.67), channel_id=1, source_target_pairs={{0,32},{16,48},{32,0},{48,16},{64,96},{80,112},{96,64},{112,80},{1... | collective-permute-start | bytes 393224 | tf_op jit(solution)/shard_map/ppermute | solution.py:250
  49.2 6.9 %collective-permute-start.2 = (bf16[4,2,64,128]{3,2,1,0:T(8,128)(2,1)S(1)}, bf16[4,2,64,128]{3,2,1,0:T(8,128)(2,1)S(1)}, u32[]{:S(2)}, u32[]{:S(2)}) collective-permute-start(bf16[4,2,64,128]{3,2,1,0:T(8,128)(2,1)S(1)} %slice.62), channel_id=1, source_target_pairs={{0,480},{16,496},{32,64},{48,80},{64,32},{80,48},{96,128},{112,144... | collective-permute-start | bytes 393224 | tf_op jit(solution)/shard_map/ppermute | solution.py:250
  56.1 19.9 %collective-permute-start.5 = (bf16[2,128,128]{2,1,0:T(8,128)(2,1)S(1)}, bf16[2,128,128]{2,1,0:T(8,128)(2,1)S(1)}, u32[]{:S(2)}, u32[]{:S(2)}) collective-permute-start(bf16[2,128,128]{2,1,0:T(8,128)(2,1)S(1)} %get-tuple-element.16), channel_id=1, source_target_pairs={{0,384},{16,400},{32,416},{48,432},{64,448},{80,464},{96,480},{112... | collective-permute-start | bytes 196616 | tf_op jit(solution)/shard_map/ppermute | solution.py:256
  62.3 15.8 %collective-permute-start.6 = (bf16[2,128,128]{2,1,0:T(8,128)(2,1)S(1)}, bf16[2,128,128]{2,1,0:T(8,128)(2,1)S(1)}, u32[]{:S(2)}, u32[]{:S(2)}) collective-permute-start(bf16[2,128,128]{2,1,0:T(8,128)(2,1)S(1)} %get-tuple-element.17), channel_id=1, source_target_pairs={{0,256},{16,272},{32,288},{48,304},{64,320},{80,336},{96,352},{112... | collective-permute-start | bytes 196616 | tf_op jit(solution)/shard_map/ppermute | solution.py:256
  67.8 14.8 %collective-permute-start.7 = (bf16[2,128,128]{2,1,0:T(8,128)(2,1)S(1)}, bf16[2,128,128]{2,1,0:T(8,128)(2,1)S(1)}, u32[]{:S(2)}, u32[]{:S(2)}) collective-permute-start(bf16[2,128,128]{2,1,0:T(8,128)(2,1)S(1)} %get-tuple-element.18), channel_id=1, source_target_pairs={{0,128},{16,144},{32,160},{48,176},{64,192},{80,208},{96,224},{112... | collective-permute-start | bytes 196616 | tf_op jit(solution)/shard_map/ppermute | solution.py:256
  75.0 0.7 copy-start.1
